TPU v7x, 32 devices: a whole 2x2x4 slice. The times are simulated.
32 devices in a mesh: fsdp: 2 (over x), ctx: 4 (over y, core), tp: 4 (over z).
Axes of the slice: x: 2, y: 2, z: 4, core: 2. Of those that a mesh axis runs over, the one named last changes fastest.
Arguments:
- tokens: bfloat16 [2048, 4, 1024], P(('ctx', 'tp'), 'fsdp'), may hold values from -6 to 6
- segment_ids: int32 [4, 2048], P('fsdp', 'ctx'), may hold values from 0 to 5, never falling along the last dimension, each value on 1 to 800 neighbouring positions
- decay_rate: float32 [8], P('tp'), may hold values from 0.0005 to 0.07
- w_query: float32 [1024, 1024], P(('fsdp', 'ctx'), 'tp'), may hold values from -0.1875 to 0.1875
- w_key: float32 [1024, 1024], P(('fsdp', 'ctx'), 'tp'), may hold values from -0.1875 to 0.1875
- w_value: float32 [1024, 1024], P(('fsdp', 'ctx'), 'tp'), may hold values from -0.1875 to 0.1875
- w_gate: float32 [1024, 1024], P(('fsdp', 'ctx'), 'tp'), may hold values from -0.1875 to 0.1875
- w_out: float32 [1024, 1024], P('tp', ('fsdp', 'ctx')), may hold values from -0.375 to 0.375
- glu_left: float32 [1024, 2816], P(('fsdp', 'ctx'), 'tp'), may hold values from -0.1875 to 0.1875
- glu_right: float32 [1024, 2816], P(('fsdp', 'ctx'), 'tp'), may hold values from -0.1875 to 0.1875
- glu_down: float32 [2816, 1024], P('tp', ('fsdp', 'ctx')), may hold values from -0.109375 to 0.109375
- cotangent: bfloat16 [2048, 4, 1024], P(('ctx', 'tp'), 'fsdp'), may hold values from -6 to 6
Outputs:
- output: bfloat16 [2048, 4, 1024], P(('ctx', 'tp'), 'fsdp')
- grad_tokens: float32 [2048, 4, 1024], P(('ctx', 'tp'), 'fsdp')
- grad_query: float32 [1024, 1024], P(('fsdp', 'ctx'), 'tp')
- grad_key: float32 [1024, 1024], P(('fsdp', 'ctx'), 'tp')
- grad_value: float32 [1024, 1024], P(('fsdp', 'ctx'), 'tp')
- grad_gate: float32 [1024, 1024], P(('fsdp', 'ctx'), 'tp')
- grad_out: float32 [1024, 1024], P('tp', ('fsdp', 'ctx'))
- grad_left: float32 [1024, 2816], P(('fsdp', 'ctx'), 'tp')
- grad_right: float32 [1024, 2816], P(('fsdp', 'ctx'), 'tp')
- grad_down: float32 [2816, 1024], P('tp', ('fsdp', 'ctx'))
Inputs may be any that keep to these rules, and one draw needn't show every extreme that they name: `segment_ids`: along each sequence the document numbers never fall; every document has 1 to 800 tokens and one has exactly 800.
All inputs are finite; a program needn't handle non-finite values.
Results may differ from a plain program's by a relative error of at most 0.013.
Values may be sent and summed in bfloat16 or wider, within the bound.
A program may use at most 128 MiB of HBM per device.

v0:
```python
import jax
import jax.numpy as jnp
from jax import lax
from jax.sharding import PartitionSpec as P

DH = 128


EPSILON = 1e-06
HEAD_FLOOR = 1.0
HIGHEST = lax.Precision.HIGHEST


def entering(x, axis, join, neutral):
    place = lax.axis_index(axis)
    gathered = jax.tree.map(
        lambda a, kind: lax.all_gather(a.astype(kind), axis),
        x,
        (jnp.bfloat16, jnp.bfloat16, jnp.bfloat16, jnp.bfloat16),
    )
    state = jax.tree.map(lambda a, e: jnp.zeros_like(a) + jnp.asarray(e, a.dtype), x, neutral)

    def one(lap, state):
        return join(
            state,
            jax.tree.map(
                lambda a, own: lax.dynamic_index_in_dim(a, lap, 0, False).astype(own.dtype),
                gathered,
                x,
            ),
        )

    return lax.fori_loop(0, place, one, state)


def entering_2(x, axis, join, neutral):
    count = lax.axis_size(axis)
    place = lax.axis_index(axis)
    ahead = count - 1 - place
    gathered = jax.tree.map(
        lambda a, kind: lax.all_gather(a.astype(kind), axis), x, (jnp.bfloat16, jnp.bfloat16)
    )
    state = jax.tree.map(lambda a, e: jnp.zeros_like(a) + jnp.asarray(e, a.dtype), x, neutral)

    def one(lap, state):
        source = count - 1 - lap
        return join(
            state,
            jax.tree.map(
                lambda a, own: lax.dynamic_index_in_dim(a, source, 0, False).astype(own.dtype),
                gathered,
                x,
            ),
        )

    return lax.fori_loop(0, ahead, one, state)


def normalize(values, floor_value=EPSILON):
    return values * lax.rsqrt(jnp.mean(values * values, axis=-1, keepdims=True) + floor_value)


def norm_backward(values, upstream, floor_value=EPSILON):
    inverse = lax.rsqrt(jnp.mean(values * values, axis=-1, keepdims=True) + floor_value)
    inner_mean = jnp.mean(upstream * values, axis=-1, keepdims=True)
    return inverse * (upstream - values * inner_mean * inverse * inverse)


def silu_slope(values):
    sigmoid_value = jax.nn.sigmoid(values)
    return sigmoid_value * (1.0 + values * (1.0 - sigmoid_value))


def chain_forward(earlier, later):
    early_first, early_last, early_decay, early_state = earlier
    late_first, late_last, late_decay, late_state = later
    linked = (late_first == early_last) | (early_last < 0.0) | (late_first < 0.0)
    carried = jnp.where(linked[:, None], late_decay, 0.0)
    first_seg = jnp.where(early_first < 0.0, late_first, early_first)
    last_seg = jnp.where(late_last < 0.0, early_last, late_last)
    return (
        first_seg,
        last_seg,
        early_decay * carried,
        late_state + carried[:, :, None, None] * early_state,
    )


def chain_backward(earlier, later):
    return (earlier[0] * later[0], later[1] + later[0][:, :, None, None] * earlier[1])


def shards(
    tokens,
    segment_ids,
    decay_rate,
    w_query,
    w_key,
    w_value,
    w_gate,
    w_out,
    glu_left,
    glu_right,
    glu_down,
    cotangent,
):
    shard_len, seq_count, model_width = tokens.shape
    tok_float = tokens.astype(jnp.float32)
    normed_part = normalize(tok_float).astype(jnp.bfloat16)
    gathered = (
        lax.all_gather(w_query.astype(jnp.bfloat16), ("fsdp", "ctx"), axis=0, tiled=True),
        lax.all_gather(w_key.astype(jnp.bfloat16), ("fsdp", "ctx"), axis=0, tiled=True),
        lax.all_gather(w_value.astype(jnp.bfloat16), ("fsdp", "ctx"), axis=0, tiled=True),
        lax.all_gather(w_gate.astype(jnp.bfloat16), ("fsdp", "ctx"), axis=0, tiled=True),
        lax.all_gather(w_out.astype(jnp.bfloat16), ("fsdp", "ctx"), axis=1, tiled=True),
        lax.all_gather(glu_left.astype(jnp.bfloat16), ("fsdp", "ctx"), axis=0, tiled=True),
        lax.all_gather(glu_right.astype(jnp.bfloat16), ("fsdp", "ctx"), axis=0, tiled=True),
        lax.all_gather(glu_down.astype(jnp.bfloat16), ("fsdp", "ctx"), axis=1, tiled=True),
    )
    full_query, full_key, full_value, full_gate, full_out, full_left, full_right, full_down = (
        gathered
    )
    normed = lax.all_gather(normed_part, "tp", axis=0, tiled=True)
    block_len = normed.shape[0]
    total_rows = block_len * seq_count
    normed_flat = normed.reshape(total_rows, model_width)
    local_width = full_query.shape[1]
    head_count = local_width // DH
    head_shape = (block_len, seq_count, head_count, DH)
    proj_query = jnp.dot(normed_flat, full_query, preferred_element_type=jnp.float32)
    proj_key = jnp.dot(normed_flat, full_key, preferred_element_type=jnp.float32)
    proj_value = jnp.dot(normed_flat, full_value, preferred_element_type=jnp.float32)
    proj_gate = jnp.dot(normed_flat, full_gate, preferred_element_type=jnp.float32)
    queries = jax.nn.silu(proj_query).astype(jnp.bfloat16).reshape(head_shape)
    keys_low = jax.nn.silu(proj_key).astype(jnp.bfloat16).reshape(head_shape)
    values_low = proj_value.astype(jnp.bfloat16).reshape(head_shape)
    seg_pos = segment_ids.T
    seg_float = seg_pos.astype(jnp.float32)
    position = jnp.arange(block_len).astype(jnp.float32)
    distance = position[:, None] - position[None, :]
    same_doc = (segment_ids[:, :, None] == segment_ids[:, None, :]) & (distance >= 0.0)[None]
    decay_grid = jnp.where(
        same_doc[:, None],
        jnp.exp(-decay_rate[None, :, None, None] * jnp.maximum(distance, 0.0)[None, None]),
        0.0,
    )
    end_weight = jnp.where(
        (seg_pos == seg_pos[-1:])[:, :, None],
        jnp.exp(-(block_len - 1.0 - position)[:, None, None] * decay_rate[None, None, :]),
        0.0,
    )
    keys_end = (keys_low.astype(jnp.float32) * end_weight[..., None]).astype(jnp.bfloat16)
    update = jnp.einsum("tbhd,tbhe->bhde", keys_end, values_low, preferred_element_type=jnp.float32)
    first_seg = seg_float[0]
    last_seg = seg_float[-1]
    span_decay = jnp.where(
        (first_seg == last_seg)[:, None], jnp.exp(-block_len * decay_rate)[None, :], 0.0
    )
    identity = (
        -jnp.ones((seq_count,), jnp.float32),
        -jnp.ones((seq_count,), jnp.float32),
        jnp.ones((seq_count, head_count), jnp.float32),
        jnp.zeros((seq_count, head_count, DH, DH), jnp.float32),
    )
    scanned = entering((first_seg, last_seg, span_decay, update), "ctx", chain_forward, identity)
    prior_last = scanned[1]
    state_low = scanned[3].astype(jnp.bfloat16)
    inflow = jnp.where(
        (seg_pos == prior_last[None, :])[:, :, None],
        jnp.exp(-(position + 1.0)[:, None, None] * decay_rate[None, None, :]),
        0.0,
    )
    scores = jnp.einsum("tbhd,sbhd->bhts", queries, keys_low, preferred_element_type=jnp.float32)
    weights_low = (scores * decay_grid).astype(jnp.bfloat16)
    intra = jnp.einsum(
        "bhts,sbhd->tbhd", weights_low, values_low, preferred_element_type=jnp.float32
    )
    inter = (
        jnp.einsum("tbhd,bhde->tbhe", queries, state_low, preferred_element_type=jnp.float32)
        * inflow[..., None]
    )
    attended = intra + inter
    attended_norm = normalize(attended, HEAD_FLOOR)
    gate_value = jax.nn.sigmoid(proj_gate).reshape(head_shape)
    mixed_heads = (
        (attended_norm * gate_value).astype(jnp.bfloat16).reshape(block_len, seq_count, local_width)
    )
    row_count = shard_len * lax.axis_size("tp")
    piece_rows = mixed_heads.reshape(row_count * seq_count, local_width)
    branch = lax.psum_scatter(
        jnp.dot(piece_rows, full_out, preferred_element_type=jnp.float32).reshape(
            row_count, seq_count, model_width
        ),
        "tp",
        scatter_dimension=0,
        tiled=True,
    )
    residual = tok_float + branch
    second_part = normalize(residual).astype(jnp.bfloat16)
    second = lax.all_gather(second_part, "tp", axis=0, tiled=True)
    second_flat = second.reshape(total_rows, model_width)
    left_proj = jnp.dot(second_flat, full_left, preferred_element_type=jnp.float32)
    right_proj = jnp.dot(second_flat, full_right, preferred_element_type=jnp.float32)
    hidden = (left_proj * right_proj).astype(jnp.bfloat16)
    ffn_width = hidden.shape[1]
    hidden_blocks = hidden.reshape(block_len, seq_count, ffn_width)
    row_count = shard_len * lax.axis_size("tp")
    piece_rows = hidden_blocks.reshape(row_count * seq_count, ffn_width)
    ffn_branch = lax.psum_scatter(
        jnp.dot(piece_rows, full_down, preferred_element_type=jnp.float32)
        .reshape(row_count, seq_count, model_width)
        .astype(jnp.bfloat16),
        "tp",
        scatter_dimension=0,
        tiled=True,
    ).astype(jnp.float32)
    output = (residual + ffn_branch).astype(jnp.bfloat16)
    upstream = lax.all_gather(cotangent, "tp", axis=0, tiled=True).reshape(total_rows, model_width)
    grad_down = jnp.dot(hidden.T, upstream, preferred_element_type=jnp.float32)
    grad_hidden = jnp.dot(upstream, full_down.T, preferred_element_type=jnp.float32)
    grad_left_proj = (grad_hidden * right_proj).astype(jnp.bfloat16)
    grad_right_proj = (grad_hidden * left_proj).astype(jnp.bfloat16)
    grad_left = jnp.dot(second_flat.T, grad_left_proj, preferred_element_type=jnp.float32)
    grad_right = jnp.dot(second_flat.T, grad_right_proj, preferred_element_type=jnp.float32)
    left_blocks = grad_left_proj.reshape(block_len, seq_count, ffn_width)
    right_blocks = grad_right_proj.reshape(block_len, seq_count, ffn_width)
    row_count = shard_len * lax.axis_size("tp")
    left_rows = left_blocks.reshape(row_count * seq_count, ffn_width)
    right_rows = right_blocks.reshape(row_count * seq_count, ffn_width)
    summed = jnp.dot(left_rows, full_left.T, preferred_element_type=jnp.float32) + jnp.dot(
        right_rows, full_right.T, preferred_element_type=jnp.float32
    )
    grad_second = lax.psum_scatter(
        summed.reshape(row_count, seq_count, model_width), "tp", scatter_dimension=0, tiled=True
    )
    grad_residual = cotangent.astype(jnp.float32) + norm_backward(residual, grad_second)
    branch_low = grad_residual.astype(jnp.bfloat16)
    grad_branch = lax.all_gather(branch_low, "tp", axis=0, tiled=True).reshape(
        total_rows, model_width
    )
    grad_wout = jnp.dot(
        mixed_heads.reshape(total_rows, local_width).T,
        grad_branch,
        preferred_element_type=jnp.float32,
    )
    grad_mixed = jnp.dot(grad_branch, full_out.T, preferred_element_type=jnp.float32).reshape(
        head_shape
    )
    grad_gate_proj = (
        (grad_mixed * attended_norm * gate_value * (1.0 - gate_value))
        .astype(jnp.bfloat16)
        .reshape(total_rows, local_width)
    )
    grad_attended = norm_backward(attended, grad_mixed * gate_value, HEAD_FLOOR).astype(
        jnp.bfloat16
    )
    grad_weights = jnp.einsum(
        "tbhd,sbhd->bhts", grad_attended, values_low, preferred_element_type=jnp.float32
    )
    grad_scores = (grad_weights * decay_grid).astype(jnp.bfloat16)
    grad_queries = jnp.einsum(
        "bhts,sbhd->tbhd", grad_scores, keys_low, preferred_element_type=jnp.float32
    )
    grad_queries = (
        grad_queries
        + jnp.einsum(
            "tbhe,bhde->tbhd", grad_attended, state_low, preferred_element_type=jnp.float32
        )
        * inflow[..., None]
    )
    grad_keys = jnp.einsum(
        "bhts,tbhd->sbhd", grad_scores, queries, preferred_element_type=jnp.float32
    )
    grad_values = jnp.einsum(
        "bhts,tbhd->sbhd", weights_low, grad_attended, preferred_element_type=jnp.float32
    )
    weighted_queries = queries.astype(jnp.float32) * inflow[..., None]
    grad_prior_local = jnp.einsum(
        "tbhd,tbhe->bhde", weighted_queries, grad_attended.astype(jnp.float32), precision=HIGHEST
    )
    link_decay = jnp.where((first_seg == prior_last)[:, None], span_decay, 0.0)
    back_identity = (
        jnp.ones((seq_count, head_count), jnp.float32),
        jnp.zeros((seq_count, head_count, DH, DH), jnp.float32),
    )
    grad_update = entering_2((link_decay, grad_prior_local), "ctx", chain_backward, back_identity)[
        1
    ]
    grad_values = grad_values + jnp.einsum(
        "tbhd,bhde->tbhe", keys_end.astype(jnp.float32), grad_update, precision=HIGHEST
    )
    grad_keys = (
        grad_keys
        + jnp.einsum(
            "tbhe,bhde->tbhd", values_low.astype(jnp.float32), grad_update, precision=HIGHEST
        )
        * end_weight[..., None]
    )
    grad_query_proj = (
        (grad_queries * silu_slope(proj_query).reshape(head_shape))
        .astype(jnp.bfloat16)
        .reshape(total_rows, local_width)
    )
    grad_key_proj = (
        (grad_keys * silu_slope(proj_key).reshape(head_shape))
        .astype(jnp.bfloat16)
        .reshape(total_rows, local_width)
    )
    grad_value_proj = grad_values.astype(jnp.bfloat16).reshape(total_rows, local_width)
    grad_wquery = jnp.dot(normed_flat.T, grad_query_proj, preferred_element_type=jnp.float32)
    grad_wkey = jnp.dot(normed_flat.T, grad_key_proj, preferred_element_type=jnp.float32)
    grad_wvalue = jnp.dot(normed_flat.T, grad_value_proj, preferred_element_type=jnp.float32)
    grad_wgate = jnp.dot(normed_flat.T, grad_gate_proj, preferred_element_type=jnp.float32)
    query_blocks = grad_query_proj.reshape(block_len, seq_count, local_width)
    key_blocks = grad_key_proj.reshape(block_len, seq_count, local_width)
    value_blocks = grad_value_proj.reshape(block_len, seq_count, local_width)
    gate_blocks = grad_gate_proj.reshape(block_len, seq_count, local_width)
    row_count = shard_len * lax.axis_size("tp")
    summed = jnp.zeros((row_count * seq_count, model_width), jnp.float32)
    for grad_blocks, weight_full in (
        (query_blocks, full_query),
        (key_blocks, full_key),
        (value_blocks, full_value),
        (gate_blocks, full_gate),
    ):
        piece_rows = grad_blocks.reshape(row_count * seq_count, local_width)
        summed = summed + jnp.dot(piece_rows, weight_full.T, preferred_element_type=jnp.float32)
    grad_normed = lax.psum_scatter(
        summed.reshape(row_count, seq_count, model_width).astype(jnp.bfloat16),
        "tp",
        scatter_dimension=0,
        tiled=True,
    ).astype(jnp.float32)
    grad_tokens = grad_residual + norm_backward(tok_float, grad_normed)
    every_grad = (
        lax.psum_scatter(grad_wquery, ("fsdp", "ctx"), scatter_dimension=0, tiled=True),
        lax.psum_scatter(grad_wkey, ("fsdp", "ctx"), scatter_dimension=0, tiled=True),
        lax.psum_scatter(grad_wvalue, ("fsdp", "ctx"), scatter_dimension=0, tiled=True),
        lax.psum_scatter(grad_wgate, ("fsdp", "ctx"), scatter_dimension=0, tiled=True),
        lax.psum_scatter(grad_wout, ("fsdp", "ctx"), scatter_dimension=1, tiled=True),
        lax.psum_scatter(grad_left, ("fsdp", "ctx"), scatter_dimension=0, tiled=True),
        lax.psum_scatter(grad_right, ("fsdp", "ctx"), scatter_dimension=0, tiled=True),
        lax.psum_scatter(grad_down, ("fsdp", "ctx"), scatter_dimension=1, tiled=True),
    )
    return (
        output,
        grad_tokens,
        every_grad[0],
        every_grad[1],
        every_grad[2],
        every_grad[3],
        every_grad[4],
        every_grad[5],
        every_grad[6],
        every_grad[7],
    )


def solution(mesh):
    in_specs = (
        P(("ctx", "tp"), "fsdp", None),
        P("fsdp", "ctx"),
        P("tp"),
        P(("fsdp", "ctx"), "tp"),
        P(("fsdp", "ctx"), "tp"),
        P(("fsdp", "ctx"), "tp"),
        P(("fsdp", "ctx"), "tp"),
        P("tp", ("fsdp", "ctx")),
        P(("fsdp", "ctx"), "tp"),
        P(("fsdp", "ctx"), "tp"),
        P("tp", ("fsdp", "ctx")),
        P(("ctx", "tp"), "fsdp", None),
    )
    out_specs = (
        P(("ctx", "tp"), "fsdp", None),
        P(("ctx", "tp"), "fsdp", None),
        P(("fsdp", "ctx"), "tp"),
        P(("fsdp", "ctx"), "tp"),
        P(("fsdp", "ctx"), "tp"),
        P(("fsdp", "ctx"), "tp"),
        P("tp", ("fsdp", "ctx")),
        P(("fsdp", "ctx"), "tp"),
        P(("fsdp", "ctx"), "tp"),
        P("tp", ("fsdp", "ctx")),
    )
    return jax.shard_map(shards, mesh=mesh, in_specs=in_specs, out_specs=out_specs, check_vma=False)
```

profile of v0, /device:TPU:0, one launch (start us, length us, event | category | flops | bytes accessed | tf_op | source)
XLA Modules:
  0.0 1034.6 jit_solution(431356184398698397)
XLA Ops:
  11.0 6.0 all-gather.3
  17.2 5.3 all-gather.2
  28.1 10.1 all_gather.67
  38.2 9.8 all_gather.65
  48.0 9.9 all_gather.66
  57.9 10.7 %all_gather.73 = bf16[1024,256]{1,0:T(8,128)(2,1)} all-gather(bf16[128,256]{1,0:T(8,128)(2,1)S(1)} %convert_element_type.256), channel_id=1, replica_groups=mesh['fsdp'=2,'ctx'=4,'tp'=4] {'fsdp','ctx'}, dimensions={0}, use_global_device_ids=true | all-gather | bytes 589824 | tf_op jit(solution)/shard_map/all_gather | solution.py:114
  68.7 10.1 all_gather.74
  102.0 7.8 all-gather
  134.3 80.6 %reduce-scatter.13.cloned.1.call-done = f32[128,2,1024]{2,0,1:T(8,128)} async-done(((f32[512,2,1024]{2,0,1:T(8,128)}), f32[128,2,1024]{2,0,1:T(8,128)}) %reduce-scatter.13.cloned.1.call-update) | async-done | bytes 1048592 | tf_op jit(solution)/shard_map/reduce_scatter | solution.py:190
  221.8 41.2 %all-gather.22.cloned.1.call-done = bf16[512,2,1024]{2,1,0:T(2,128)(2,1)} async-done(((bf16[128,2,1024]{2,1,0:T(2,128)(2,1)}), bf16[512,2,1024]{2,1,0:T(2,128)(2,1)}) %all-gather.22.cloned.1.call-update) | async-done | bytes 2097168 | tf_op jit(solution)/shard_map/all_gather | solution.py:218
  267.1 42.1 %all-gather.14.cloned.1.call-done = bf16[512,2,1024]{2,0,1:T(8,128)(2,1)} async-done(((bf16[128,2,1024]{2,0,1:T(8,128)(2,1)}), bf16[512,2,1024]{2,0,1:T(8,128)(2,1)}) %all-gather.14.cloned.1.call-update) | async-done | bytes 2097168 | tf_op jit(solution)/shard_map/all_gather | solution.py:200
  318.5 17.2 %all-gather.16.cloned.1.call-done = bf16[1024,704]{0,1:T(8,128)(2,1)} async-done(((bf16[128,704]{0,1:T(8,128)(2,1)}), bf16[1024,704]{0,1:T(8,128)(2,1)}) %all-gather.16.cloned.1.call-update) | async-done | bytes 1441808 | tf_op jit(solution)/shard_map/all_gather | solution.py:116
  335.7 5.3 fusion.68
  341.0 22.5 %all-gather.18.cloned.1.call-done = bf16[1024,704]{0,1:T(8,128)(2,1)} async-done(((bf16[128,704]{0,1:T(8,128)(2,1)}), bf16[1024,704]{0,1:T(8,128)(2,1)}) %all-gather.18.cloned.1.call-update) | async-done | bytes 1441808 | tf_op jit(solution)/shard_map/all_gather | solution.py:117
  363.5 5.2 fusion.69
  368.7 22.7 %all-gather.20.cloned.1.call-done = bf16[704,1024]{1,0:T(8,128)(2,1)} async-done(((bf16[704,128]{1,0:T(8,128)(2,1)}), bf16[704,1024]{1,0:T(8,128)(2,1)}) %all-gather.20.cloned.1.call-update) | async-done | bytes 1441808 | tf_op jit(solution)/shard_map/all_gather | solution.py:118
  391.4 6.8 multiply_convert_fusion
  404.5 6.0 reshape.426
  410.5 5.5 copy.115
  416.1 76.9 %reduce-scatter.17.cloned.1.call-done = f32[128,2,1024]{2,0,1:T(8,128)} async-done(((f32[512,2,1024]{2,0,1:T(8,128)}), f32[128,2,1024]{2,0,1:T(8,128)}) %reduce-scatter.17.cloned.1.call-update) | async-done | bytes 1048592 | tf_op jit(solution)/shard_map/reduce_scatter | solution.py:233
  511.6 31.4 %all-gather.24.cloned.1.call-done = bf16[512,2,1024]{2,0,1:T(8,128)(2,1)} async-done(((bf16[128,2,1024]{2,0,1:T(8,128)(2,1)}), bf16[512,2,1024]{2,0,1:T(8,128)(2,1)}) %all-gather.24.cloned.1.call-update) | async-done | bytes 2097168 | tf_op jit(solution)/shard_map/all_gather | solution.py:238
  554.6 7.3 all-gather.1
  582.1 5.6 add_convert_fusion
  648.5 33.1 %reduce-scatter.15.cloned.1.call-done = bf16[128,2,1024]{2,0,1:T(8,128)(2,1)} async-done(((bf16[512,2,1024]{2,0,1:T(8,128)(2,1)}), bf16[128,2,1024]{2,0,1:T(8,128)(2,1)}) %reduce-scatter.15.cloned.1.call-update) | async-done | bytes 524304 | tf_op jit(solution)/shard_map/reduce_scatter | solution.py:209
  686.6 43.0 %reduce-scatter.31.cloned.1.call-done = f32[128,704]{0,1:T(8,128)} async-done(((f32[1024,704]{0,1:T(8,128)}), f32[128,704]{0,1:T(8,128)}) %reduce-scatter.31.cloned.1.call-update) | async-done | bytes 360464 | tf_op jit(solution)/shard_map/reduce_scatter | solution.py:341
  729.6 49.2 %reduce-scatter.33.cloned.1.call-done = f32[128,704]{0,1:T(8,128)} async-done(((f32[1024,704]{0,1:T(8,128)}), f32[128,704]{0,1:T(8,128)}) %reduce-scatter.33.cloned.1.call-update) | async-done | bytes 360464 | tf_op jit(solution)/shard_map/reduce_scatter | solution.py:342
  778.9 48.7 %reduce-scatter.35.cloned.1.call-done = f32[704,128]{1,0:T(8,128)} async-done(((f32[704,1024]{1,0:T(8,128)}), f32[704,128]{1,0:T(8,128)}) %reduce-scatter.35.cloned.1.call-update) | async-done | bytes 360464 | tf_op jit(solution)/shard_map/reduce_scatter | solution.py:343
  827.6 40.0 %reduce-scatter.29.cloned.1.call-done = f32[256,128]{1,0:T(8,128)} async-done(((f32[256,1024]{1,0:T(8,128)}), f32[256,128]{1,0:T(8,128)}) %reduce-scatter.29.cloned.1.call-update) | async-done | bytes 131088 | tf_op jit(solution)/shard_map/reduce_scatter | solution.py:340
  867.6 40.0 %reduce-scatter.23.cloned.1.call-done = f32[128,256]{1,0:T(8,128)} async-done(((f32[1024,256]{1,0:T(8,128)}), f32[128,256]{1,0:T(8,128)}) %reduce-scatter.23.cloned.1.call-update) | async-done | bytes 131088 | tf_op jit(solution)/shard_map/reduce_scatter | solution.py:337
  907.6 40.0 %reduce-scatter.21.cloned.1.call-done = f32[128,256]{1,0:T(8,128)} async-done(((f32[1024,256]{1,0:T(8,128)}), f32[128,256]{1,0:T(8,128)}) %reduce-scatter.21.cloned.1.call-update) | async-done | bytes 131088 | tf_op jit(solution)/shard_map/reduce_scatter | solution.py:336
  947.6 40.0 %reduce-scatter.25.cloned.1.call-done = f32[128,256]{1,0:T(8,128)} async-done(((f32[1024,256]{1,0:T(8,128)}), f32[128,256]{1,0:T(8,128)}) %reduce-scatter.25.cloned.1.call-update) | async-done | bytes 131088 | tf_op jit(solution)/shard_map/reduce_scatter | solution.py:338
  987.5 40.1 %reduce-scatter.27.cloned.1.call-done = f32[128,256]{1,0:T(8,128)} async-done(((f32[1024,256]{1,0:T(8,128)}), f32[128,256]{1,0:T(8,128)}) %reduce-scatter.27.cloned.1.call-update) | async-done | bytes 131088 | tf_op jit(solution)/shard_map/reduce_scatter | solution.py:339
  (277 shorter events, 199.8 us)
Async XLA Ops:
  7.2 20.4 %copy-start.50 = (f32[128,256]{1,0:T(8,128)S(1)}, f32[128,256]{1,0:T(8,128)}, u32[]{:S(2)}) copy-start(f32[128,256]{1,0:T(8,128)} %param.21) | copy-start | bytes 393220
  7.2 20.6 %copy-start.51 = (f32[128,256]{1,0:T(8,128)S(1)}, f32[128,256]{1,0:T(8,128)}, u32[]{:S(2)}) copy-start(f32[128,256]{1,0:T(8,128)} %param.19) | copy-start | bytes 393220
  7.2 20.6 %copy-start.52 = (f32[128,256]{1,0:T(8,128)S(1)}, f32[128,256]{1,0:T(8,128)}, u32[]{:S(2)}) copy-start(f32[128,256]{1,0:T(8,128)} %param.22) | copy-start | bytes 393220
  7.2 20.6 %copy-start.53 = (f32[256,128]{1,0:T(8,128)S(1)}, f32[256,128]{1,0:T(8,128)}, u32[]{:S(2)}) copy-start(f32[256,128]{1,0:T(8,128)} %param.23) | copy-start | bytes 393220
  7.2 73.8 %all-gather.12.cloned.1.call-start = ((), (), s32[]{:S(2)}) async-start(), calls=%async_computation.12 | async-start | bytes 2621440 | tf_op jit(solution)/shard_map/all_gather | solution.py:123
  10.7 204.1 %reduce-scatter.13.cloned.1.call-start = ((), (), s32[]{:S(2)}) async-start(), calls=%async_computation.13 | async-start | bytes 5242880 | tf_op jit(solution)/shard_map/reduce_scatter | solution.py:190
  38.2 52.1 %copy-start.38 = (bf16[1024,256]{1,0:T(8,128)(2,1)}, bf16[1024,256]{1,0:T(8,128)(2,1)S(1)}, u32[]{:S(2)}) copy-start(bf16[1024,256]{1,0:T(8,128)(2,1)S(1)} %all_gather.67) | copy-start | bytes 1572868
  48.0 49.2 %copy-start.36 = (bf16[1024,256]{1,0:T(8,128)(2,1)}, bf16[1024,256]{1,0:T(8,128)(2,1)S(1)}, u32[]{:S(2)}) copy-start(bf16[1024,256]{1,0:T(8,128)(2,1)S(1)} %all_gather.65) | copy-start | bytes 1572868
  133.5 81.4 %copy-start = (bf16[128,2,1024]{2,1,0:T(2,128)(2,1)S(1)}, bf16[128,2,1024]{2,1,0:T(2,128)(2,1)}, u32[]{:S(2)}) copy-start(bf16[128,2,1024]{2,1,0:T(2,128)(2,1)} %param.16) | copy-start | bytes 1572868
  133.5 129.5 %all-gather.22.cloned.1.call-start = ((), (), s32[]{:S(2)}) async-start(), calls=%async_computation.19 | async-start | bytes 2621440 | tf_op jit(solution)/shard_map/all_gather | solution.py:218
  134.2 83.3 %copy-start.48 = (f32[128,704]{0,1:T(8,128)S(1)}, f32[128,704]{0,1:T(8,128)}, u32[]{:S(2)}) copy-start(f32[128,704]{0,1:T(8,128)} %param.24) | copy-start | bytes 1081348
  134.2 175.0 %all-gather.14.cloned.1.call-start = ((), (), s32[]{:S(2)}) async-start(), calls=%async_computation.14 | async-start | bytes 2621440 | tf_op jit(solution)/shard_map/all_gather | solution.py:200
  217.4 118.3 %all-gather.16.cloned.1.call-start = ((), (), s32[]{:S(2)}) async-start(), calls=%async_computation.15 | async-start | bytes 1622016 | tf_op jit(solution)/shard_map/all_gather | solution.py:116
  218.2 145.3 %all-gather.18.cloned.1.call-start = ((), (), s32[]{:S(2)}) async-start(), calls=%async_computation.16 | async-start | bytes 1622016 | tf_op jit(solution)/shard_map/all_gather | solution.py:117
  220.0 171.5 %all-gather.20.cloned.1.call-start = ((), (), s32[]{:S(2)}) async-start(), calls=%async_computation.17 | async-start | bytes 1622016 | tf_op jit(solution)/shard_map/all_gather | solution.py:118
  221.7 271.2 %reduce-scatter.17.cloned.1.call-start = ((), (), s32[]{:S(2)}) async-start(), calls=%async_computation.20 | async-start | bytes 5242880 | tf_op jit(solution)/shard_map/reduce_scatter | solution.py:233
  416.0 78.9 %copy-start.19 = (bf16[128,2,1024]{2,1,0:T(2,128)(2,1)S(1)}, bf16[128,2,1024]{2,1,0:T(2,128)(2,1)}, u32[]{:S(2)}) copy-start(bf16[128,2,1024]{2,1,0:T(2,128)(2,1)} %param.27) | copy-start | bytes 1572868
  416.0 127.0 %all-gather.24.cloned.1.call-start = ((), (), s32[]{:S(2)}) async-start(), calls=%async_computation.21 | async-start | bytes 2621440 | tf_op jit(solution)/shard_map/all_gather | solution.py:238
  496.4 150.7 %reduce-scatter.19.cloned.1.call-start = ((), (), s32[]{:S(2)}) async-start(), calls=%async_computation.22 | async-start | bytes 2621440 | tf_op jit(solution)/shard_map/reduce_scatter | solution.py:328
  506.5 36.4 %copy-start.24 = (bf16[256,1024]{1,0:T(8,128)(2,1)S(1)}, bf16[256,1024]{1,0:T(8,128)(2,1)}, u32[]{:S(2)}) copy-start(bf16[256,1024]{1,0:T(8,128)(2,1)} %all_gather.74) | copy-start | bytes 1572868
  593.7 87.9 %reduce-scatter.15.cloned.1.call-start = ((), (), s32[]{:S(2)}) async-start(), calls=%async_computation.18 | async-start | bytes 2621440 | tf_op jit(solution)/shard_map/reduce_scatter | solution.py:209
  602.9 126.7 %reduce-scatter.31.cloned.1.call-start = ((), (), s32[]{:S(2)}) async-start(), calls=%async_computation.28 | async-start | bytes 3244032 | tf_op jit(solution)/shard_map/reduce_scatter | solution.py:341
  609.1 169.8 %reduce-scatter.33.cloned.1.call-start = ((), (), s32[]{:S(2)}) async-start(), calls=%async_computation.29 | async-start | bytes 3244032 | tf_op jit(solution)/shard_map/reduce_scatter | solution.py:342
  615.4 212.3 %reduce-scatter.35.cloned.1.call-start = ((), (), s32[]{:S(2)}) async-start(), calls=%async_computation.30 | async-start | bytes 3244032 | tf_op jit(solution)/shard_map/reduce_scatter | solution.py:343
  621.7 245.9 %reduce-scatter.29.cloned.1.call-start = ((), (), s32[]{:S(2)}) async-start(), calls=%async_computation.27 | async-start | bytes 1179648 | tf_op jit(solution)/shard_map/reduce_scatter | solution.py:340
  633.1 274.5 %reduce-scatter.23.cloned.1.call-start = ((), (), s32[]{:S(2)}) async-start(), calls=%async_computation.24 | async-start | bytes 1179648 | tf_op jit(solution)/shard_map/reduce_scatter | solution.py:337
  636.6 311.0 %reduce-scatter.21.cloned.1.call-start = ((), (), s32[]{:S(2)}) async-start(), calls=%async_computation.23 | async-start | bytes 1179648 | tf_op jit(solution)/shard_map/reduce_scatter | solution.py:336
  640.1 347.5 %reduce-scatter.25.cloned.1.call-start = ((), (), s32[]{:S(2)}) async-start(), calls=%async_computation.25 | async-start | bytes 1179648 | tf_op jit(solution)/shard_map/reduce_scatter | solution.py:338
  643.5 384.1 %reduce-scatter.27.cloned.1.call-start = ((), (), s32[]{:S(2)}) async-start(), calls=%async_computation.26 | async-start | bytes 1179648 | tf_op jit(solution)/shard_map/reduce_scatter | solution.py:339
  643.6 38.0 %copy-start.20 = (bf16[128,2,1024]{2,1,0:T(2,128)(2,1)S(1)}, bf16[128,2,1024]{2,1,0:T(2,128)(2,1)}, u32[]{:S(2)}) copy-start(bf16[128,2,1024]{2,1,0:T(2,128)(2,1)} %param.27) | copy-start | bytes 1572868
  647.0 34.6 %copy-start.3 = (f32[128,2,1024]{2,0,1:T(8,128)S(1)}, f32[128,2,1024]{2,0,1:T(8,128)}, u32[]{:S(2)}) copy-start(f32[128,2,1024]{2,0,1:T(8,128)} %reduce-scatter.13.cloned.1.call-done) | copy-start | bytes 3145732
  647.0 34.6 %copy-start.11 = (f32[128,2,1024]{2,0,1:T(8,128)S(1)}, f32[128,2,1024]{2,0,1:T(8,128)}, u32[]{:S(2)}) copy-start(f32[128,2,1024]{2,0,1:T(8,128)} %reduce-scatter.17.cloned.1.call-done) | copy-start | bytes 3145732
  (45 other events, 164.8 us)
Sparse Core Ops, SparseCore 0:
  10.8 48.6 all-gather.11
  133.6 81.2 reduce-scatter.12
  216.5 46.4 all-gather.21
  264.5 44.6 all-gather.13
  311.7 24.0 all-gather.15
  338.2 25.2 all-gather.17
  366.1 25.2 all-gather.19
  416.1 76.7 reduce-scatter.16
  496.5 46.4 all-gather.23
  593.8 42.1 reduce-scatter.18
  638.4 43.1 reduce-scatter.14
  685.4 44.1 reduce-scatter.30
  734.0 44.8 reduce-scatter.32
  782.7 44.8 reduce-scatter.34
  831.5 36.0 reduce-scatter.28
  871.5 36.0 reduce-scatter.22
  911.5 36.0 reduce-scatter.20
  951.5 35.9 reduce-scatter.24
  991.6 35.9 reduce-scatter.26
where the time goes:
time: 1040 us; the launch traced here: 1030 us
  waiting for transfers between devices  710 us (68%)
  matrix products  107 us (10%)
  local copies, waits for them, and re-layouts  92.6 us (9%)
  blocking collectives  87 us (8%)
  other arithmetic  21.5 us (2%)
  between operations  15.3 us (1%)
    reduce_scatter x1, waiting for transfers between devices, shards(): lax.psum_scatter(jnp.dot(piece_rows, full_out, preferred_element_type=jnp...  80.6 us
    reduce_scatter x1, waiting for transfers between devices, shards(): lax.psum_scatter(summed.reshape(row_count, seq_count, model_width), 'tp',...  76.9 us
    reduce_scatter x1, waiting for transfers between devices, shards(): lax.psum_scatter(grad_right, ('fsdp', 'ctx'), scatter_dimension=0, tiled=...  49.2 us
    reduce_scatter x1, waiting for transfers between devices, shards(): lax.psum_scatter(grad_down, ('fsdp', 'ctx'), scatter_dimension=1, tiled=T...  48.7 us
    reduce_scatter x1, waiting for transfers between devices, shards(): lax.psum_scatter(grad_left, ('fsdp', 'ctx'), scatter_dimension=0, tiled=T...  43 us
    all_gather x1, waiting for transfers between devices, shards(): second = lax.all_gather(second_part, 'tp', axis=0, tiled=True)  42.1 us
    all_gather x1, waiting for transfers between devices, shards(): lax.all_gather(cotangent, 'tp', axis=0, tiled=True)  41.2 us
    reduce_scatter x1, waiting for transfers between devices, shards(): lax.psum_scatter(grad_wgate, ('fsdp', 'ctx'), scatter_dimension=0, tiled=...  40.1 us
  transfers between devices with their start and end apart: 19, of which 17 were waited for; matrix products, arithmetic and copies ran while one was open for 9% of the time, Pallas kernels for 0%

commit v1 on v0

--- a/solution.py
+++ b/solution.py
@@ -1,14 +1,930 @@
+import functools
+
 import jax
 import jax.numpy as jnp
 from jax import lax
+from jax.experimental import pallas as pl
+from jax.experimental.pallas import tpu as pltpu
 from jax.sharding import PartitionSpec as P
 
 DH = 128
-
-
+CH = 256
 EPSILON = 1e-06
 HEAD_FLOOR = 1.0
-HIGHEST = lax.Precision.HIGHEST
+BF = jnp.bfloat16
+F32 = jnp.float32
+MESH = pl.DeviceIdType.MESH
+MIB = 1 << 20
+
+
+def dg(a, b, ca, cb):
+    return lax.dot_general(a, b, (((ca,), (cb,)), ((), ())), preferred_element_type=F32)
+
+
+def rows128(i):
+    return pl.ds(pl.multiple_of(i * 128, 128), 128)
+
+
+def inverse_norm(v, floor_value):
+    return lax.rsqrt(jnp.mean(v * v, axis=-1, keepdims=True) + floor_value)
+
+
+def norm_slope(v, d, floor_value):
+    inv = inverse_norm(v, floor_value)
+    inner = jnp.mean(d * v, axis=-1, keepdims=True)
+    return inv * (d - v * (inner * inv * inv))
+
+
+class Place:
+    def __init__(self):
+        x, k, z = lax.axis_index("fsdp"), lax.axis_index("ctx"), lax.axis_index("tp")
+        self.x, self.k, self.z = x, k, z
+        self.y, self.c = k // 2, k % 2
+        self.t, self.zh = z % 2, z // 2
+        self.r = x * 4 + k
+        self.peer = {
+            "X": (1 - x, k, z),
+            "Y": (x, (k + 2) % 4, z),
+            "C": (x, k + 1 - 2 * self.c, z),
+            "P": (x, k, z + 1 - 2 * self.t),
+            "Q": (x, k, (z + 2) % 4),
+        }
+
+    def flip(self, r, axis):
+        if axis == "X":
+            return (r + 4) % 8
+        if axis == "Y":
+            return r + 2 - 4 * ((r // 2) % 2)
+        return r + 1 - 2 * (r % 2)
+
+    def greet(self):
+        bar = pltpu.get_barrier_semaphore()
+        for peer in self.peer.values():
+            pl.semaphore_signal(bar, inc=1, device_id=peer, device_id_type=MESH)
+
+    def meet(self):
+        pl.semaphore_wait(pltpu.get_barrier_semaphore(), len(self.peer))
+
+
+class Links:
+    def __init__(self, place, send, recv, local):
+        self.place, self.send, self.recv, self.local = place, send, recv, local
+        self.n = self.m = 0
+        self.sent, self.kept = [], []
+
+    def remote(self, src, dst, peer):
+        cp = pltpu.make_async_remote_copy(
+            src_ref=src,
+            dst_ref=dst,
+            send_sem=self.send.at[self.n],
+            recv_sem=self.recv.at[self.n],
+            device_id=self.place.peer[peer],
+            device_id_type=MESH,
+        )
+        self.n += 1
+        return cp
+
+    def go(self, src, dst, peer):
+        cp = self.remote(src, dst, peer)
+        cp.start()
+        self.sent.append(cp)
+        return cp
+
+    def keep(self, src, dst):
+        cp = pltpu.make_async_copy(src, dst, self.local.at[self.m])
+        self.m += 1
+        cp.start()
+        self.kept.append(cp)
+        return cp
+
+    def fetch(self, src, dst):
+        cp = pltpu.make_async_copy(src, dst, self.local.at[self.m])
+        self.m += 1
+        cp.start()
+        return cp
+
+    def drain(self):
+        for cp in self.sent:
+            cp.wait_send()
+        for cp in self.kept:
+            cp.wait()
+
+
+class Gather:
+    def __init__(self, links, order, view, own=None):
+        self.links, self.view = links, view
+        pc = links.place
+        self.pc, self.own = pc, own
+        self.first, self.second = ("X", "Y") if order == "A" else ("Y", "X")
+        self.rf = pc.flip(pc.r, self.first)
+        self.rs = pc.flip(pc.r, self.second)
+        self.rfs = pc.flip(self.rf, self.second)
+        self.cps = [{}, {}]
+
+    def put(self, slot, name, r, peer, src=None):
+        b = self.pc.zh if slot == 0 else 1 - self.pc.zh
+        src = self.view(b, r) if src is None else src
+        self.cps[slot][name] = self.links.go(src, self.view(b, r), peer)
+
+    def launch(self, slot, src=None):
+        r = self.pc.r
+        self.put(slot, "f", r, self.first, src)
+        self.put(slot, "sa", r, self.second, src)
+        self.put(slot, "c0", r, "C", src)
+
+    def start(self):
+        self.put(0, "z", self.pc.r, "Q", self.own)
+        self.launch(0, self.own)
+
+    def other(self):
+        self.cps[0]["z"].wait_recv()
+        self.launch(1)
+
+    def step1(self, slot):
+        self.cps[slot]["f"].wait_recv()
+        self.put(slot, "sb", self.rf, self.second)
+        self.put(slot, "c1", self.rf, "C")
+
+    def step2(self, slot):
+        self.cps[slot]["sa"].wait_recv()
+        self.put(slot, "c2", self.rs, "C")
+        self.cps[slot]["sb"].wait_recv()
+        self.put(slot, "c3", self.rfs, "C")
+
+    def step3(self, slot):
+        for name in ("c0", "c1", "c2", "c3"):
+            self.cps[slot][name].wait_recv()
+
+
+def last_id(ids, kk, half, s):
+    at = 255 + 256 * half
+    return ids[kk, s : s + 1, at : at + 1]
+
+
+def prior_id(pc, ids, s):
+    before = jnp.where(pc.zh == 1, last_id(ids, pc.k, 0, s), last_id(ids, (pc.k + 3) % 4, 1, s))
+    return jnp.where((pc.zh == 1) | (pc.k > 0), before, -1.0)
+
+
+def same(a, b):
+    return jnp.where(a == b, 1.0, 0.0)
+
+
+def fill_decay(rate, grid, wend, gin):
+    ti = lax.broadcasted_iota(jnp.int32, (CH, CH), 0).astype(F32)
+    si = lax.broadcasted_iota(jnp.int32, (CH, CH), 1).astype(F32)
+    dist = ti - si
+    pos = lax.broadcasted_iota(jnp.int32, (CH, DH), 0).astype(F32)
+
+    def head(h, _):
+        lane = rate[h, 0:1, :]
+        both = jnp.concatenate([lane, lane], axis=1)
+        grid[h] = jnp.where(dist >= 0.0, jnp.exp(-both * jnp.maximum(dist, 0.0)), 0.0)
+        wend[h] = jnp.exp(-lane * (CH - 1.0 - pos))
+        gin[h] = jnp.exp(-lane * (pos + 1.0))
+        return 0
+
+    lax.fori_loop(0, 4, head, 0)
+
+
+def fill_masks(pc, ids, mask, endf, inf):
+    for s in range(2):
+        row = ids[pc.k, s : s + 1, pl.ds(pl.multiple_of(pc.zh * CH, CH), CH)]
+        along = jnp.broadcast_to(row, (CH, CH))
+        down = along.T
+        mask[s] = same(along, down)
+        col = down[:, :DH]
+        endf[s] = same(col, jnp.broadcast_to(row[:, CH - 1 : CH], (CH, DH)))
+        inf[s] = same(col, jnp.broadcast_to(prior_id(pc, ids, s), (CH, DH)))
+
+
+def attn_forward(
+    rate_in, tok, cot, seg, wq, wk, wv, wg, wo_in, gl, gr, gd,
+    n1_o, ct_o, n2_o, x1_o, proj_o, qkv_o, p_o, att_o, mix_o, sb_o, w_o, wo_o,
+    gl_o, gr_o, gd_o, ids_o, rate_o,
+    n1, ct, n2, x1, proj, qkv, pm, att, mix, sb, wb, wo, glb, grb, gdb,
+    ids, rate, grid, wend, gin, mask, endf, inf, uf, us, ur, ts, tr, vs, vr, pf,
+    br_s, br_r, send, recv, local,
+):
+    pc = Place()
+    pc.greet()
+    ln = Links(pc, send, recv, local)
+    own, r = pc.zh, pc.r
+
+    for i, w in enumerate((wk, wv, wq, wg)):
+        wb[i, own, rows128(r), :] = w[...].astype(BF)
+    ids[pc.k] = jnp.zeros((8, 512), F32)
+    ids[pc.k, 0:2, :] = seg[...].astype(F32)
+    for hh in range(2):
+        rate[own * 2 + hh] = jnp.full((8, DH), rate_in[hh], F32)
+    for s in range(2):
+        xf = tok[s].astype(F32)
+        n1[pl.ds(pl.multiple_of(s * CH + pc.t * 128, 128), 128), :] = (
+            xf * inverse_norm(xf, EPSILON)
+        ).astype(BF)
+        ct[pl.ds(pl.multiple_of(s * CH + pc.t * 128, 128), 128), :] = cot[s]
+    pc.meet()
+
+    def mine(s):
+        return pl.ds(pl.multiple_of(s * CH + pc.t * 128, 128), 128)
+
+    def theirs(s):
+        return pl.ds(pl.multiple_of(s * CH + (1 - pc.t) * 128, 128), 128)
+
+    def wview(i):
+        return lambda b, rr: wb.at[i, b, rows128(rr), :]
+
+    qkvg = [Gather(ln, "AB"[i % 2], wview(i)) for i in range(4)]
+    for g in qkvg:
+        g.start()
+    rate_cp = ln.go(rate.at[pl.ds(own * 2, 2)], rate.at[pl.ds(own * 2, 2)], "Q")
+    ids_y = ln.go(ids.at[pc.k], ids.at[pc.k], "Y")
+    ids_c = ln.go(ids.at[pc.k], ids.at[pc.k], "C")
+    n1_cp = [ln.go(n1.at[mine(s)], n1.at[mine(s)], "P") for s in range(2)]
+
+    wo[pl.ds(pl.multiple_of(own * 256, 256), 256), rows128(r)] = wo_in[...].astype(BF)
+    glb[...] = gl[...].astype(BF)
+    grb[...] = gr[...].astype(BF)
+    gdb[...] = gd[...].astype(BF)
+
+    kf = (pc.k + 2) % 4
+    ids_y.wait_recv()
+    ids_f = ln.go(ids.at[kf], ids.at[kf], "C")
+    rate_cp.wait_recv()
+    fill_decay(rate, grid, wend, gin)
+
+    for g in qkvg:
+        g.step1(0)
+    for g in qkvg:
+        g.other()
+    ids_c.wait_recv()
+    ids_f.wait_recv()
+    fill_masks(pc, ids, mask, endf, inf)
+    for g in qkvg:
+        g.step2(0)
+    for g in qkvg:
+        g.step1(1)
+    for g in qkvg:
+        g.step3(0)
+    for g in qkvg:
+        g.step2(1)
+
+    gather_o = Gather(ln, "A", lambda b, rr: wo.at[pl.ds(pl.multiple_of(b * 256, 256), 256), rows128(rr)])
+    gather_l = Gather(ln, "A", lambda b, rr: gl_o.at[b, rows128(rr), :], glb)
+    gather_r = Gather(ln, "B", lambda b, rr: gr_o.at[b, rows128(rr), :], grb)
+    gather_d = Gather(ln, "A", lambda b, rr: gd_o.at[b, :, rows128(rr)], gdb)
+    later = [gather_o, gather_l, gather_r, gather_d]
+    for g in later:
+        g.start()
+    ln.keep(glb, gl_o.at[own, rows128(r), :])
+    ln.keep(grb, gr_o.at[own, rows128(r), :])
+    ln.keep(gdb, gd_o.at[own, :, rows128(r)])
+    ct_cp = [ln.go(ct.at[mine(s)], ct.at[mine(s)], "P") for s in range(2)]
+    for cp in n1_cp:
+        cp.wait_recv()
+
+    def project(i):
+        def block(b, _):
+            p = dg(n1[...], wb[i, b], 1, 0)
+            for hh in range(2):
+                h = b * 2 + hh
+                part = p[:, hh * DH : (hh + 1) * DH]
+                if i == 1:
+                    qkv[1, h] = part.astype(BF)
+                elif i == 3:
+                    proj[2, h] = part
+                else:
+                    proj[i // 2, h] = part
+                    qkv[i, h] = (part * jax.nn.sigmoid(part)).astype(BF)
+            return 0
+
+        lax.fori_loop(0, 2, block, 0)
+
+    for i in range(4):
+        qkvg[i].step3(1)
+        project(i)
+        if i == 1:
+            for s in range(2):
+                rs_ = pl.ds(s * CH, CH)
+
+                def state(h, _):
+                    kw = (qkv[0, h, rs_, :].astype(F32) * (wend[h] * endf[s])).astype(BF)
+                    u = dg(kw, qkv[1, h, rs_, :], 0, 0)
+                    uf[s, h] = u
+                    us[s, h] = u.astype(BF)
+                    return 0
+
+                lax.fori_loop(0, 4, state, 0)
+            u_cp = [ln.go(us.at[s], ur.at[s], "Q") for s in range(2)]
+    for i in range(4):
+        ln.keep(wb.at[i], w_o.at[i])
+    ln.keep(n1, n1_o)
+    ln.keep(proj, proj_o)
+    ln.keep(qkv, qkv_o)
+    ln.keep(ids, ids_o)
+    ln.keep(rate, rate_o)
+    for g in later:
+        g.step1(0)
+
+    for s in range(2):
+        rs_ = pl.ds(s * CH, CH)
+
+        def inside(h, _):
+            sc = dg(qkv[2, h, rs_, :], qkv[0, h, rs_, :], 1, 1)
+            p = (sc * grid[h] * mask[s]).astype(BF)
+            pm[s, h] = p
+            att[h, rs_, :] = dg(p, qkv[1, h, rs_, :], 1, 0)
+            return 0
+
+        lax.fori_loop(0, 4, inside, 0)
+    ln.keep(pm, p_o)
+    for g in later:
+        g.other()
+
+    t_cp, v_cp = [], []
+    for s in range(2):
+        u_cp[s].wait_recv()
+        fl = same(last_id(ids, pc.k, 0, s), last_id(ids, pc.k, 1, s))
+
+        def pair(h, _):
+            lane = jnp.exp(-CH * rate[h, 0:1, :]) * fl
+            got = ur[s, h].astype(F32)
+            wo_ = jnp.where(pc.zh == 1, jnp.ones_like(lane), lane)
+            wr_ = jnp.where(pc.zh == 1, lane, jnp.ones_like(lane))
+            tot = wo_ * uf[s, h] + wr_ * got
+            pf[s, h] = jnp.where(pc.zh == 1, got, jnp.zeros_like(got))
+            uf[s, h] = tot
+            ts[s, h] = tot.astype(BF)
+            return 0
+
+        lax.fori_loop(0, 4, pair, 0)
+        t_cp.append(ln.go(ts.at[s], tr.at[s], "C"))
+    for g in later:
+        g.step2(0)
+    for s in range(2):
+        t_cp[s].wait_recv()
+        prior = prior_id(pc, ids, s)
+        low = last_id(ids, pc.y * 2, 1, s)
+        fl = same(low, last_id(ids, pc.y * 2 + 1, 1, s))
+        fp = same(low, prior) * jnp.where(pc.c == 1, 1.0, 0.0)
+
+        def quad(h, _):
+            one = rate[h, 0:1, :]
+            lane = jnp.exp(-2.0 * CH * one) * fl
+            got = tr[s, h].astype(F32)
+            wo_ = jnp.where(pc.c == 1, jnp.ones_like(lane), lane)
+            wr_ = jnp.where(pc.c == 1, lane, jnp.ones_like(lane))
+            vs[s, h] = (wo_ * uf[s, h] + wr_ * got).astype(BF)
+            pf[s, h] = pf[s, h] + (jnp.exp(-(CH * 1.0) * pc.zh.astype(F32) * one) * fp) * got
+            return 0
+
+        lax.fori_loop(0, 4, quad, 0)
+        v_cp.append(ln.go(vs.at[s], vr.at[s], "Y"))
+    for g in later:
+        g.step1(1)
+    for s in range(2):
+        v_cp[s].wait_recv()
+        fp = same(last_id(ids, 1, 1, s), prior_id(pc, ids, s)) * jnp.where(pc.y == 1, 1.0, 0.0)
+        far = (2 * pc.c + pc.zh).astype(F32) * CH
+        rs_ = pl.ds(s * CH, CH)
+
+        def enter(h, _):
+            got = vr[s, h].astype(F32)
+            st = pf[s, h] + (jnp.exp(-far * rate[h, 0:1, :]) * fp) * got
+            low_st = st.astype(BF)
+            sb[s, h] = low_st
+            o = att[h, rs_, :] + (gin[h] * inf[s]) * dg(qkv[2, h, rs_, :], low_st, 1, 0)
+            att[h, rs_, :] = o
+            on = o * inverse_norm(o, HEAD_FLOOR)
+            mix[rs_, rows128(h)] = (on * jax.nn.sigmoid(proj[2, h, rs_, :])).astype(BF)
+            return 0
+
+        lax.fori_loop(0, 4, enter, 0)
+        if s == 0:
+            gather_o.step3(0)
+            gather_o.step2(1)
+            gather_o.step3(1)
+            b_cp = []
+        br_s[s] = dg(mix[theirs(s), :], wo[...], 1, 0).astype(BF)
+        b_cp.append(ln.go(br_s.at[s], br_r.at[s], "P"))
+        x1[s] = tok[s].astype(F32) + dg(mix[mine(s), :], wo[...], 1, 0)
+    ln.keep(att, att_o)
+    ln.keep(mix, mix_o)
+    ln.keep(sb, sb_o)
+    ln.keep(wo, wo_o)
+    n2_cp = []
+    for s in range(2):
+        b_cp[s].wait_recv()
+        v = x1[s] + br_r[s].astype(F32)
+        x1[s] = v
+        n2[mine(s), :] = (v * inverse_norm(v, EPSILON)).astype(BF)
+        n2_cp.append(ln.go(n2.at[mine(s)], n2.at[mine(s)], "P"))
+    ln.keep(x1, x1_o)
+    for g in later[1:]:
+        g.step2(1)
+    for g in later[1:]:
+        g.step3(0)
+        g.step3(1)
+    for cp in ct_cp:
+        cp.wait_recv()
+    ln.keep(ct, ct_o)
+    for cp in n2_cp:
+        cp.wait_recv()
+    ln.keep(n2, n2_o)
+    ln.drain()
+
+
+def call_forward(rate, tok, cot, seg, ws, wo, gl, gr, gd):
+    sd = jax.ShapeDtypeStruct
+    ff = gl.shape[1]
+    vm = pltpu.VMEM
+    outs = [
+        sd((512, 1024), BF),
+        sd((512, 1024), BF),
+        sd((512, 1024), BF),
+        sd((2, 128, 1024), F32),
+        sd((3, 4, 512, DH), F32),
+        sd((3, 4, 512, DH), BF),
+        sd((2, 4, CH, CH), BF),
+        sd((4, 512, DH), F32),
+        sd((512, 512), BF),
+        sd((2, 4, DH, DH), BF),
+        sd((4, 2, 1024, 256), BF),
+        sd((512, 1024), BF),
+        sd((2, 1024, ff), BF),
+        sd((2, 1024, ff), BF),
+        sd((2, ff, 1024), BF),
+        sd((4, 8, 512), F32),
+        sd((4, 8, DH), F32),
+    ]
+    scratch = [
+        vm((512, 1024), BF), vm((512, 1024), BF), vm((512, 1024), BF), vm((2, 128, 1024), F32),
+        vm((3, 4, 512, DH), F32), vm((3, 4, 512, DH), BF), vm((2, 4, CH, CH), BF),
+        vm((4, 512, DH), F32), vm((512, 512), BF), vm((2, 4, DH, DH), BF),
+        vm((4, 2, 1024, 256), BF), vm((512, 1024), BF),
+        vm((128, ff), BF), vm((128, ff), BF), vm((ff, 128), BF),
+        vm((4, 8, 512), F32), vm((4, 8, DH), F32),
+        vm((4, CH, CH), F32), vm((4, CH, DH), F32), vm((4, CH, DH), F32),
+        vm((2, CH, CH), F32), vm((2, CH, DH), F32), vm((2, CH, DH), F32),
+        vm((2, 4, DH, DH), F32), vm((2, 4, DH, DH), BF), vm((2, 4, DH, DH), BF),
+        vm((2, 4, DH, DH), BF), vm((2, 4, DH, DH), BF), vm((2, 4, DH, DH), BF), vm((2, 4, DH, DH), BF),
+        vm((2, 4, DH, DH), F32),
+        vm((2, 128, 1024), BF), vm((2, 128, 1024), BF),
+        pltpu.SemaphoreType.DMA((144,)), pltpu.SemaphoreType.DMA((144,)), pltpu.SemaphoreType.DMA((24,)),
+    ]
+    vin = pl.BlockSpec(memory_space=pltpu.VMEM)
+    return pl.pallas_call(
+        attn_forward,
+        out_shape=outs,
+        in_specs=[pl.BlockSpec(memory_space=pltpu.SMEM)] + [vin] * 11,
+        out_specs=[pl.BlockSpec(memory_space=pl.ANY)] * len(outs),
+        scratch_shapes=scratch,
+        compiler_params=pltpu.CompilerParams(
+            collective_id=0, has_side_effects=True, vmem_limit_bytes=60 * MIB
+        ),
+        name="attention_forward",
+    )(rate, tok, cot, seg, *ws, wo, gl, gr, gd)
+
+
+class Scatter:
+    def __init__(self, links, order, kind, bufs):
+        self.links, self.kind = links, kind
+        pc = links.place
+        self.pc = pc
+        self.acc, self.sc, self.rc, self.sf, self.rf, self.ss, self.rs, self.sz, self.rz, self.tile = bufs
+        if order == "A":
+            self.first, self.second, self.fv, self.sv = "X", "Y", pc.x, pc.y
+            self.at = lambda f, m: 2 * f + m
+        else:
+            self.first, self.second, self.fv, self.sv = "Y", "X", pc.y, pc.x
+            self.at = lambda f, m: 2 * m + f
+        self.c_cp, self.f_cp, self.s_cp = {}, {}, {}
+
+    def part(self, half):
+        return self.tile[rows128(half), :] if self.kind == "rows" else self.tile[:, rows128(half)]
+
+    def core_stage(self, b, product):
+        def pair(i, _):
+            self.tile[...] = product(b, i)
+            self.sc[b, i] = self.part(1 - self.pc.c).astype(BF)
+            self.acc[b, i] = self.part(self.pc.c)
+            return 0
+
+        lax.fori_loop(0, 4, pair, 0)
+        self.c_cp[b] = self.links.go(self.sc.at[b], self.rc.at[b], "C")
+
+    def first_stage(self, b):
+        self.c_cp[b].wait_recv()
+        for m in range(2):
+            away, here = self.at(1 - self.fv, m), self.at(self.fv, m)
+            self.sf[b, m] = (self.acc[b, away] + self.rc[b, away].astype(F32)).astype(BF)
+        self.f_cp[b] = self.links.go(self.sf.at[b], self.rf.at[b], self.first)
+        for m in range(2):
+            here = self.at(self.fv, m)
+            self.acc[b, here] = self.acc[b, here] + self.rc[b, here].astype(F32)
+
+    def second_stage(self, b):
+        self.f_cp[b].wait_recv()
+        away, here = self.at(self.fv, 1 - self.sv), self.at(self.fv, self.sv)
+        self.ss[b] = (self.acc[b, away] + self.rf[b, 1 - self.sv].astype(F32)).astype(BF)
+        self.s_cp[b] = self.links.go(self.ss.at[b], self.rs.at[b], self.second)
+        self.acc[b, here] = self.acc[b, here] + self.rf[b, self.sv].astype(F32)
+
+    def plane_stage(self):
+        here = self.at(self.fv, self.sv)
+        away = 1 - self.pc.zh
+        for b in range(2):
+            self.s_cp[b].wait_recv()
+        self.sz[...] = (self.acc[away, here] + self.rs[away].astype(F32)).astype(BF)
+        self.z_cp = self.links.go(self.sz, self.rz, "Q")
+
+    def total(self):
+        here = self.at(self.fv, self.sv)
+        zh = self.pc.zh
+        self.z_cp.wait_recv()
+        return self.acc[zh, here] + self.rs[zh].astype(F32) + self.rz[...].astype(F32)
+
+
+def scatter_bufs(slab, tile):
+    vm = pltpu.VMEM
+    return [
+        vm((2, 4) + slab, F32), vm((2, 4) + slab, BF), vm((2, 4) + slab, BF),
+        vm((2, 2) + slab, BF), vm((2, 2) + slab, BF), vm((2,) + slab, BF), vm((2,) + slab, BF),
+        vm(slab, BF), vm(slab, BF), vm(tile, F32),
+    ]
+
+
+def cols256(i):
+    return pl.ds(pl.multiple_of(i * 256, 256), 256)
+
+
+def glu(
+    n2_i, ct_i, x1_i, gl_i, gr_i, gd_i,
+    dr_o, dx1_o, fs_o, fo_o, dpr_o, gdown_o, gleft_o,
+    n2, ct, x1, gl, gr, gd, hid, dpl, dpr, tmp, dsend, drecv, dx1, dr, fs, fo, gdown, gleft,
+    *rest,
+):
+    down_b, left_b = rest[:10], rest[10:20]
+    send, recv, local = rest[20:]
+    pc = Place()
+    pc.greet()
+    ln = Links(pc, send, recv, local)
+    got = {}
+    got["n2"] = ln.fetch(n2_i, n2)
+    got["gl"] = ln.fetch(gl_i, gl)
+    got["gr"] = ln.fetch(gr_i, gr)
+    got["ct"] = ln.fetch(ct_i, ct)
+    got["gd"] = ln.fetch(gd_i, gd)
+    got["x1"] = ln.fetch(x1_i, x1)
+    pc.meet()
+
+    def mine(s):
+        return pl.ds(pl.multiple_of(s * CH + pc.t * 128, 128), 128)
+
+    for name in ("n2", "gl", "gr", "ct", "gd"):
+        got[name].wait()
+    d_cp = []
+    for s in range(2):
+        rs_ = pl.ds(s * CH, CH)
+
+        def block(b, _):
+            a = dg(n2[rs_, :], gl[b], 1, 0)
+            c = dg(n2[rs_, :], gr[b], 1, 0)
+            hid[b, rs_, :] = (a * c).astype(BF)
+            dh = dg(ct[rs_, :], gd[b], 1, 1)
+            dpl[b, rs_, :] = (dh * c).astype(BF)
+            dpr[b, rs_, :] = (dh * a).astype(BF)
+            return 0
+
+        lax.fori_loop(0, 2, block, 0)
+        tmp[...] = (
+            dg(dpl[0, rs_, :], gl[0], 1, 1) + dg(dpr[0, rs_, :], gr[0], 1, 1)
+            + dg(dpl[1, rs_, :], gl[1], 1, 1) + dg(dpr[1, rs_, :], gr[1], 1, 1)
+        )
+        dsend[s] = tmp[rows128(1 - pc.t), :].astype(BF)
+        d_cp.append(ln.go(dsend.at[s], drecv.at[s], "P"))
+        dx1[s] = tmp[rows128(pc.t), :]
+
+    down = Scatter(ln, "A", "cols", down_b)
+    left = Scatter(ln, "B", "rows", left_b)
+    for b in range(2):
+        down.core_stage(b, lambda b, i: dg(hid[b], ct[:, cols256(i)], 0, 0))
+    got["x1"].wait()
+    r_cp = []
+
+    def turn(s):
+        d_cp[s].wait_recv()
+        v = x1[s]
+        dn = dx1[s] + drecv[s].astype(F32)
+        g = ct[mine(s), :].astype(F32) + norm_slope(v, dn, EPSILON)
+        dx1[s] = g
+        dr[mine(s), :] = g.astype(BF)
+        r_cp.append(ln.go(dr.at[mine(s)], dr.at[mine(s)], "P"))
+
+    turn(0)
+    for b in range(2):
+        down.first_stage(b)
+    for b in range(2):
+        left.core_stage(b, lambda b, i: dg(n2[:, cols256(i)], dpl[b], 0, 0))
+    turn(1)
+    ln.keep(dx1, dx1_o)
+    ln.keep(dpr, dpr_o)
+    for s in range(2):
+        rs_ = pl.ds(s * CH, CH)
+        tmp[...] = dg(hid[0, rs_, :], gd[0], 1, 0) + dg(hid[1, rs_, :], gd[1], 1, 0)
+        fs[s] = tmp[rows128(1 - pc.t), :].astype(BF)
+        fo[s] = x1[s] + tmp[rows128(pc.t), :]
+    ln.keep(fs, fs_o)
+    ln.keep(fo, fo_o)
+    for b in range(2):
+        down.second_stage(b)
+    for b in range(2):
+        left.first_stage(b)
+    down.plane_stage()
+    for b in range(2):
+        left.second_stage(b)
+    left.plane_stage()
+    for cp in r_cp:
+        cp.wait_recv()
+    ln.keep(dr, dr_o)
+    gdown[...] = down.total()
+    ln.keep(gdown, gdown_o)
+    gleft[...] = left.total()
+    ln.keep(gleft, gleft_o)
+    ln.drain()
+
+
+def call_glu(n2, ct, x1, gl, gr, gd):
+    sd, vm = jax.ShapeDtypeStruct, pltpu.VMEM
+    ff = gl.shape[2]
+    outs = [
+        sd((512, 1024), BF), sd((2, 128, 1024), F32), sd((2, 128, 1024), BF),
+        sd((2, 128, 1024), F32), sd((2, 512, ff), BF), sd((ff, 128), F32), sd((128, ff), F32),
+    ]
+    scratch = [
+        vm((512, 1024), BF), vm((512, 1024), BF), vm((2, 128, 1024), F32),
+        vm((2, 1024, ff), BF), vm((2, 1024, ff), BF), vm((2, ff, 1024), BF),
+        vm((2, 512, ff), BF), vm((2, 512, ff), BF), vm((2, 512, ff), BF),
+        vm((CH, 1024), F32), vm((2, 128, 1024), BF), vm((2, 128, 1024), BF),
+        vm((2, 128, 1024), F32), vm((512, 1024), BF), vm((2, 128, 1024), BF),
+        vm((2, 128, 1024), F32), vm((ff, 128), F32), vm((128, ff), F32),
+        *scatter_bufs((ff, 128), (ff, 256)), *scatter_bufs((128, ff), (256, ff)),
+        pltpu.SemaphoreType.DMA((24,)), pltpu.SemaphoreType.DMA((24,)), pltpu.SemaphoreType.DMA((24,)),
+    ]
+    return pl.pallas_call(
+        glu,
+        out_shape=outs,
+        in_specs=[pl.BlockSpec(memory_space=pl.ANY)] * 6,
+        out_specs=[pl.BlockSpec(memory_space=pl.ANY)] * len(outs),
+        scratch_shapes=scratch,
+        compiler_params=pltpu.CompilerParams(
+            collective_id=1, has_side_effects=True, vmem_limit_bytes=62 * MIB
+        ),
+        name="glu",
+    )(n2, ct, x1, gl, gr, gd)
+
+
+def silu_slope(v):
+    g = jax.nn.sigmoid(v)
+    return g * (1.0 + v * (1.0 - g))
+
+
+N_BACK_IN = 18
+
+
+def attn_backward(*refs):
+    ins, refs = refs[:N_BACK_IN], refs[N_BACK_IN:]
+    outs, refs = refs[:8], refs[8:]
+    bufs, refs = refs[:N_BACK_IN], refs[N_BACK_IN:]
+    out_o, gtok_o, gq_o, gk_o, gv_o, gg_o, go_o, gr_o = outs
+    (dr, dx1, n1, n2, dpr, mix, wo, wb, proj, qkv, pm, att, sb, ids, rate, fs, fo, x) = bufs
+    (
+        grid, wend, gin, mask, endf, inf, dm, dob, dp, dki, dvi, vf, vs, vr, ts, tr, ws, wr, rf, du,
+        tmp, nsend, nrecv, frecv, outb, gtok, gw, gout, gright,
+    ) = refs[:29]
+    refs = refs[29:]
+    sc_bufs = [refs[10 * i : 10 * i + 10] for i in range(6)]
+    send, recv, local = refs[60:]
+    pc = Place()
+    pc.greet()
+    ln = Links(pc, send, recv, local)
+    got = [ln.fetch(a, b) for a, b in zip(ins, bufs)]
+    pc.meet()
+    for cp in got:
+        cp.wait()
+    f_cp = ln.go(fs, frecv, "P")
+    fill_decay(rate, grid, wend, gin)
+    fill_masks(pc, ids, mask, endf, inf)
+
+    def mine(s):
+        return pl.ds(pl.multiple_of(s * CH + pc.t * 128, 128), 128)
+
+    def through(b, _):
+        dm[:, cols256(b)] = dg(dr[...], wo[cols256(b), :], 1, 1)
+        return 0
+
+    lax.fori_loop(0, 2, through, 0)
+    v_cp = []
+    for s in range(2):
+        rs_ = pl.ds(s * CH, CH)
+
+        def outer(h, _):
+            d, o = dm[rs_, rows128(h)], att[h, rs_, :]
+            g = jax.nn.sigmoid(proj[2, h, rs_, :])
+            inv = inverse_norm(o, HEAD_FLOOR)
+            dp[3, rs_, rows128(h)] = (d * (o * inv) * g * (1.0 - g)).astype(BF)
+            e = d * g
+            inner = jnp.mean(e * o, axis=-1, keepdims=True)
+            do = (inv * (e - o * (inner * inv * inv))).astype(BF)
+            dob[h, rs_, :] = do
+            gq = (qkv[2, h, rs_, :].astype(F32) * (gin[h] * inf[s])).astype(BF)
+            v = dg(gq, do, 0, 0)
+            vf[s, h] = v
+            vs[s, h] = v.astype(BF)
+            return 0
+
+        lax.fori_loop(0, 4, outer, 0)
+        v_cp.append(ln.go(vs.at[s], vr.at[s], "Q"))
+
+    right = Scatter(ln, "A", "rows", sc_bufs[0])
+    s_out = Scatter(ln, "B", "cols", sc_bufs[1])
+    s_w = [Scatter(ln, "AB"[i % 2], "rows", sc_bufs[2 + i]) for i in range(4)]
+
+    def product(i):
+        return lambda b, j: dg(n1[:, cols256(j)], dp[i, :, cols256(b)], 0, 0)
+
+    for b in range(2):
+        right.core_stage(b, lambda b, i: dg(n2[:, cols256(i)], dpr[b], 0, 0))
+    for b in range(2):
+        right.first_stage(b)
+
+    for s in range(2):
+        rs_ = pl.ds(s * CH, CH)
+
+        def inside(h, _):
+            do, q, k = dob[h, rs_, :], qkv[2, h, rs_, :], qkv[0, h, rs_, :]
+            dsc = (dg(do, qkv[1, h, rs_, :], 1, 1) * grid[h] * mask[s]).astype(BF)
+            dq = dg(dsc, k, 1, 0) + (gin[h] * inf[s]) * dg(do, sb[s, h], 1, 1)
+            dp[2, rs_, rows128(h)] = (dq * silu_slope(proj[1, h, rs_, :])).astype(BF)
+            dki[h, rs_, :] = dg(dsc, q, 0, 0)
+            dvi[h, rs_, :] = dg(pm[s, h], do, 0, 0)
+            return 0
+
+        lax.fori_loop(0, 4, inside, 0)
+
+    for b in range(2):
+        s_out.core_stage(b, lambda b, i: dg(mix[:, cols256(b)], dr[:, cols256(i)], 0, 0))
+    for i in (3, 2):
+        for b in range(2):
+            s_w[i].core_stage(b, product(i))
+    for b in range(2):
+        right.second_stage(b)
+        s_out.first_stage(b)
+
+    t_cp, w_cp = [], []
+    for s in range(2):
+        v_cp[s].wait_recv()
+        before = jnp.where(pc.k > 0, last_id(ids, (pc.k + 3) % 4, 1, s), -1.0)
+        fb = same(before, last_id(ids, pc.k, 0, s))
+
+        def pair(h, _):
+            lane = jnp.exp(-CH * rate[h, 0:1, :]) * fb
+            g = vr[s, h].astype(F32)
+            wo_ = jnp.where(pc.zh == 0, jnp.ones_like(lane), lane)
+            wr_ = jnp.where(pc.zh == 0, lane, jnp.ones_like(lane))
+            tot = wo_ * vf[s, h] + wr_ * g
+            rf[s, h] = jnp.where(pc.zh == 0, g, jnp.zeros_like(g))
+            vf[s, h] = tot
+            ts[s, h] = tot.astype(BF)
+            return 0
+
+        lax.fori_loop(0, 4, pair, 0)
+        t_cp.append(ln.go(ts.at[s], tr.at[s], "C"))
+    for i in (3, 2):
+        for b in range(2):
+            s_w[i].first_stage(b)
+    for s in range(2):
+        t_cp[s].wait_recv()
+        low = last_id(ids, pc.y * 2, 1, s)
+        before = jnp.where(pc.y > 0, last_id(ids, (pc.y * 2 + 3) % 4, 1, s), -1.0)
+        fb = same(before, low)
+        here = jnp.where(pc.zh == 1, last_id(ids, pc.k, 1, s), last_id(ids, pc.k, 0, s))
+        fp = same(here, low) * jnp.where(pc.c == 0, 1.0, 0.0)
+        far = (1 - pc.zh).astype(F32) * CH
+
+        def quad(h, _):
+            one = rate[h, 0:1, :]
+            lane = jnp.exp(-2.0 * CH * one) * fb
+            g = tr[s, h].astype(F32)
+            wo_ = jnp.where(pc.c == 0, jnp.ones_like(lane), lane)
+            wr_ = jnp.where(pc.c == 0, lane, jnp.ones_like(lane))
+            ws[s, h] = (wo_ * vf[s, h] + wr_ * g).astype(BF)
+            rf[s, h] = rf[s, h] + (jnp.exp(-far * one) * fp) * g
+            return 0
+
+        lax.fori_loop(0, 4, quad, 0)
+        w_cp.append(ln.go(ws.at[s], wr.at[s], "Y"))
+    for b in range(2):
+        s_out.second_stage(b)
+    n_cp = []
+    for s in range(2):
+        w_cp[s].wait_recv()
+        here = jnp.where(pc.zh == 1, last_id(ids, pc.k, 1, s), last_id(ids, pc.k, 0, s))
+        fp = same(here, last_id(ids, 1, 1, s)) * jnp.where(pc.y == 0, 1.0, 0.0)
+        far = (2 * (1 - pc.c) + (1 - pc.zh)).astype(F32) * CH
+        rs_ = pl.ds(s * CH, CH)
+
+        def close(h, _):
+            d = (rf[s, h] + (jnp.exp(-far * rate[h, 0:1, :]) * fp) * wr[s, h].astype(F32)).astype(BF)
+            k, v = qkv[0, h, rs_, :], qkv[1, h, rs_, :]
+            w = wend[h] * endf[s]
+            kw = (k.astype(F32) * w).astype(BF)
+            dp[1, rs_, rows128(h)] = (dvi[h, rs_, :] + dg(kw, d, 1, 0)).astype(BF)
+            dk = dki[h, rs_, :] + w * dg(v, d, 1, 1)
+            dp[0, rs_, rows128(h)] = (dk * silu_slope(proj[0, h, rs_, :])).astype(BF)
+            return 0
+
+        lax.fori_loop(0, 4, close, 0)
+        acc = None
+        for i in range(4):
+            for b in range(2):
+                p = dg(dp[i, rs_, b * 256 : (b + 1) * 256], wb[i, b], 1, 1)
+                acc = p if acc is None else acc + p
+        tmp[...] = acc
+        nsend[s] = tmp[rows128(1 - pc.t), :].astype(BF)
+        n_cp.append(ln.go(nsend.at[s], nrecv.at[s], "P"))
+        gtok[s] = tmp[rows128(pc.t), :]
+    for i in (0, 1):
+        for b in range(2):
+            s_w[i].core_stage(b, product(i))
+    for i in (3, 2):
+        for b in range(2):
+            s_w[i].second_stage(b)
+    right.plane_stage()
+    s_out.plane_stage()
+    for i in (0, 1):
+        for b in range(2):
+            s_w[i].first_stage(b)
+    for i in (3, 2):
+        s_w[i].plane_stage()
+    f_cp.wait_recv()
+    outb[...] = (fo[...] + frecv[...].astype(F32)).astype(BF)
+    ln.keep(outb, out_o)
+    for s in range(2):
+        n_cp[s].wait_recv()
+        dn = gtok[s] + nrecv[s].astype(F32)
+        gtok[s] = dx1[s] + norm_slope(x[s].astype(F32), dn, EPSILON)
+    ln.keep(gtok, gtok_o)
+    for i in (0, 1):
+        for b in range(2):
+            s_w[i].second_stage(b)
+    gright[...] = right.total()
+    ln.keep(gright, gr_o)
+    for i in (0, 1):
+        s_w[i].plane_stage()
+    gout[...] = s_out.total()
+    ln.keep(gout, go_o)
+    for i, o in ((3, gg_o), (2, gq_o), (0, gk_o), (1, gv_o)):
+        gw[i] = s_w[i].total()
+        ln.keep(gw.at[i], o)
+    ln.drain()
+
+
+def call_backward(*args):
+    sd, vm = jax.ShapeDtypeStruct, pltpu.VMEM
+    ff = args[4].shape[2]
+    outs = [
+        sd((2, 128, 1024), BF), sd((2, 128, 1024), F32),
+        sd((128, 256), F32), sd((128, 256), F32), sd((128, 256), F32), sd((128, 256), F32),
+        sd((256, 128), F32), sd((128, ff), F32),
+    ]
+    st = (2, 4, DH, DH)
+    scratch = [vm(a.shape, a.dtype) for a in args] + [
+        vm((4, CH, CH), F32), vm((4, CH, DH), F32), vm((4, CH, DH), F32),
+        vm((2, CH, CH), F32), vm((2, CH, DH), F32), vm((2, CH, DH), F32),
+        vm((512, 512), F32), vm((4, 512, DH), BF), vm((4, 512, 512), BF),
+        vm((4, 512, DH), F32), vm((4, 512, DH), F32),
+        vm(st, F32), vm(st, BF), vm(st, BF), vm(st, BF), vm(st, BF), vm(st, BF), vm(st, BF),
+        vm(st, F32), vm((8, 128), BF),
+        vm((CH, 1024), F32), vm((2, 128, 1024), BF), vm((2, 128, 1024), BF), vm((2, 128, 1024), BF),
+        vm((2, 128, 1024), BF), vm((2, 128, 1024), F32), vm((4, 128, 256), F32),
+        vm((256, 128), F32), vm((128, ff), F32),
+        *scatter_bufs((128, ff), (256, ff)), *scatter_bufs((256, 128), (256, 256)),
+        *scatter_bufs((128, 256), (256, 256)), *scatter_bufs((128, 256), (256, 256)),
+        *scatter_bufs((128, 256), (256, 256)), *scatter_bufs((128, 256), (256, 256)),
+        pltpu.SemaphoreType.DMA((64,)), pltpu.SemaphoreType.DMA((64,)), pltpu.SemaphoreType.DMA((40,)),
+    ]
+    return pl.pallas_call(
+        attn_backward,
+        out_shape=outs,
+        in_specs=[pl.BlockSpec(memory_space=pl.ANY)] * len(args),
+        out_specs=[pl.BlockSpec(memory_space=pl.ANY)] * len(outs),
+        scratch_shapes=scratch,
+        compiler_params=pltpu.CompilerParams(
+            collective_id=2, has_side_effects=True, vmem_limit_bytes=63 * MIB
+        ),
+        name="attention_backward",
+    )(*args)
 
 
 def entering(x, axis, join, neutral):
@@ -66,7 +982,7 @@
     return inverse * (upstream - values * inner_mean * inverse * inverse)
 
 
-def silu_slope(values):
+def silu_grad(values):
     sigmoid_value = jax.nn.sigmoid(values)
     return sigmoid_value * (1.0 + values * (1.0 - sigmoid_value))
 
@@ -276,7 +1192,7 @@
     )
     weighted_queries = queries.astype(jnp.float32) * inflow[..., None]
     grad_prior_local = jnp.einsum(
-        "tbhd,tbhe->bhde", weighted_queries, grad_attended.astype(jnp.float32), precision=HIGHEST
+        "tbhd,tbhe->bhde", weighted_queries, grad_attended.astype(jnp.float32), precision=lax.Precision.HIGHEST
     )
     link_decay = jnp.where((first_seg == prior_last)[:, None], span_decay, 0.0)
     back_identity = (
@@ -287,22 +1203,22 @@
         1
     ]
     grad_values = grad_values + jnp.einsum(
-        "tbhd,bhde->tbhe", keys_end.astype(jnp.float32), grad_update, precision=HIGHEST
+        "tbhd,bhde->tbhe", keys_end.astype(jnp.float32), grad_update, precision=lax.Precision.HIGHEST
     )
     grad_keys = (
         grad_keys
         + jnp.einsum(
-            "tbhe,bhde->tbhd", values_low.astype(jnp.float32), grad_update, precision=HIGHEST
+            "tbhe,bhde->tbhd", values_low.astype(jnp.float32), grad_update, precision=lax.Precision.HIGHEST
         )
         * end_weight[..., None]
     )
     grad_query_proj = (
-        (grad_queries * silu_slope(proj_query).reshape(head_shape))
+        (grad_queries * silu_grad(proj_query).reshape(head_shape))
         .astype(jnp.bfloat16)
         .reshape(total_rows, local_width)
     )
     grad_key_proj = (
-        (grad_keys * silu_slope(proj_key).reshape(head_shape))
+        (grad_keys * silu_grad(proj_key).reshape(head_shape))
         .astype(jnp.bfloat16)
         .reshape(total_rows, local_width)
     )
@@ -356,6 +1272,27 @@
     )
 
 
+def paired(
+    tokens, segment_ids, decay_rate, w_query, w_key, w_value, w_gate, w_out,
+    glu_left, glu_right, glu_down, cotangent,
+):
+    tok, cot = tokens.transpose(1, 0, 2), cotangent.transpose(1, 0, 2)
+    (
+        n1, ct, n2, x1, proj, qkv, pm, att, mix, sb, wb, wo, gl, gr, gd, ids, rate,
+    ) = call_forward(
+        decay_rate, tok, cot, segment_ids, (w_query, w_key, w_value, w_gate), w_out,
+        glu_left, glu_right, glu_down,
+    )
+    dr, dx1, fs, fo, dpr, g_down, g_left = call_glu(n2, ct, x1, gl, gr, gd)
+    out, g_tok, g_q, g_k, g_v, g_g, g_o, g_right = call_backward(
+        dr, dx1, n1, n2, dpr, mix, wo, wb, proj, qkv, pm, att, sb, ids, rate, fs, fo, tok
+    )
+    return (
+        out.transpose(1, 0, 2), g_tok.transpose(1, 0, 2),
+        g_q, g_k, g_v, g_g, g_o, g_left, g_right, g_down,
+    )
+
+
 def solution(mesh):
     in_specs = (
         P(("ctx", "tp"), "fsdp", None),
@@ -383,4 +1320,6 @@
         P(("fsdp", "ctx"), "tp"),
         P("tp", ("fsdp", "ctx")),
     )
-    return jax.shard_map(shards, mesh=mesh, in_specs=in_specs, out_specs=out_specs, check_vma=False)
+    sizes = tuple(mesh.shape[a] for a in ("fsdp", "ctx", "tp"))
+    body = paired if sizes == (2, 4, 4) else shards
+    return jax.shard_map(body, mesh=mesh, in_specs=in_specs, out_specs=out_specs, check_vma=False)

time: 1040 us -> 289 us (0.28)
  waiting for transfers between devices: 710 us -> 0 us
  Pallas kernels: 0 us -> 270 us
  matrix products: 107 us -> 0 us
  blocking collectives: 87 us -> 0 us
  local copies, waits for them, and re-layouts: 92.6 us -> 17.6 us
  other arithmetic: 21.5 us -> 0 us
  between operations: 15.3 us -> 0.74 us
    reduce_scatter x12 -> x0, waiting for transfers between devices: 532 us -> none  [the longest x1 80.6 us: shards(): lax.psum_scatter(jnp.dot(piece_rows, full_out, preferred_element_type=jnp...]
    pallas_call x0 -> x3, Pallas kernels: none -> 270 us  [the longest x1 108 us: call_forward(): pl.pallas_call(attn_forward, out_shape=outs, in_specs=[pl.BlockSpec(memor...]
    all_gather x7 -> x0, waiting for transfers between devices: 177 us -> none  [the longest x1 42.1 us: shards(): second = lax.all_gather(second_part, 'tp', axis=0, tiled=True)]
    dot_general x36 -> x0, matrix products: 107 us -> none  [the longest x4 16.3 us: shards(): jnp.dot(piece_rows, weight_full.T, preferred_element_type=jnp.float32)]
    all_gather x11 -> x0, blocking collectives: 87 us -> none  [the longest x4 24.1 us: entering(): lax.all_gather(a.astype(kind), axis)]
    reshape x17 -> x0, local copies, waits for them, and re-layouts: 48.3 us -> none  [the longest x2 11.5 us: shards(): summed.reshape(row_count, seq_count, model_width)]
    convert_element_type x10 -> x0, local copies, waits for them, and re-layouts: 16.3 us -> none  [the longest x2 5.95 us: shards(): summed.reshape(row_count, seq_count, model_width).astype(jnp.bfloat16)]
    all_gather x5 -> x0, local copies, waits for them, and re-layouts: 14 us -> none  [the longest x1 5.19 us: shards(): second = lax.all_gather(second_part, 'tp', axis=0, tiled=True)]
  transfers between devices with their start and end apart: 19 -> 0, of which waited for: 17 -> 0; matrix products, arithmetic and copies ran while one was open for 9% -> 0% of each run, Pallas kernels for 0% -> 0%
where the time goes in v1:
time: 289 us
  Pallas kernels  270 us (93%)
  local copies, waits for them, and re-layouts  17.6 us (6%)
    pallas_call x1, Pallas kernels, call_forward(): pl.pallas_call(attn_forward, out_shape=outs, in_specs=[pl.BlockSpec(memor...  108 us
    pallas_call x1, Pallas kernels, call_backward(): pl.pallas_call(attn_backward, out_shape=outs, in_specs=[pl.BlockSpec(memo...  88 us
    pallas_call x1, Pallas kernels, call_glu(): pl.pallas_call(glu, out_shape=outs, in_specs=[pl.BlockSpec(memory_space=p...  74.5 us
    unnamed x28, local copies, waits for them, and re-layouts  15.1 us

profile of v1, /device:TPU:0, one launch (start us, length us, event | category | flops | bytes accessed | tf_op | source)
XLA Modules:
  0.0 288.7 jit_solution(9513023493050400235)
XLA Ops:
  0.6 1.9 copy.24.gl
  2.5 1.9 copy.25.gr
  4.4 2.4 copy_bitcast_fusion
  6.9 107.8 %attention_forward.1 = (bf16[512,1024]{1,0:T(8,128)(2,1)}, bf16[512,1024]{1,0:T(8,128)(2,1)}, bf16[512,1024]{1,0:T(8,128)(2,1)}, f32[2,128,1024]{2,1,0:T(8,128)}...) custom-call(f32[2]{0:T(128)} %rate_in.1, ...), custom_call_target="tpu_custom_call" | custom-call | tf_op jit(solution)/shard_map/attention_forward/pallas_call | solution.py:476
  114.7 74.5 %glu.1 = (bf16[512,1024]{1,0:T(8,128)(2,1)}, f32[2,128,1024]{2,1,0:T(8,128)}, bf16[2,128,1024]{2,1,0:T(8,128)(2,1)}, f32[2,128,1024]{2,1,0:T(8,128)}, bf16[2,512...) custom-call(bf16[512,1024]{1,0:T(8,128)(2,1)} %get-tuple-element.42.n2_i.refs_3_, ...), custom_call_target="tpu_custom_call" | custom-call | tf_op jit(solution)/shard_map/glu/pallas_call | solution.py:674
  189.2 88.0 %attention_backward.1 = (bf16[2,128,1024]{2,1,0:T(8,128)(2,1)}, f32[2,128,1024]{2,1,0:T(8,128)}, f32[128,256]{1,0:T(8,128)}, f32[128,256]{1,0:T(8,128)}, f32[128...) custom-call(bf16[512,1024]{1,0:T(8,128)(2,1)} %get-tuple-element.48.refs_0_, ...), custom_call_target="tpu_custom_call" | custom-call | tf_op jit(solution)/shard_map/attention_backward/pallas_call | solution.py:917
  277.2 0.0 copy-start.1
  277.2 0.0 copy-start
  277.3 0.0 copy-start.7
  277.3 0.0 copy-start.6
  277.3 0.0 copy-start.5
  277.3 0.0 copy-start.4
  277.3 0.0 copy-start.3
  277.3 0.0 copy-start.2
  277.3 2.5 copy.26
  279.8 3.0 %copy.27 = f32[128,2,1024]{2,1,0:T(2,128)} copy(f32[128,2,1024]{2,0,1:T(8,128)} %bitcast.6) | data formatting | bytes 2097152
  282.8 0.0 copy-done.1
  282.8 0.9 copy.29
  283.7 0.0 copy-done
  283.7 0.9 copy.28
  284.6 0.0 copy-done.7
  284.6 0.7 copy.38
  285.3 0.0 copy-done.6
  285.3 0.7 copy.39
  285.9 0.0 copy-done.5
  285.9 0.7 copy.40
  286.6 0.0 copy-done.4
  286.6 0.7 copy.41
  287.3 0.0 copy-done.3
  287.3 0.7 copy.42
  287.9 0.0 copy-done.2
  287.9 0.7 copy.43
Async XLA Ops:
  277.2 5.6 %copy-start.1 = (f32[128,704]{1,0:T(8,128)S(1)}, f32[128,704]{1,0:T(8,128)}, u32[]{:S(2)}) copy-start(f32[128,704]{1,0:T(8,128)} %get-tuple-element.82) | copy-start | bytes 1081348
  277.2 6.5 %copy-start = (f32[128,704]{1,0:T(8,128)S(1)}, f32[128,704]{1,0:T(8,128)}, u32[]{:S(2)}) copy-start(f32[128,704]{1,0:T(8,128)} %get-tuple-element.81) | copy-start | bytes 1081348
  277.3 7.4 %copy-start.7 = (f32[128,256]{1,0:T(8,128)S(1)}, f32[128,256]{1,0:T(8,128)}, u32[]{:S(2)}) copy-start(f32[128,256]{1,0:T(8,128)} %get-tuple-element.98) | copy-start | bytes 393220
  277.3 8.0 %copy-start.6 = (f32[128,256]{1,0:T(8,128)S(1)}, f32[128,256]{1,0:T(8,128)}, u32[]{:S(2)}) copy-start(f32[128,256]{1,0:T(8,128)} %get-tuple-element.99) | copy-start | bytes 393220
  277.3 8.7 %copy-start.5 = (f32[128,256]{1,0:T(8,128)S(1)}, f32[128,256]{1,0:T(8,128)}, u32[]{:S(2)}) copy-start(f32[128,256]{1,0:T(8,128)} %get-tuple-element.100) | copy-start | bytes 393220
  277.3 9.3 %copy-start.4 = (f32[128,256]{1,0:T(8,128)S(1)}, f32[128,256]{1,0:T(8,128)}, u32[]{:S(2)}) copy-start(f32[128,256]{1,0:T(8,128)} %get-tuple-element.101) | copy-start | bytes 393220
  277.3 10.0 %copy-start.3 = (f32[256,128]{1,0:T(8,128)S(1)}, f32[256,128]{1,0:T(8,128)}, u32[]{:S(2)}) copy-start(f32[256,128]{1,0:T(8,128)} %get-tuple-element.102) | copy-start | bytes 393220
  277.3 10.6 %copy-start.2 = (f32[704,128]{1,0:T(8,128)S(1)}, f32[704,128]{1,0:T(8,128)}, u32[]{:S(2)}) copy-start(f32[704,128]{1,0:T(8,128)} %get-tuple-element.105) | copy-start | bytes 1081348

commit v2 on v1

--- a/solution.py
+++ b/solution.py
@@ -23,6 +23,10 @@
 
 def rows128(i):
     return pl.ds(pl.multiple_of(i * 128, 128), 128)
+
+
+def cols256(i):
+    return pl.ds(pl.multiple_of(i * 256, 256), 256)
 
 
 def inverse_norm(v, floor_value):
@@ -103,6 +107,14 @@
         cp.start()
         return cp
 
+    def gone(self, cp):
+        cp.wait_send()
+        self.sent = [other for other in self.sent if other is not cp]
+
+    def written(self, cp):
+        cp.wait()
+        self.kept = [other for other in self.kept if other is not cp]
+
     def drain(self):
         for cp in self.sent:
             cp.wait_send()
@@ -132,9 +144,12 @@
         self.put(slot, "sa", r, self.second, src)
         self.put(slot, "c0", r, "C", src)
 
+    def cross(self):
+        self.put(0, "z", self.pc.r, "Q", self.own)
+
     def start(self):
-        self.put(0, "z", self.pc.r, "Q", self.own)
         self.launch(0, self.own)
+        self.cross()
 
     def other(self):
         self.cps[0]["z"].wait_recv()
@@ -198,134 +213,216 @@
         inf[s] = same(col, jnp.broadcast_to(prior_id(pc, ids, s), (CH, DH)))
 
 
-def attn_forward(
-    rate_in, tok, cot, seg, wq, wk, wv, wg, wo_in, gl, gr, gd,
-    n1_o, ct_o, n2_o, x1_o, proj_o, qkv_o, p_o, att_o, mix_o, sb_o, w_o, wo_o,
-    gl_o, gr_o, gd_o, ids_o, rate_o,
-    n1, ct, n2, x1, proj, qkv, pm, att, mix, sb, wb, wo, glb, grb, gdb,
+class Scatter:
+    def __init__(self, links, kind, bufs):
+        self.links, self.kind = links, kind
+        pc = links.place
+        self.pc = pc
+        self.acc, self.sc, self.rc, self.sf, self.rf, self.ss, self.rs, self.sz, self.rz = bufs
+        self.c_cp, self.f_cp, self.s_cp = {}, {}, {}
+        self.last = 2 * pc.x + pc.y
+
+    def way(self, b):
+        x, y = self.pc.x, self.pc.y
+        if b == 0:
+            return "X", "Y", x, y, lambda f, m: 2 * f + m
+        return "Y", "X", y, x, lambda f, m: 2 * m + f
+
+    def core_stage(self, b, product, after=None):
+        if after is not None:
+            self.links.gone(after.c_cp[b])
+
+        def pair(i, _):
+            p = product(b, i)
+            lo, hi = (p[:128], p[128:]) if self.kind == "rows" else (p[:, :128], p[:, 128:])
+            self.sc[b, i] = jnp.where(self.pc.c == 0, hi, lo).astype(BF)
+            self.acc[b, i] = jnp.where(self.pc.c == 0, lo, hi).astype(self.acc.dtype)
+            return 0
+
+        lax.fori_loop(0, 4, pair, 0)
+        self.c_cp[b] = self.links.go(self.sc.at[b], self.rc.at[b], "C")
+
+    def add(self, b, i, got):
+        return self.acc[b, i].astype(F32) + got.astype(F32)
+
+    def first_stage(self, b, joined=False):
+        first, _, fv, _, at = self.way(b)
+        if not joined:
+            self.c_cp[b].wait_recv()
+        for m in range(2):
+            i = at(1 - fv, m)
+            self.sf[b, m] = (self.acc[b, i] if joined else self.add(b, i, self.rc[b, i])).astype(BF)
+        self.f_cp[b] = self.links.go(self.sf.at[b], self.rf.at[b], first)
+        if not joined:
+            for m in range(2):
+                i = at(fv, m)
+                self.acc[b, i] = self.add(b, i, self.rc[b, i]).astype(self.acc.dtype)
+
+    def join(self, b):
+        self.c_cp[b].wait_recv()
+        for i in range(4):
+            self.acc[b, i] = self.add(b, i, self.rc[b, i]).astype(self.acc.dtype)
+
+    def second_stage(self, b):
+        _, second, fv, sv, at = self.way(b)
+        self.f_cp[b].wait_recv()
+        self.ss[b] = self.add(b, at(fv, 1 - sv), self.rf[b, 1 - sv]).astype(BF)
+        self.s_cp[b] = self.links.go(self.ss.at[b], self.rs.at[b], second)
+        self.acc[b, self.last] = self.add(b, self.last, self.rf[b, sv]).astype(self.acc.dtype)
+
+    def plane_stage(self):
+        away = 1 - self.pc.zh
+        for b in range(2):
+            self.s_cp[b].wait_recv()
+        self.sz[...] = self.add(away, self.last, self.rs[away]).astype(BF)
+        self.z_cp = self.links.go(self.sz, self.rz, "Q")
+
+    def total(self):
+        zh = self.pc.zh
+        self.z_cp.wait_recv()
+        return self.add(zh, self.last, self.rs[zh]) + self.rz[...].astype(F32)
+
+
+def scatter_bufs(slab, acc=F32, core=2):
+    vm = pltpu.VMEM
+    return [vm((2, 4) + slab, acc)] + [vm((2, 4) + slab, BF)] * core + [
+        vm((2, 2) + slab, BF), vm((2, 2) + slab, BF), vm((2,) + slab, BF), vm((2,) + slab, BF),
+        vm(slab, BF), vm(slab, BF),
+    ]
+
+
+def forward_and_glu(
+    rate_in, tok, cot, seg, wq, wk, wv, wg, wo_in, gl_in, gr_in, gd_in,
+    n1_o, n2_o, pkq_o, pg_o, qkv_o, p_o, att_o, mix_o, sb_o, w_o, wo_o, ids_o, rate_o,
+    dr_o, dx1_o, fs_o, fo_o, dpr_o, gdown_o, left_o,
+    xb, n1, ct, n2, x1, pg, qkv, pm, att, mix, sb, wb, wo, gl, gr, gd,
     ids, rate, grid, wend, gin, mask, endf, inf, uf, us, ur, ts, tr, vs, vr, pf,
-    br_s, br_r, send, recv, local,
+    br_s, br_r, dn_r, dn, hid, dpl, dpr, tmp, dr, fs, fo, gdown, left_acc,
+    *rest,
 ):
+    down_b, left_b = rest[:9], (left_acc, rest[1], rest[9]) + (None,) * 6
+    send, recv, local = rest[10:]
     pc = Place()
     pc.greet()
     ln = Links(pc, send, recv, local)
     own, r = pc.zh, pc.r
-
+    far_b = 1 - own
+
+    def mine(s):
+        return pl.ds(pl.multiple_of(s * CH + pc.t * 128, 128), 128)
+
+    def theirs(s):
+        return pl.ds(pl.multiple_of(s * CH + (1 - pc.t) * 128, 128), 128)
+
+    def wview(i):
+        return lambda b, rr: wb.at[i, b, rows128(rr), :]
+
+    def gview(w):
+        return lambda b, rr: w.at[b, :, rows128(rr)]
+
+    for hh in range(2):
+        rate[own * 2 + hh] = jnp.full((8, DH), rate_in[hh], F32)
+    for s in range(2):
+        xb[mine(s), :] = tok[s]
+        ct[mine(s), :] = cot[s]
     for i, w in enumerate((wk, wv, wq, wg)):
         wb[i, own, rows128(r), :] = w[...].astype(BF)
+    wo[pl.ds(pl.multiple_of(own * 256, 256), 256), rows128(r)] = wo_in[...].astype(BF)
     ids[pc.k] = jnp.zeros((8, 512), F32)
     ids[pc.k, 0:2, :] = seg[...].astype(F32)
-    for hh in range(2):
-        rate[own * 2 + hh] = jnp.full((8, DH), rate_in[hh], F32)
-    for s in range(2):
-        xf = tok[s].astype(F32)
-        n1[pl.ds(pl.multiple_of(s * CH + pc.t * 128, 128), 128), :] = (
-            xf * inverse_norm(xf, EPSILON)
-        ).astype(BF)
-        ct[pl.ds(pl.multiple_of(s * CH + pc.t * 128, 128), 128), :] = cot[s]
     pc.meet()
 
-    def mine(s):
-        return pl.ds(pl.multiple_of(s * CH + pc.t * 128, 128), 128)
-
-    def theirs(s):
-        return pl.ds(pl.multiple_of(s * CH + (1 - pc.t) * 128, 128), 128)
-
-    def wview(i):
-        return lambda b, rr: wb.at[i, b, rows128(rr), :]
-
-    qkvg = [Gather(ln, "AB"[i % 2], wview(i)) for i in range(4)]
-    for g in qkvg:
-        g.start()
+    g_o = Gather(ln, "A", lambda b, rr: wo.at[pl.ds(pl.multiple_of(b * 256, 256), 256), rows128(rr)])
+    qkvgo = [Gather(ln, "AB"[i % 2], wview(i)) for i in range(4)] + [g_o]
+    g_l, g_r, g_d = Gather(ln, "A", gview(gl)), Gather(ln, "B", gview(gr)), Gather(ln, "A", gview(gd))
     rate_cp = ln.go(rate.at[pl.ds(own * 2, 2)], rate.at[pl.ds(own * 2, 2)], "Q")
     ids_y = ln.go(ids.at[pc.k], ids.at[pc.k], "Y")
     ids_c = ln.go(ids.at[pc.k], ids.at[pc.k], "C")
-    n1_cp = [ln.go(n1.at[mine(s)], n1.at[mine(s)], "P") for s in range(2)]
-
-    wo[pl.ds(pl.multiple_of(own * 256, 256), 256), rows128(r)] = wo_in[...].astype(BF)
-    glb[...] = gl[...].astype(BF)
-    grb[...] = gr[...].astype(BF)
-    gdb[...] = gd[...].astype(BF)
-
+    for g in qkvgo[:2]:
+        g.cross()
+        g.launch(0)
+    x_cp = [ln.go(xb.at[mine(s)], xb.at[mine(s)], "P") for s in range(2)]
+    for g in qkvgo[2:]:
+        g.launch(0)
+    for g in qkvgo[2:]:
+        g.cross()
+    ct_cp = [ln.go(ct.at[mine(0)], ct.at[mine(0)], "P")]
+    for s in range(2):
+        xf = tok[s].astype(F32)
+        n1[mine(s), :] = (xf * inverse_norm(xf, EPSILON)).astype(BF)
+    for w, w_in in ((gl, gl_in), (gr, gr_in), (gd, gd_in)):
+        w[own, :, rows128(r)] = w_in[...].astype(BF)
     kf = (pc.k + 2) % 4
     ids_y.wait_recv()
     ids_f = ln.go(ids.at[kf], ids.at[kf], "C")
+    for g in qkvgo:
+        g.step1(0)
     rate_cp.wait_recv()
     fill_decay(rate, grid, wend, gin)
-
-    for g in qkvg:
-        g.step1(0)
-    for g in qkvg:
+    for g in qkvgo[:2]:
         g.other()
+    for g in qkvgo:
+        g.step2(0)
     ids_c.wait_recv()
     ids_f.wait_recv()
     fill_masks(pc, ids, mask, endf, inf)
-    for g in qkvg:
-        g.step2(0)
-    for g in qkvg:
+    for g in qkvgo[:2]:
         g.step1(1)
-    for g in qkvg:
-        g.step3(0)
-    for g in qkvg:
+    g_l.launch(0)
+    g_r.launch(0)
+    for g in qkvgo[:2]:
         g.step2(1)
-
-    gather_o = Gather(ln, "A", lambda b, rr: wo.at[pl.ds(pl.multiple_of(b * 256, 256), 256), rows128(rr)])
-    gather_l = Gather(ln, "A", lambda b, rr: gl_o.at[b, rows128(rr), :], glb)
-    gather_r = Gather(ln, "B", lambda b, rr: gr_o.at[b, rows128(rr), :], grb)
-    gather_d = Gather(ln, "A", lambda b, rr: gd_o.at[b, :, rows128(rr)], gdb)
-    later = [gather_o, gather_l, gather_r, gather_d]
-    for g in later:
-        g.start()
-    ln.keep(glb, gl_o.at[own, rows128(r), :])
-    ln.keep(grb, gr_o.at[own, rows128(r), :])
-    ln.keep(gdb, gd_o.at[own, :, rows128(r)])
-    ct_cp = [ln.go(ct.at[mine(s)], ct.at[mine(s)], "P") for s in range(2)]
-    for cp in n1_cp:
-        cp.wait_recv()
+    for s in range(2):
+        x_cp[s].wait_recv()
+        xf = xb[theirs(s), :].astype(F32)
+        n1[theirs(s), :] = (xf * inverse_norm(xf, EPSILON)).astype(BF)
 
     def project(i):
+        for slot in range(2):
+            qkvgo[i].step3(slot)
+
         def block(b, _):
             p = dg(n1[...], wb[i, b], 1, 0)
-            for hh in range(2):
-                h = b * 2 + hh
-                part = p[:, hh * DH : (hh + 1) * DH]
-                if i == 1:
-                    qkv[1, h] = part.astype(BF)
-                elif i == 3:
-                    proj[2, h] = part
-                else:
-                    proj[i // 2, h] = part
-                    qkv[i, h] = (part * jax.nn.sigmoid(part)).astype(BF)
+            if i == 0:
+                x1[:, cols256(b)] = p
+            elif i == 2:
+                x1[:, cols256(2 + b)] = p
+            elif i == 3:
+                pg[:, cols256(b)] = p
+            if i < 3:
+                a = (p if i == 1 else p * jax.nn.sigmoid(p)).astype(BF)
+                qkv[i, b * 2] = a[:, :DH]
+                qkv[i, b * 2 + 1] = a[:, DH:]
             return 0
 
         lax.fori_loop(0, 2, block, 0)
 
-    for i in range(4):
-        qkvg[i].step3(1)
-        project(i)
-        if i == 1:
-            for s in range(2):
-                rs_ = pl.ds(s * CH, CH)
-
-                def state(h, _):
-                    kw = (qkv[0, h, rs_, :].astype(F32) * (wend[h] * endf[s])).astype(BF)
-                    u = dg(kw, qkv[1, h, rs_, :], 0, 0)
-                    uf[s, h] = u
-                    us[s, h] = u.astype(BF)
-                    return 0
-
-                lax.fori_loop(0, 4, state, 0)
-            u_cp = [ln.go(us.at[s], ur.at[s], "Q") for s in range(2)]
-    for i in range(4):
-        ln.keep(wb.at[i], w_o.at[i])
-    ln.keep(n1, n1_o)
-    ln.keep(proj, proj_o)
-    ln.keep(qkv, qkv_o)
-    ln.keep(ids, ids_o)
-    ln.keep(rate, rate_o)
-    for g in later:
-        g.step1(0)
-
+    project(0)
+    project(1)
+    u_cp = []
+    for s in range(2):
+        rs_ = pl.ds(s * CH, CH)
+
+        def state(h, _):
+            kw = (qkv[0, h, rs_, :].astype(F32) * (wend[h] * endf[s])).astype(BF)
+            u = dg(kw, qkv[1, h, rs_, :], 0, 0)
+            uf[s, h] = u
+            us[s, h] = u.astype(BF)
+            return 0
+
+        lax.fori_loop(0, 4, state, 0)
+        u_cp.append(ln.go(us.at[s], ur.at[s], "Q"))
+    for g in qkvgo[2:]:
+        g.other()
+    g_l.cross()
+    g_r.cross()
+    g_l.step1(0)
+    g_r.step1(0)
+    for g in qkvgo[2:]:
+        g.step1(1)
+    for g in qkvgo[2:]:
+        g.step2(1)
+    project(2)
     for s in range(2):
         rs_ = pl.ds(s * CH, CH)
 
@@ -337,9 +434,22 @@
             return 0
 
         lax.fori_loop(0, 4, inside, 0)
+    project(3)
+    g_o.step3(0)
+    g_o.step3(1)
+    pkq_cp = ln.keep(x1, pkq_o)
+    for i in range(4):
+        ln.keep(wb.at[i], w_o.at[i])
+    ln.keep(n1, n1_o)
+    ln.keep(pg, pg_o)
+    ln.keep(qkv, qkv_o)
+    ln.keep(ids, ids_o)
+    ln.keep(rate, rate_o)
     ln.keep(pm, p_o)
-    for g in later:
-        g.other()
+    ln.keep(wo, wo_o)
+    g_l.step2(0)
+    g_r.step2(0)
+    g_d.launch(0)
 
     t_cp, v_cp = [], []
     for s in range(2):
@@ -359,8 +469,6 @@
 
         lax.fori_loop(0, 4, pair, 0)
         t_cp.append(ln.go(ts.at[s], tr.at[s], "C"))
-    for g in later:
-        g.step2(0)
     for s in range(2):
         t_cp[s].wait_recv()
         prior = prior_id(pc, ids, s)
@@ -380,8 +488,8 @@
 
         lax.fori_loop(0, 4, quad, 0)
         v_cp.append(ln.go(vs.at[s], vr.at[s], "Y"))
-    for g in later:
-        g.step1(1)
+    ln.written(pkq_cp)
+    b_cp = []
     for s in range(2):
         v_cp[s].wait_recv()
         fp = same(last_id(ids, 1, 1, s), prior_id(pc, ids, s)) * jnp.where(pc.y == 1, 1.0, 0.0)
@@ -396,292 +504,149 @@
             o = att[h, rs_, :] + (gin[h] * inf[s]) * dg(qkv[2, h, rs_, :], low_st, 1, 0)
             att[h, rs_, :] = o
             on = o * inverse_norm(o, HEAD_FLOOR)
-            mix[rs_, rows128(h)] = (on * jax.nn.sigmoid(proj[2, h, rs_, :])).astype(BF)
+            mix[rs_, rows128(h)] = (on * jax.nn.sigmoid(pg[rs_, rows128(h)])).astype(BF)
             return 0
 
         lax.fori_loop(0, 4, enter, 0)
+        part = dg(mix[rs_, :], wo[...], 1, 0)
+        br_s[rs_, :] = part.astype(BF)
+        b_cp.append(ln.go(br_s.at[rs_], br_r.at[rs_], "P"))
+        x1[rs_, :] = xb[rs_, :].astype(F32) + part
         if s == 0:
-            gather_o.step3(0)
-            gather_o.step2(1)
-            gather_o.step3(1)
-            b_cp = []
-        br_s[s] = dg(mix[theirs(s), :], wo[...], 1, 0).astype(BF)
-        b_cp.append(ln.go(br_s.at[s], br_r.at[s], "P"))
-        x1[s] = tok[s].astype(F32) + dg(mix[mine(s), :], wo[...], 1, 0)
+            g_d.cross()
+            g_d.step1(0)
+            g_l.other()
+    ct_cp.append(ln.go(ct.at[mine(1)], ct.at[mine(1)], "P"))
     ln.keep(att, att_o)
     ln.keep(mix, mix_o)
     ln.keep(sb, sb_o)
-    ln.keep(wo, wo_o)
-    n2_cp = []
-    for s in range(2):
+    g_r.other()
+    g_d.step2(0)
+    g_l.step1(1)
+    g_r.step1(1)
+    for g in (g_l, g_r, g_d):
+        g.step3(0)
+    g_l.step2(1)
+    g_r.step2(1)
+    d_cp = []
+
+    def units(s, b):
+        rs_ = pl.ds(s * CH, CH)
+        a = dg(n2[rs_, :], gl[b], 1, 1)
+        c = dg(n2[rs_, :], gr[b], 1, 1)
+        hid[b, rs_, :] = (a * c).astype(BF)
+        dh = dg(ct[rs_, :], gd[b], 1, 1)
+        dpl[b, rs_, :] = (dh * c).astype(BF)
+        dpr[b, rs_, :] = (dh * a).astype(BF)
+
+    for s in range(2):
+        rs_ = pl.ds(s * CH, CH)
         b_cp[s].wait_recv()
-        v = x1[s] + br_r[s].astype(F32)
-        x1[s] = v
-        n2[mine(s), :] = (v * inverse_norm(v, EPSILON)).astype(BF)
-        n2_cp.append(ln.go(n2.at[mine(s)], n2.at[mine(s)], "P"))
-    ln.keep(x1, x1_o)
-    for g in later[1:]:
-        g.step2(1)
-    for g in later[1:]:
-        g.step3(0)
-        g.step3(1)
-    for cp in ct_cp:
-        cp.wait_recv()
-    ln.keep(ct, ct_o)
-    for cp in n2_cp:
-        cp.wait_recv()
+        v = x1[rs_, :] + br_r[rs_, :].astype(F32)
+        x1[rs_, :] = v
+        n2[rs_, :] = (v * inverse_norm(v, EPSILON)).astype(BF)
+        if s == 0:
+            g_d.other()
+        ct_cp[s].wait_recv()
+        units(s, own)
+        if s == 0:
+            g_d.step1(1)
+            g_l.step3(1)
+            g_r.step3(1)
+            g_d.step2(1)
+            g_d.step3(1)
+        units(s, far_b)
+        part = (
+            dg(dpl[0, rs_, :], gl[0], 1, 0) + dg(dpr[0, rs_, :], gr[0], 1, 0)
+            + dg(dpl[1, rs_, :], gl[1], 1, 0) + dg(dpr[1, rs_, :], gr[1], 1, 0)
+        )
+        dn[rs_, :] = part
+        ln.gone(b_cp[s])
+        br_s[rs_, :] = part.astype(BF)
+        d_cp.append(ln.go(br_s.at[rs_], dn_r.at[rs_], "P"))
     ln.keep(n2, n2_o)
+    ln.keep(dpr, dpr_o)
+
+    down = Scatter(ln, "cols", down_b)
+    left = Scatter(ln, "cols", left_b)
+    for b in range(2):
+        down.core_stage(b, lambda b, i: dg(hid[b], ct[:, cols256(i)], 0, 0))
+
+    def turn(s):
+        rs_ = pl.ds(s * CH, CH)
+        d_cp[s].wait_recv()
+        g = ct[rs_, :].astype(F32) + norm_slope(x1[rs_, :], dn[rs_, :] + dn_r[rs_, :].astype(F32), EPSILON)
+        dn[rs_, :] = g
+        dr[rs_, :] = g.astype(BF)
+        ln.keep(dr.at[rs_], dr_o.at[rs_])
+        ln.keep(dn.at[mine(s)], dx1_o.at[s])
+
+    def feed(s):
+        rs_ = pl.ds(s * CH, CH)
+        tmp[...] = dg(hid[0, rs_, :], gd[0], 1, 0) + dg(hid[1, rs_, :], gd[1], 1, 0)
+        fs[s] = tmp[rows128(1 - pc.t), :].astype(BF)
+        fo[s] = x1[mine(s), :] + tmp[rows128(pc.t), :]
+
+    feed(0)
+    for b in range(2):
+        down.first_stage(b)
+    for b in range(2):
+        left.core_stage(b, lambda b, i: dg(dpl[b], n2[:, cols256(i)], 0, 0), down)
+    turn(0)
+    feed(1)
+    ln.keep(fs, fs_o)
+    ln.keep(fo, fo_o)
+    for b in range(2):
+        down.second_stage(b)
+    for b in range(2):
+        left.join(b)
+    ln.keep(left.acc, left_o)
+    down.plane_stage()
+    turn(1)
+    gdown[...] = down.total()
+    ln.keep(gdown, gdown_o)
     ln.drain()
 
 
 def call_forward(rate, tok, cot, seg, ws, wo, gl, gr, gd):
-    sd = jax.ShapeDtypeStruct
-    ff = gl.shape[1]
-    vm = pltpu.VMEM
+    sd, vm = jax.ShapeDtypeStruct, pltpu.VMEM
+    ff = gl.shape[0]
+    act = (512, 1024)
+    st = (2, 4, DH, DH)
     outs = [
-        sd((512, 1024), BF),
-        sd((512, 1024), BF),
-        sd((512, 1024), BF),
-        sd((2, 128, 1024), F32),
-        sd((3, 4, 512, DH), F32),
-        sd((3, 4, 512, DH), BF),
-        sd((2, 4, CH, CH), BF),
-        sd((4, 512, DH), F32),
-        sd((512, 512), BF),
-        sd((2, 4, DH, DH), BF),
-        sd((4, 2, 1024, 256), BF),
-        sd((512, 1024), BF),
-        sd((2, 1024, ff), BF),
-        sd((2, 1024, ff), BF),
-        sd((2, ff, 1024), BF),
-        sd((4, 8, 512), F32),
-        sd((4, 8, DH), F32),
+        sd(act, BF), sd(act, BF), sd(act, F32), sd((512, 512), F32), sd((3, 4, 512, DH), BF),
+        sd((2, 4, CH, CH), BF), sd((4, 512, DH), F32), sd((512, 512), BF), sd(st, BF),
+        sd((4, 2, 1024, 256), BF), sd(act, BF), sd((4, 8, 512), F32), sd((4, 8, DH), F32),
+        sd(act, BF), sd((2, 128, 1024), F32), sd((2, 128, 1024), BF), sd((2, 128, 1024), F32),
+        sd((2, 512, ff), BF), sd((ff, 128), F32), sd((2, 4, ff, 128), BF),
     ]
     scratch = [
-        vm((512, 1024), BF), vm((512, 1024), BF), vm((512, 1024), BF), vm((2, 128, 1024), F32),
-        vm((3, 4, 512, DH), F32), vm((3, 4, 512, DH), BF), vm((2, 4, CH, CH), BF),
-        vm((4, 512, DH), F32), vm((512, 512), BF), vm((2, 4, DH, DH), BF),
-        vm((4, 2, 1024, 256), BF), vm((512, 1024), BF),
-        vm((128, ff), BF), vm((128, ff), BF), vm((ff, 128), BF),
+        vm(act, BF), vm(act, BF), vm(act, BF), vm(act, BF), vm(act, F32), vm((512, 512), F32),
+        vm((3, 4, 512, DH), BF), vm((2, 4, CH, CH), BF), vm((4, 512, DH), F32), vm((512, 512), BF),
+        vm(st, BF), vm((4, 2, 1024, 256), BF), vm(act, BF),
+        vm((2, ff, 1024), BF), vm((2, ff, 1024), BF), vm((2, ff, 1024), BF),
         vm((4, 8, 512), F32), vm((4, 8, DH), F32),
         vm((4, CH, CH), F32), vm((4, CH, DH), F32), vm((4, CH, DH), F32),
         vm((2, CH, CH), F32), vm((2, CH, DH), F32), vm((2, CH, DH), F32),
-        vm((2, 4, DH, DH), F32), vm((2, 4, DH, DH), BF), vm((2, 4, DH, DH), BF),
-        vm((2, 4, DH, DH), BF), vm((2, 4, DH, DH), BF), vm((2, 4, DH, DH), BF), vm((2, 4, DH, DH), BF),
-        vm((2, 4, DH, DH), F32),
-        vm((2, 128, 1024), BF), vm((2, 128, 1024), BF),
-        pltpu.SemaphoreType.DMA((144,)), pltpu.SemaphoreType.DMA((144,)), pltpu.SemaphoreType.DMA((24,)),
+        vm(st, F32), vm(st, BF), vm(st, BF), vm(st, BF), vm(st, BF), vm(st, BF), vm(st, BF), vm(st, F32),
+        vm(act, BF), vm(act, BF), vm(act, BF), vm(act, F32),
+        vm((2, 512, ff), BF), vm((2, 512, ff), BF), vm((2, 512, ff), BF),
+        vm((CH, 1024), F32), vm(act, BF), vm((2, 128, 1024), BF), vm((2, 128, 1024), F32), vm((ff, 128), F32), vm((2, 4, ff, 128), BF),
+        *scatter_bufs((ff, 128), BF), vm((2, 4, ff, 128), BF),
+        pltpu.SemaphoreType.DMA((160,)), pltpu.SemaphoreType.DMA((160,)), pltpu.SemaphoreType.DMA((40,)),
     ]
     vin = pl.BlockSpec(memory_space=pltpu.VMEM)
     return pl.pallas_call(
-        attn_forward,
+        forward_and_glu,
         out_shape=outs,
         in_specs=[pl.BlockSpec(memory_space=pltpu.SMEM)] + [vin] * 11,
         out_specs=[pl.BlockSpec(memory_space=pl.ANY)] * len(outs),
         scratch_shapes=scratch,
         compiler_params=pltpu.CompilerParams(
-            collective_id=0, has_side_effects=True, vmem_limit_bytes=60 * MIB
+            collective_id=0, has_side_effects=True, vmem_limit_bytes=63 * MIB
         ),
-        name="attention_forward",
+        name="forward_and_glu",
     )(rate, tok, cot, seg, *ws, wo, gl, gr, gd)
-
-
-class Scatter:
-    def __init__(self, links, order, kind, bufs):
-        self.links, self.kind = links, kind
-        pc = links.place
-        self.pc = pc
-        self.acc, self.sc, self.rc, self.sf, self.rf, self.ss, self.rs, self.sz, self.rz, self.tile = bufs
-        if order == "A":
-            self.first, self.second, self.fv, self.sv = "X", "Y", pc.x, pc.y
-            self.at = lambda f, m: 2 * f + m
-        else:
-            self.first, self.second, self.fv, self.sv = "Y", "X", pc.y, pc.x
-            self.at = lambda f, m: 2 * m + f
-        self.c_cp, self.f_cp, self.s_cp = {}, {}, {}
-
-    def part(self, half):
-        return self.tile[rows128(half), :] if self.kind == "rows" else self.tile[:, rows128(half)]
-
-    def core_stage(self, b, product):
-        def pair(i, _):
-            self.tile[...] = product(b, i)
-            self.sc[b, i] = self.part(1 - self.pc.c).astype(BF)
-            self.acc[b, i] = self.part(self.pc.c)
-            return 0
-
-        lax.fori_loop(0, 4, pair, 0)
-        self.c_cp[b] = self.links.go(self.sc.at[b], self.rc.at[b], "C")
-
-    def first_stage(self, b):
-        self.c_cp[b].wait_recv()
-        for m in range(2):
-            away, here = self.at(1 - self.fv, m), self.at(self.fv, m)
-            self.sf[b, m] = (self.acc[b, away] + self.rc[b, away].astype(F32)).astype(BF)
-        self.f_cp[b] = self.links.go(self.sf.at[b], self.rf.at[b], self.first)
-        for m in range(2):
-            here = self.at(self.fv, m)
-            self.acc[b, here] = self.acc[b, here] + self.rc[b, here].astype(F32)
-
-    def second_stage(self, b):
-        self.f_cp[b].wait_recv()
-        away, here = self.at(self.fv, 1 - self.sv), self.at(self.fv, self.sv)
-        self.ss[b] = (self.acc[b, away] + self.rf[b, 1 - self.sv].astype(F32)).astype(BF)
-        self.s_cp[b] = self.links.go(self.ss.at[b], self.rs.at[b], self.second)
-        self.acc[b, here] = self.acc[b, here] + self.rf[b, self.sv].astype(F32)
-
-    def plane_stage(self):
-        here = self.at(self.fv, self.sv)
-        away = 1 - self.pc.zh
-        for b in range(2):
-            self.s_cp[b].wait_recv()
-        self.sz[...] = (self.acc[away, here] + self.rs[away].astype(F32)).astype(BF)
-        self.z_cp = self.links.go(self.sz, self.rz, "Q")
-
-    def total(self):
-        here = self.at(self.fv, self.sv)
-        zh = self.pc.zh
-        self.z_cp.wait_recv()
-        return self.acc[zh, here] + self.rs[zh].astype(F32) + self.rz[...].astype(F32)
-
-
-def scatter_bufs(slab, tile):
-    vm = pltpu.VMEM
-    return [
-        vm((2, 4) + slab, F32), vm((2, 4) + slab, BF), vm((2, 4) + slab, BF),
-        vm((2, 2) + slab, BF), vm((2, 2) + slab, BF), vm((2,) + slab, BF), vm((2,) + slab, BF),
-        vm(slab, BF), vm(slab, BF), vm(tile, F32),
-    ]
-
-
-def cols256(i):
-    return pl.ds(pl.multiple_of(i * 256, 256), 256)
-
-
-def glu(
-    n2_i, ct_i, x1_i, gl_i, gr_i, gd_i,
-    dr_o, dx1_o, fs_o, fo_o, dpr_o, gdown_o, gleft_o,
-    n2, ct, x1, gl, gr, gd, hid, dpl, dpr, tmp, dsend, drecv, dx1, dr, fs, fo, gdown, gleft,
-    *rest,
-):
-    down_b, left_b = rest[:10], rest[10:20]
-    send, recv, local = rest[20:]
-    pc = Place()
-    pc.greet()
-    ln = Links(pc, send, recv, local)
-    got = {}
-    got["n2"] = ln.fetch(n2_i, n2)
-    got["gl"] = ln.fetch(gl_i, gl)
-    got["gr"] = ln.fetch(gr_i, gr)
-    got["ct"] = ln.fetch(ct_i, ct)
-    got["gd"] = ln.fetch(gd_i, gd)
-    got["x1"] = ln.fetch(x1_i, x1)
-    pc.meet()
-
-    def mine(s):
-        return pl.ds(pl.multiple_of(s * CH + pc.t * 128, 128), 128)
-
-    for name in ("n2", "gl", "gr", "ct", "gd"):
-        got[name].wait()
-    d_cp = []
-    for s in range(2):
-        rs_ = pl.ds(s * CH, CH)
-
-        def block(b, _):
-            a = dg(n2[rs_, :], gl[b], 1, 0)
-            c = dg(n2[rs_, :], gr[b], 1, 0)
-            hid[b, rs_, :] = (a * c).astype(BF)
-            dh = dg(ct[rs_, :], gd[b], 1, 1)
-            dpl[b, rs_, :] = (dh * c).astype(BF)
-            dpr[b, rs_, :] = (dh * a).astype(BF)
-            return 0
-
-        lax.fori_loop(0, 2, block, 0)
-        tmp[...] = (
-            dg(dpl[0, rs_, :], gl[0], 1, 1) + dg(dpr[0, rs_, :], gr[0], 1, 1)
-            + dg(dpl[1, rs_, :], gl[1], 1, 1) + dg(dpr[1, rs_, :], gr[1], 1, 1)
-        )
-        dsend[s] = tmp[rows128(1 - pc.t), :].astype(BF)
-        d_cp.append(ln.go(dsend.at[s], drecv.at[s], "P"))
-        dx1[s] = tmp[rows128(pc.t), :]
-
-    down = Scatter(ln, "A", "cols", down_b)
-    left = Scatter(ln, "B", "rows", left_b)
-    for b in range(2):
-        down.core_stage(b, lambda b, i: dg(hid[b], ct[:, cols256(i)], 0, 0))
-    got["x1"].wait()
-    r_cp = []
-
-    def turn(s):
-        d_cp[s].wait_recv()
-        v = x1[s]
-        dn = dx1[s] + drecv[s].astype(F32)
-        g = ct[mine(s), :].astype(F32) + norm_slope(v, dn, EPSILON)
-        dx1[s] = g
-        dr[mine(s), :] = g.astype(BF)
-        r_cp.append(ln.go(dr.at[mine(s)], dr.at[mine(s)], "P"))
-
-    turn(0)
-    for b in range(2):
-        down.first_stage(b)
-    for b in range(2):
-        left.core_stage(b, lambda b, i: dg(n2[:, cols256(i)], dpl[b], 0, 0))
-    turn(1)
-    ln.keep(dx1, dx1_o)
-    ln.keep(dpr, dpr_o)
-    for s in range(2):
-        rs_ = pl.ds(s * CH, CH)
-        tmp[...] = dg(hid[0, rs_, :], gd[0], 1, 0) + dg(hid[1, rs_, :], gd[1], 1, 0)
-        fs[s] = tmp[rows128(1 - pc.t), :].astype(BF)
-        fo[s] = x1[s] + tmp[rows128(pc.t), :]
-    ln.keep(fs, fs_o)
-    ln.keep(fo, fo_o)
-    for b in range(2):
-        down.second_stage(b)
-    for b in range(2):
-        left.first_stage(b)
-    down.plane_stage()
-    for b in range(2):
-        left.second_stage(b)
-    left.plane_stage()
-    for cp in r_cp:
-        cp.wait_recv()
-    ln.keep(dr, dr_o)
-    gdown[...] = down.total()
-    ln.keep(gdown, gdown_o)
-    gleft[...] = left.total()
-    ln.keep(gleft, gleft_o)
-    ln.drain()
-
-
-def call_glu(n2, ct, x1, gl, gr, gd):
-    sd, vm = jax.ShapeDtypeStruct, pltpu.VMEM
-    ff = gl.shape[2]
-    outs = [
-        sd((512, 1024), BF), sd((2, 128, 1024), F32), sd((2, 128, 1024), BF),
-        sd((2, 128, 1024), F32), sd((2, 512, ff), BF), sd((ff, 128), F32), sd((128, ff), F32),
-    ]
-    scratch = [
-        vm((512, 1024), BF), vm((512, 1024), BF), vm((2, 128, 1024), F32),
-        vm((2, 1024, ff), BF), vm((2, 1024, ff), BF), vm((2, ff, 1024), BF),
-        vm((2, 512, ff), BF), vm((2, 512, ff), BF), vm((2, 512, ff), BF),
-        vm((CH, 1024), F32), vm((2, 128, 1024), BF), vm((2, 128, 1024), BF),
-        vm((2, 128, 1024), F32), vm((512, 1024), BF), vm((2, 128, 1024), BF),
-        vm((2, 128, 1024), F32), vm((ff, 128), F32), vm((128, ff), F32),
-        *scatter_bufs((ff, 128), (ff, 256)), *scatter_bufs((128, ff), (256, ff)),
-        pltpu.SemaphoreType.DMA((24,)), pltpu.SemaphoreType.DMA((24,)), pltpu.SemaphoreType.DMA((24,)),
-    ]
-    return pl.pallas_call(
-        glu,
-        out_shape=outs,
-        in_specs=[pl.BlockSpec(memory_space=pl.ANY)] * 6,
-        out_specs=[pl.BlockSpec(memory_space=pl.ANY)] * len(outs),
-        scratch_shapes=scratch,
-        compiler_params=pltpu.CompilerParams(
-            collective_id=1, has_side_effects=True, vmem_limit_bytes=62 * MIB
-        ),
-        name="glu",
-    )(n2, ct, x1, gl, gr, gd)
 
 
 def silu_slope(v):
@@ -689,32 +654,44 @@
     return g * (1.0 + v * (1.0 - g))
 
 
-N_BACK_IN = 18
+N_BACK_IN = 20
+
+
+def cut_bufs(refs):
+    sets = []
+    for n in (6, 9, 9, 9, 9, 9, 9):
+        sets.append(tuple(refs[:n]))
+        refs = refs[n:]
+    return sets, refs
 
 
 def attn_backward(*refs):
     ins, refs = refs[:N_BACK_IN], refs[N_BACK_IN:]
-    outs, refs = refs[:8], refs[8:]
+    outs, refs = refs[:9], refs[9:]
     bufs, refs = refs[:N_BACK_IN], refs[N_BACK_IN:]
-    out_o, gtok_o, gq_o, gk_o, gv_o, gg_o, go_o, gr_o = outs
-    (dr, dx1, n1, n2, dpr, mix, wo, wb, proj, qkv, pm, att, sb, ids, rate, fs, fo, x) = bufs
+    out_o, gtok_o, gq_o, gk_o, gv_o, gg_o, go_o, gl_o, gr_o = outs
+    (ids, rate, dr, wo, att, pg, qkv, left_acc, n2, dpr, pm, sb, pkq, n1, mix, wb, fs, fo, dx1, x) = bufs
     (
-        grid, wend, gin, mask, endf, inf, dm, dob, dp, dki, dvi, vf, vs, vr, ts, tr, ws, wr, rf, du,
-        tmp, nsend, nrecv, frecv, outb, gtok, gw, gout, gright,
-    ) = refs[:29]
-    refs = refs[29:]
-    sc_bufs = [refs[10 * i : 10 * i + 10] for i in range(6)]
-    send, recv, local = refs[60:]
+        grid, wend, gin, mask, endf, inf, dm, dob, dp, vf, vs, vr, ts, tr, ws, wr, rf, du,
+        tmp, nsend, nrecv, frecv, gtok, gw, gout, gleft, gright,
+    ) = refs[:27]
+    refs = refs[27:]
+    sc_bufs, refs = cut_bufs(refs)
+    send, recv, local = refs
     pc = Place()
     pc.greet()
     ln = Links(pc, send, recv, local)
     got = [ln.fetch(a, b) for a, b in zip(ins, bufs)]
+
+    def ready(n):
+        while len(got) > N_BACK_IN - n:
+            got.pop(0).wait()
+
     pc.meet()
-    for cp in got:
-        cp.wait()
-    f_cp = ln.go(fs, frecv, "P")
+    ready(2)
     fill_decay(rate, grid, wend, gin)
     fill_masks(pc, ids, mask, endf, inf)
+    ready(4)
 
     def mine(s):
         return pl.ds(pl.multiple_of(s * CH + pc.t * 128, 128), 128)
@@ -724,13 +701,14 @@
         return 0
 
     lax.fori_loop(0, 2, through, 0)
+    ready(7)
     v_cp = []
     for s in range(2):
         rs_ = pl.ds(s * CH, CH)
 
         def outer(h, _):
             d, o = dm[rs_, rows128(h)], att[h, rs_, :]
-            g = jax.nn.sigmoid(proj[2, h, rs_, :])
+            g = jax.nn.sigmoid(pg[rs_, rows128(h)])
             inv = inverse_norm(o, HEAD_FLOOR)
             dp[3, rs_, rows128(h)] = (d * (o * inv) * g * (1.0 - g)).astype(BF)
             e = d * g
@@ -746,17 +724,21 @@
         lax.fori_loop(0, 4, outer, 0)
         v_cp.append(ln.go(vs.at[s], vr.at[s], "Q"))
 
-    right = Scatter(ln, "A", "rows", sc_bufs[0])
-    s_out = Scatter(ln, "B", "cols", sc_bufs[1])
-    s_w = [Scatter(ln, "AB"[i % 2], "rows", sc_bufs[2 + i]) for i in range(4)]
+    left = Scatter(ln, "cols", (left_acc, None, None) + sc_bufs[0])
+    right = Scatter(ln, "cols", sc_bufs[1])
+    s_out = Scatter(ln, "cols", sc_bufs[2])
+    s_w = [Scatter(ln, "rows", sc_bufs[3 + i]) for i in range(4)]
 
     def product(i):
         return lambda b, j: dg(n1[:, cols256(j)], dp[i, :, cols256(b)], 0, 0)
 
+    ready(8)
     for b in range(2):
-        right.core_stage(b, lambda b, i: dg(n2[:, cols256(i)], dpr[b], 0, 0))
+        left.first_stage(b, True)
+    ready(10)
     for b in range(2):
-        right.first_stage(b)
+        right.core_stage(b, lambda b, i: dg(dpr[b], n2[:, cols256(i)], 0, 0))
+    ready(13)
 
     for s in range(2):
         rs_ = pl.ds(s * CH, CH)
@@ -765,22 +747,22 @@
             do, q, k = dob[h, rs_, :], qkv[2, h, rs_, :], qkv[0, h, rs_, :]
             dsc = (dg(do, qkv[1, h, rs_, :], 1, 1) * grid[h] * mask[s]).astype(BF)
             dq = dg(dsc, k, 1, 0) + (gin[h] * inf[s]) * dg(do, sb[s, h], 1, 1)
-            dp[2, rs_, rows128(h)] = (dq * silu_slope(proj[1, h, rs_, :])).astype(BF)
-            dki[h, rs_, :] = dg(dsc, q, 0, 0)
-            dvi[h, rs_, :] = dg(pm[s, h], do, 0, 0)
+            dp[2, rs_, rows128(h)] = (dq * silu_slope(pkq[rs_, rows128(4 + h)])).astype(BF)
+            dm[rs_, rows128(h)] = dg(dsc, q, 0, 0)
+            att[h, rs_, :] = dg(pm[s, h], do, 0, 0)
             return 0
 
         lax.fori_loop(0, 4, inside, 0)
 
+    for b in range(2):
+        right.first_stage(b)
+    ready(20)
+    f_cp = ln.go(fs, frecv, "P")
     for b in range(2):
         s_out.core_stage(b, lambda b, i: dg(mix[:, cols256(b)], dr[:, cols256(i)], 0, 0))
     for i in (3, 2):
         for b in range(2):
             s_w[i].core_stage(b, product(i))
-    for b in range(2):
-        right.second_stage(b)
-        s_out.first_stage(b)
-
     t_cp, w_cp = [], []
     for s in range(2):
         v_cp[s].wait_recv()
@@ -800,9 +782,8 @@
 
         lax.fori_loop(0, 4, pair, 0)
         t_cp.append(ln.go(ts.at[s], tr.at[s], "C"))
-    for i in (3, 2):
-        for b in range(2):
-            s_w[i].first_stage(b)
+    for b in range(2):
+        left.second_stage(b)
     for s in range(2):
         t_cp[s].wait_recv()
         low = last_id(ids, pc.y * 2, 1, s)
@@ -825,7 +806,11 @@
         lax.fori_loop(0, 4, quad, 0)
         w_cp.append(ln.go(ws.at[s], wr.at[s], "Y"))
     for b in range(2):
-        s_out.second_stage(b)
+        right.second_stage(b)
+        s_out.first_stage(b)
+    for i in (3, 2):
+        for b in range(2):
+            s_w[i].first_stage(b)
     n_cp = []
     for s in range(2):
         w_cp[s].wait_recv()
@@ -839,9 +824,9 @@
             k, v = qkv[0, h, rs_, :], qkv[1, h, rs_, :]
             w = wend[h] * endf[s]
             kw = (k.astype(F32) * w).astype(BF)
-            dp[1, rs_, rows128(h)] = (dvi[h, rs_, :] + dg(kw, d, 1, 0)).astype(BF)
-            dk = dki[h, rs_, :] + w * dg(v, d, 1, 1)
-            dp[0, rs_, rows128(h)] = (dk * silu_slope(proj[0, h, rs_, :])).astype(BF)
+            dp[1, rs_, rows128(h)] = (att[h, rs_, :] + dg(kw, d, 1, 0)).astype(BF)
+            dk = dm[rs_, rows128(h)] + w * dg(v, d, 1, 1)
+            dp[0, rs_, rows128(h)] = (dk * silu_slope(pkq[rs_, rows128(h)])).astype(BF)
             return 0
 
         lax.fori_loop(0, 4, close, 0)
@@ -857,19 +842,22 @@
     for i in (0, 1):
         for b in range(2):
             s_w[i].core_stage(b, product(i))
+    left.plane_stage()
+    right.plane_stage()
+    for b in range(2):
+        s_out.second_stage(b)
     for i in (3, 2):
         for b in range(2):
             s_w[i].second_stage(b)
-    right.plane_stage()
-    s_out.plane_stage()
     for i in (0, 1):
         for b in range(2):
             s_w[i].first_stage(b)
+    s_out.plane_stage()
     for i in (3, 2):
         s_w[i].plane_stage()
     f_cp.wait_recv()
-    outb[...] = (fo[...] + frecv[...].astype(F32)).astype(BF)
-    ln.keep(outb, out_o)
+    frecv[...] = (fo[...] + frecv[...].astype(F32)).astype(BF)
+    ln.keep(frecv, out_o)
     for s in range(2):
         n_cp[s].wait_recv()
         dn = gtok[s] + nrecv[s].astype(F32)
@@ -878,6 +866,8 @@
     for i in (0, 1):
         for b in range(2):
             s_w[i].second_stage(b)
+    gleft[...] = left.total()
+    ln.keep(gleft, gl_o)
     gright[...] = right.total()
     ln.keep(gright, gr_o)
     for i in (0, 1):
@@ -892,26 +882,25 @@
 
 def call_backward(*args):
     sd, vm = jax.ShapeDtypeStruct, pltpu.VMEM
-    ff = args[4].shape[2]
+    ff = args[9].shape[2]
     outs = [
         sd((2, 128, 1024), BF), sd((2, 128, 1024), F32),
         sd((128, 256), F32), sd((128, 256), F32), sd((128, 256), F32), sd((128, 256), F32),
-        sd((256, 128), F32), sd((128, ff), F32),
+        sd((256, 128), F32), sd((ff, 128), F32), sd((ff, 128), F32),
     ]
     st = (2, 4, DH, DH)
     scratch = [vm(a.shape, a.dtype) for a in args] + [
         vm((4, CH, CH), F32), vm((4, CH, DH), F32), vm((4, CH, DH), F32),
         vm((2, CH, CH), F32), vm((2, CH, DH), F32), vm((2, CH, DH), F32),
         vm((512, 512), F32), vm((4, 512, DH), BF), vm((4, 512, 512), BF),
-        vm((4, 512, DH), F32), vm((4, 512, DH), F32),
         vm(st, F32), vm(st, BF), vm(st, BF), vm(st, BF), vm(st, BF), vm(st, BF), vm(st, BF),
         vm(st, F32), vm((8, 128), BF),
         vm((CH, 1024), F32), vm((2, 128, 1024), BF), vm((2, 128, 1024), BF), vm((2, 128, 1024), BF),
-        vm((2, 128, 1024), BF), vm((2, 128, 1024), F32), vm((4, 128, 256), F32),
-        vm((256, 128), F32), vm((128, ff), F32),
-        *scatter_bufs((128, ff), (256, ff)), *scatter_bufs((256, 128), (256, 256)),
-        *scatter_bufs((128, 256), (256, 256)), *scatter_bufs((128, 256), (256, 256)),
-        *scatter_bufs((128, 256), (256, 256)), *scatter_bufs((128, 256), (256, 256)),
+        vm((2, 128, 1024), F32), vm((4, 128, 256), F32),
+        vm((256, 128), F32), vm((ff, 128), F32), vm((ff, 128), F32),
+        *scatter_bufs((ff, 128), BF, 0)[1:], *scatter_bufs((ff, 128), BF),
+        *scatter_bufs((256, 128)), *scatter_bufs((128, 256)), *scatter_bufs((128, 256)),
+        *scatter_bufs((128, 256)), *scatter_bufs((128, 256)),
         pltpu.SemaphoreType.DMA((64,)), pltpu.SemaphoreType.DMA((64,)), pltpu.SemaphoreType.DMA((40,)),
     ]
     return pl.pallas_call(
@@ -1278,18 +1267,18 @@
 ):
     tok, cot = tokens.transpose(1, 0, 2), cotangent.transpose(1, 0, 2)
     (
-        n1, ct, n2, x1, proj, qkv, pm, att, mix, sb, wb, wo, gl, gr, gd, ids, rate,
+        n1, n2, pkq, pg, qkv, pm, att, mix, sb, wb, wo, ids, rate,
+        dr, dx1, fs, fo, dpr, g_down, left_acc,
     ) = call_forward(
         decay_rate, tok, cot, segment_ids, (w_query, w_key, w_value, w_gate), w_out,
-        glu_left, glu_right, glu_down,
-    )
-    dr, dx1, fs, fo, dpr, g_down, g_left = call_glu(n2, ct, x1, gl, gr, gd)
-    out, g_tok, g_q, g_k, g_v, g_g, g_o, g_right = call_backward(
-        dr, dx1, n1, n2, dpr, mix, wo, wb, proj, qkv, pm, att, sb, ids, rate, fs, fo, tok
+        glu_left.T, glu_right.T, glu_down,
+    )
+    out, g_tok, g_q, g_k, g_v, g_g, g_o, g_left, g_right = call_backward(
+        ids, rate, dr, wo, att, pg, qkv, left_acc, n2, dpr, pm, sb, pkq, n1, mix, wb, fs, fo, dx1, tok
     )
     return (
         out.transpose(1, 0, 2), g_tok.transpose(1, 0, 2),
-        g_q, g_k, g_v, g_g, g_o, g_left, g_right, g_down,
+        g_q, g_k, g_v, g_g, g_o, g_left.T, g_right.T, g_down,
     )
 
 

time: 289 us -> 217 us (0.75)
  Pallas kernels: 270 us -> 204 us
  local copies, waits for them, and re-layouts: 17.6 us -> 12.2 us
    pallas_call x2 -> x1, Pallas kernels: 182 us -> 132 us  [call_forward(): pl.pallas_call(forward_and_glu, out_shape=outs, in_specs=[pl.BlockSpec(me...]
    pallas_call x1, Pallas kernels: 88 us -> 72.2 us  [call_backward(): pl.pallas_call(attn_backward, out_shape=outs, in_specs=[pl.BlockSpec(memo...]
    unnamed x28, local copies, waits for them, and re-layouts: 15.1 us -> 9.77 us
where the time goes in v2:
time: 217 us
  Pallas kernels  204 us (94%)
  local copies, waits for them, and re-layouts  12.2 us (6%)
    pallas_call x1, Pallas kernels, call_forward(): pl.pallas_call(forward_and_glu, out_shape=outs, in_specs=[pl.BlockSpec(me...  132 us
    pallas_call x1, Pallas kernels, call_backward(): pl.pallas_call(attn_backward, out_shape=outs, in_specs=[pl.BlockSpec(memo...  72.2 us
    unnamed x28, local copies, waits for them, and re-layouts  9.77 us

profile of v2, /device:TPU:0, one launch (start us, length us, event | category | flops | bytes accessed | tf_op | source)
XLA Modules:
  0.0 217.0 jit_solution(18072321843144386220)
XLA Ops:
  0.6 2.5 %copy_bitcast_fusion = (bf16[2,128,1024]{2,1,0:T(8,128)(2,1)}, bf16[2,128,1024]{2,1,0:T(8,128)(2,1)}) fusion(bf16[128,2,1024]{2,1,0:T(2,128)(2,1)} %param.23, bf16[128,2,1024]{2,1,0:T(2,128)(2,1)} %param.12), kind=kLoop, calls=%fused_computation | loop fusion | bytes 2097152 | tf_op jit(solution)/shard_map/transpose | solution.py:1268
  3.1 131.9 %forward_and_glu.1 = (bf16[512,1024]{1,0:T(8,128)(2,1)}, bf16[512,1024]{1,0:T(8,128)(2,1)}, f32[512,1024]{1,0:T(8,128)}, f32[512,512]{1,0:T(8,128)}, bf16[3,4,51...) custom-call(f32[2]{0:T(128)} %rate_in.1, ...), custom_call_target="tpu_custom_call" | custom-call | tf_op jit(solution)/shard_map/forward_and_glu/pallas_call | solution.py:639
  135.0 72.2 %attention_backward.1 = (bf16[2,128,1024]{2,1,0:T(8,128)(2,1)}, f32[2,128,1024]{2,1,0:T(8,128)}, f32[128,256]{1,0:T(8,128)}, f32[128,256]{1,0:T(8,128)}, f32[128...) custom-call(f32[4,8,512]{2,1,0:T(8,128)} %get-tuple-element.39.refs_0_, ...), custom_call_target="tpu_custom_call" | custom-call | tf_op jit(solution)/shard_map/attention_backward/pallas_call | solution.py:906
  207.2 0.0 copy-start
  207.2 0.0 copy-start.8
  207.2 0.0 copy-start.7
  207.2 2.5 %copy.24 = bf16[128,2,1024]{2,1,0:T(2,128)(2,1)} copy(bf16[128,2,1024]{2,0,1:T(8,128)(2,1)} %bitcast.11) | data formatting | bytes 1048576
  209.7 0.0 copy-start.6
  209.7 0.0 copy-start.5
  209.7 0.0 copy-done
  209.7 0.0 copy-start.4
  209.7 0.0 copy-start.3
  209.7 0.0 copy-start.2
  209.7 1.8 copy.25
  211.5 0.0 copy-done.8
  211.5 0.0 copy-start.1
  211.5 0.7 copy.36
  212.2 0.0 copy-done.7
  212.2 0.7 copy.37
  212.8 0.0 copy-done.6
  212.8 0.7 copy.38
  213.5 0.0 copy-done.5
  213.5 0.7 copy.39
  214.1 0.0 copy-done.4
  214.1 0.7 copy.40
  214.8 0.0 copy-done.3
  214.8 0.7 copy.41
  215.5 0.0 copy-done.2
  215.5 0.7 copy.42
  216.3 0.0 copy-done.1
  216.3 0.7 copy.43
Async XLA Ops:
  207.2 2.5 %copy-start = (f32[2,128,1024]{2,1,0:T(8,128)S(1)}, f32[2,128,1024]{2,1,0:T(8,128)}, u32[]{:S(2)}) copy-start(f32[2,128,1024]{2,1,0:T(8,128)} %get-tuple-element.59) | copy-start | bytes 3145732
  207.2 4.3 %copy-start.8 = (f32[128,256]{1,0:T(8,128)S(1)}, f32[128,256]{1,0:T(8,128)}, u32[]{:S(2)}) copy-start(f32[128,256]{1,0:T(8,128)} %get-tuple-element.92) | copy-start | bytes 393220
  207.2 5.0 %copy-start.7 = (f32[128,256]{1,0:T(8,128)S(1)}, f32[128,256]{1,0:T(8,128)}, u32[]{:S(2)}) copy-start(f32[128,256]{1,0:T(8,128)} %get-tuple-element.93) | copy-start | bytes 393220
  209.7 3.1 %copy-start.6 = (f32[128,256]{1,0:T(8,128)S(1)}, f32[128,256]{1,0:T(8,128)}, u32[]{:S(2)}) copy-start(f32[128,256]{1,0:T(8,128)} %get-tuple-element.94) | copy-start | bytes 393220
  209.7 3.8 %copy-start.5 = (f32[128,256]{1,0:T(8,128)S(1)}, f32[128,256]{1,0:T(8,128)}, u32[]{:S(2)}) copy-start(f32[128,256]{1,0:T(8,128)} %get-tuple-element.95) | copy-start | bytes 393220
  209.7 4.4 %copy-start.4 = (f32[256,128]{1,0:T(8,128)S(1)}, f32[256,128]{1,0:T(8,128)}, u32[]{:S(2)}) copy-start(f32[256,128]{1,0:T(8,128)} %get-tuple-element.96) | copy-start | bytes 393220
  209.7 5.1 %copy-start.3 = (f32[704,128]{1,0:T(8,128)S(1)}, f32[704,128]{1,0:T(8,128)}, u32[]{:S(2)}) copy-start(f32[704,128]{1,0:T(8,128)} %get-tuple-element.65) | copy-start | bytes 1081348
  209.7 5.8 %copy-start.2 = (f32[704,128]{1,0:T(8,128)S(1)}, f32[704,128]{1,0:T(8,128)}, u32[]{:S(2)}) copy-start(f32[704,128]{1,0:T(8,128)} %get-tuple-element.66) | copy-start | bytes 1081348
  211.5 4.8 %copy-start.1 = (f32[704,128]{1,0:T(8,128)S(1)}, f32[704,128]{1,0:T(8,128)}, u32[]{:S(2)}) copy-start(f32[704,128]{1,0:T(8,128)} %get-tuple-element.99) | copy-start | bytes 1081348

commit v3 on v2

--- a/solution.py
+++ b/solution.py
@@ -213,6 +213,69 @@
         inf[s] = same(col, jnp.broadcast_to(prior_id(pc, ids, s), (CH, DH)))
 
 
+def forward_factors(pc, ids, rate, fac):
+    for s in range(2):
+        prior = prior_id(pc, ids, s)
+        low = last_id(ids, pc.y * 2, 1, s)
+        f1 = same(last_id(ids, pc.k, 0, s), last_id(ids, pc.k, 1, s))
+        f2 = same(low, last_id(ids, pc.y * 2 + 1, 1, s))
+        p2 = same(low, prior) * jnp.where(pc.c == 1, 1.0, 0.0)
+        p3 = same(last_id(ids, 1, 1, s), prior) * jnp.where(pc.y == 1, 1.0, 0.0)
+        d2 = pc.zh.astype(F32) * CH
+        d3 = (2 * pc.c + pc.zh).astype(F32) * CH
+        for h in range(4):
+            one = rate[h, 0:1, :]
+            unit = jnp.ones_like(one)
+            l1, l2 = jnp.exp(-CH * one) * f1, jnp.exp(-2.0 * CH * one) * f2
+            fac[s, h, 0:1, :] = jnp.where(pc.zh == 1, unit, l1)
+            fac[s, h, 1:2, :] = jnp.where(pc.zh == 1, l1, unit)
+            fac[s, h, 2:3, :] = jnp.where(pc.zh == 1, unit, 0.0 * unit)
+            fac[s, h, 3:4, :] = jnp.where(pc.c == 1, unit, l2)
+            fac[s, h, 4:5, :] = jnp.where(pc.c == 1, l2, unit)
+            fac[s, h, 5:6, :] = jnp.exp(-d2 * one) * p2
+            fac[s, h, 6:7, :] = jnp.exp(-d3 * one) * p3
+
+
+def backward_factors(pc, ids, rate, fac):
+    for s in range(2):
+        low = last_id(ids, pc.y * 2, 1, s)
+        prev_k = jnp.where(pc.k > 0, last_id(ids, (pc.k + 3) % 4, 1, s), -1.0)
+        prev_y = jnp.where(pc.y > 0, last_id(ids, (pc.y * 2 + 3) % 4, 1, s), -1.0)
+        here = jnp.where(pc.zh == 1, last_id(ids, pc.k, 1, s), last_id(ids, pc.k, 0, s))
+        f1, f2 = same(prev_k, last_id(ids, pc.k, 0, s)), same(prev_y, low)
+        p2 = same(here, low) * jnp.where(pc.c == 0, 1.0, 0.0)
+        p3 = same(here, last_id(ids, 1, 1, s)) * jnp.where(pc.y == 0, 1.0, 0.0)
+        d2 = (1 - pc.zh).astype(F32) * CH
+        d3 = (2 * (1 - pc.c) + (1 - pc.zh)).astype(F32) * CH
+        for h in range(4):
+            one = rate[h, 0:1, :]
+            unit = jnp.ones_like(one)
+            l1, l2 = jnp.exp(-CH * one) * f1, jnp.exp(-2.0 * CH * one) * f2
+            fac[s, h, 0:1, :] = jnp.where(pc.zh == 0, unit, l1)
+            fac[s, h, 1:2, :] = jnp.where(pc.zh == 0, l1, unit)
+            fac[s, h, 2:3, :] = jnp.where(pc.zh == 0, unit, 0.0 * unit)
+            fac[s, h, 3:4, :] = jnp.where(pc.c == 0, unit, l2)
+            fac[s, h, 4:5, :] = jnp.where(pc.c == 0, l2, unit)
+            fac[s, h, 5:6, :] = jnp.exp(-d2 * one) * p2
+            fac[s, h, 6:7, :] = jnp.exp(-d3 * one) * p3
+
+
+def pair_sum(fac, s, own, got, total, prefix):
+    for h in range(4):
+        g = got[s, h].astype(F32)
+        tot = fac[s, h, 0:1, :] * own[s, h] + fac[s, h, 1:2, :] * g
+        prefix[s, h] = fac[s, h, 2:3, :] * g
+        own[s, h] = tot
+        total[s, h] = tot.astype(BF)
+
+
+def quad_sum(fac, s, own, got, total, prefix):
+    for h in range(4):
+        g = got[s, h].astype(F32)
+        total[s, h] = (fac[s, h, 3:4, :] * own[s, h] + fac[s, h, 4:5, :] * g).astype(BF)
+        prefix[s, h] = prefix[s, h] + fac[s, h, 5:6, :] * g
+
+
 class Scatter:
     def __init__(self, links, kind, bufs):
         self.links, self.kind = links, kind
@@ -271,16 +334,20 @@
         self.acc[b, self.last] = self.add(b, self.last, self.rf[b, sv]).astype(self.acc.dtype)
 
     def plane_stage(self):
-        away = 1 - self.pc.zh
+        zh = self.pc.zh
         for b in range(2):
             self.s_cp[b].wait_recv()
-        self.sz[...] = self.add(away, self.last, self.rs[away]).astype(BF)
-        self.z_cp = self.links.go(self.sz, self.rz, "Q")
+        self.sz[...] = self.add(1 - zh, self.last, self.rs[1 - zh]).astype(BF)
+        if self.rz is not None:
+            self.z_cp = self.links.go(self.sz, self.rz, "Q")
+
+    def near(self):
+        zh = self.pc.zh
+        return self.add(zh, self.last, self.rs[zh])
 
     def total(self):
-        zh = self.pc.zh
         self.z_cp.wait_recv()
-        return self.add(zh, self.last, self.rs[zh]) + self.rz[...].astype(F32)
+        return self.near() + self.rz[...].astype(F32)
 
 
 def scatter_bufs(slab, acc=F32, core=2):
@@ -294,14 +361,14 @@
 def forward_and_glu(
     rate_in, tok, cot, seg, wq, wk, wv, wg, wo_in, gl_in, gr_in, gd_in,
     n1_o, n2_o, pkq_o, pg_o, qkv_o, p_o, att_o, mix_o, sb_o, w_o, wo_o, ids_o, rate_o,
-    dr_o, dx1_o, fs_o, fo_o, dpr_o, gdown_o, left_o,
+    dr_o, dx1_o, fs_o, fo_o, dpr_o, gdown_o, dsz_o, left_o,
     xb, n1, ct, n2, x1, pg, qkv, pm, att, mix, sb, wb, wo, gl, gr, gd,
-    ids, rate, grid, wend, gin, mask, endf, inf, uf, us, ur, ts, tr, vs, vr, pf,
+    ids, rate, fac, grid, wend, gin, mask, endf, inf, uf, us, ur, ts, tr, vs, vr, pf,
     br_s, br_r, dn_r, dn, hid, dpl, dpr, tmp, dr, fs, fo, gdown, left_acc,
     *rest,
 ):
-    down_b, left_b = rest[:9], (left_acc, rest[1], rest[9]) + (None,) * 6
-    send, recv, local = rest[10:]
+    down_b, left_b = rest[:8] + (None,), (left_acc, rest[1], rest[8]) + (None,) * 6
+    send, recv, local = rest[9:]
     pc = Place()
     pc.greet()
     ln = Links(pc, send, recv, local)
@@ -318,7 +385,7 @@
         return lambda b, rr: wb.at[i, b, rows128(rr), :]
 
     def gview(w):
-        return lambda b, rr: w.at[b, :, rows128(rr)]
+        return lambda b, rr: w.at[b, rows128(rr), :]
 
     for hh in range(2):
         rate[own * 2 + hh] = jnp.full((8, DH), rate_in[hh], F32)
@@ -327,12 +394,12 @@
         ct[mine(s), :] = cot[s]
     for i, w in enumerate((wk, wv, wq, wg)):
         wb[i, own, rows128(r), :] = w[...].astype(BF)
-    wo[pl.ds(pl.multiple_of(own * 256, 256), 256), rows128(r)] = wo_in[...].astype(BF)
+    wo[own, rows128(r), :] = wo_in[...].T.astype(BF)
     ids[pc.k] = jnp.zeros((8, 512), F32)
     ids[pc.k, 0:2, :] = seg[...].astype(F32)
     pc.meet()
 
-    g_o = Gather(ln, "A", lambda b, rr: wo.at[pl.ds(pl.multiple_of(b * 256, 256), 256), rows128(rr)])
+    g_o = Gather(ln, "A", gview(wo))
     qkvgo = [Gather(ln, "AB"[i % 2], wview(i)) for i in range(4)] + [g_o]
     g_l, g_r, g_d = Gather(ln, "A", gview(gl)), Gather(ln, "B", gview(gr)), Gather(ln, "A", gview(gd))
     rate_cp = ln.go(rate.at[pl.ds(own * 2, 2)], rate.at[pl.ds(own * 2, 2)], "Q")
@@ -346,12 +413,11 @@
         g.launch(0)
     for g in qkvgo[2:]:
         g.cross()
-    ct_cp = [ln.go(ct.at[mine(0)], ct.at[mine(0)], "P")]
     for s in range(2):
         xf = tok[s].astype(F32)
         n1[mine(s), :] = (xf * inverse_norm(xf, EPSILON)).astype(BF)
     for w, w_in in ((gl, gl_in), (gr, gr_in), (gd, gd_in)):
-        w[own, :, rows128(r)] = w_in[...].astype(BF)
+        w[own, rows128(r), :] = w_in[...].T.astype(BF)
     kf = (pc.k + 2) % 4
     ids_y.wait_recv()
     ids_f = ln.go(ids.at[kf], ids.at[kf], "C")
@@ -366,6 +432,7 @@
     ids_c.wait_recv()
     ids_f.wait_recv()
     fill_masks(pc, ids, mask, endf, inf)
+    forward_factors(pc, ids, rate, fac)
     for g in qkvgo[:2]:
         g.step1(1)
     g_l.launch(0)
@@ -412,6 +479,7 @@
 
         lax.fori_loop(0, 4, state, 0)
         u_cp.append(ln.go(us.at[s], ur.at[s], "Q"))
+    ct_cp = [ln.go(ct.at[mine(0)], ct.at[mine(0)], "P")]
     for g in qkvgo[2:]:
         g.other()
     g_l.cross()
@@ -451,55 +519,22 @@
     g_r.step2(0)
     g_d.launch(0)
 
-    t_cp, v_cp = [], []
+    v_cp = []
     for s in range(2):
         u_cp[s].wait_recv()
-        fl = same(last_id(ids, pc.k, 0, s), last_id(ids, pc.k, 1, s))
-
-        def pair(h, _):
-            lane = jnp.exp(-CH * rate[h, 0:1, :]) * fl
-            got = ur[s, h].astype(F32)
-            wo_ = jnp.where(pc.zh == 1, jnp.ones_like(lane), lane)
-            wr_ = jnp.where(pc.zh == 1, lane, jnp.ones_like(lane))
-            tot = wo_ * uf[s, h] + wr_ * got
-            pf[s, h] = jnp.where(pc.zh == 1, got, jnp.zeros_like(got))
-            uf[s, h] = tot
-            ts[s, h] = tot.astype(BF)
-            return 0
-
-        lax.fori_loop(0, 4, pair, 0)
-        t_cp.append(ln.go(ts.at[s], tr.at[s], "C"))
-    for s in range(2):
-        t_cp[s].wait_recv()
-        prior = prior_id(pc, ids, s)
-        low = last_id(ids, pc.y * 2, 1, s)
-        fl = same(low, last_id(ids, pc.y * 2 + 1, 1, s))
-        fp = same(low, prior) * jnp.where(pc.c == 1, 1.0, 0.0)
-
-        def quad(h, _):
-            one = rate[h, 0:1, :]
-            lane = jnp.exp(-2.0 * CH * one) * fl
-            got = tr[s, h].astype(F32)
-            wo_ = jnp.where(pc.c == 1, jnp.ones_like(lane), lane)
-            wr_ = jnp.where(pc.c == 1, lane, jnp.ones_like(lane))
-            vs[s, h] = (wo_ * uf[s, h] + wr_ * got).astype(BF)
-            pf[s, h] = pf[s, h] + (jnp.exp(-(CH * 1.0) * pc.zh.astype(F32) * one) * fp) * got
-            return 0
-
-        lax.fori_loop(0, 4, quad, 0)
+        pair_sum(fac, s, uf, ur, ts, pf)
+        t_cp = ln.go(ts.at[s], tr.at[s], "C")
+        t_cp.wait_recv()
+        quad_sum(fac, s, uf, tr, vs, pf)
         v_cp.append(ln.go(vs.at[s], vr.at[s], "Y"))
     ln.written(pkq_cp)
     b_cp = []
     for s in range(2):
         v_cp[s].wait_recv()
-        fp = same(last_id(ids, 1, 1, s), prior_id(pc, ids, s)) * jnp.where(pc.y == 1, 1.0, 0.0)
-        far = (2 * pc.c + pc.zh).astype(F32) * CH
         rs_ = pl.ds(s * CH, CH)
 
         def enter(h, _):
-            got = vr[s, h].astype(F32)
-            st = pf[s, h] + (jnp.exp(-far * rate[h, 0:1, :]) * fp) * got
-            low_st = st.astype(BF)
+            low_st = (pf[s, h] + fac[s, h, 6:7, :] * vr[s, h].astype(F32)).astype(BF)
             sb[s, h] = low_st
             o = att[h, rs_, :] + (gin[h] * inf[s]) * dg(qkv[2, h, rs_, :], low_st, 1, 0)
             att[h, rs_, :] = o
@@ -508,7 +543,7 @@
             return 0
 
         lax.fori_loop(0, 4, enter, 0)
-        part = dg(mix[rs_, :], wo[...], 1, 0)
+        part = dg(mix[rs_, :256], wo[0], 1, 1) + dg(mix[rs_, 256:], wo[1], 1, 1)
         br_s[rs_, :] = part.astype(BF)
         b_cp.append(ln.go(br_s.at[rs_], br_r.at[rs_], "P"))
         x1[rs_, :] = xb[rs_, :].astype(F32) + part
@@ -516,10 +551,10 @@
             g_d.cross()
             g_d.step1(0)
             g_l.other()
-    ct_cp.append(ln.go(ct.at[mine(1)], ct.at[mine(1)], "P"))
     ln.keep(att, att_o)
     ln.keep(mix, mix_o)
     ln.keep(sb, sb_o)
+    ct_cp.append(ln.go(ct.at[mine(1)], ct.at[mine(1)], "P"))
     g_r.other()
     g_d.step2(0)
     g_l.step1(1)
@@ -532,10 +567,10 @@
 
     def units(s, b):
         rs_ = pl.ds(s * CH, CH)
-        a = dg(n2[rs_, :], gl[b], 1, 1)
-        c = dg(n2[rs_, :], gr[b], 1, 1)
+        a = dg(n2[rs_, :], gl[b], 1, 0)
+        c = dg(n2[rs_, :], gr[b], 1, 0)
         hid[b, rs_, :] = (a * c).astype(BF)
-        dh = dg(ct[rs_, :], gd[b], 1, 1)
+        dh = dg(ct[rs_, :], gd[b], 1, 0)
         dpl[b, rs_, :] = (dh * c).astype(BF)
         dpr[b, rs_, :] = (dh * a).astype(BF)
 
@@ -557,8 +592,8 @@
             g_d.step3(1)
         units(s, far_b)
         part = (
-            dg(dpl[0, rs_, :], gl[0], 1, 0) + dg(dpr[0, rs_, :], gr[0], 1, 0)
-            + dg(dpl[1, rs_, :], gl[1], 1, 0) + dg(dpr[1, rs_, :], gr[1], 1, 0)
+            dg(dpl[0, rs_, :], gl[0], 1, 1) + dg(dpr[0, rs_, :], gr[0], 1, 1)
+            + dg(dpl[1, rs_, :], gl[1], 1, 1) + dg(dpr[1, rs_, :], gr[1], 1, 1)
         )
         dn[rs_, :] = part
         ln.gone(b_cp[s])
@@ -583,7 +618,7 @@
 
     def feed(s):
         rs_ = pl.ds(s * CH, CH)
-        tmp[...] = dg(hid[0, rs_, :], gd[0], 1, 0) + dg(hid[1, rs_, :], gd[1], 1, 0)
+        tmp[...] = dg(hid[0, rs_, :], gd[0], 1, 1) + dg(hid[1, rs_, :], gd[1], 1, 1)
         fs[s] = tmp[rows128(1 - pc.t), :].astype(BF)
         fo[s] = x1[mine(s), :] + tmp[rows128(pc.t), :]
 
@@ -593,18 +628,19 @@
     for b in range(2):
         left.core_stage(b, lambda b, i: dg(dpl[b], n2[:, cols256(i)], 0, 0), down)
     turn(0)
+    for b in range(2):
+        down.second_stage(b)
     feed(1)
     ln.keep(fs, fs_o)
     ln.keep(fo, fo_o)
     for b in range(2):
-        down.second_stage(b)
-    for b in range(2):
         left.join(b)
     ln.keep(left.acc, left_o)
     down.plane_stage()
+    ln.keep(down.sz, dsz_o)
+    gdown[...] = down.near()
+    ln.keep(gdown, gdown_o)
     turn(1)
-    gdown[...] = down.total()
-    ln.keep(gdown, gdown_o)
     ln.drain()
 
 
@@ -616,23 +652,23 @@
     outs = [
         sd(act, BF), sd(act, BF), sd(act, F32), sd((512, 512), F32), sd((3, 4, 512, DH), BF),
         sd((2, 4, CH, CH), BF), sd((4, 512, DH), F32), sd((512, 512), BF), sd(st, BF),
-        sd((4, 2, 1024, 256), BF), sd(act, BF), sd((4, 8, 512), F32), sd((4, 8, DH), F32),
+        sd((4, 2, 1024, 256), BF), sd((2, 1024, 256), BF), sd((4, 8, 512), F32), sd((4, 8, DH), F32),
         sd(act, BF), sd((2, 128, 1024), F32), sd((2, 128, 1024), BF), sd((2, 128, 1024), F32),
-        sd((2, 512, ff), BF), sd((ff, 128), F32), sd((2, 4, ff, 128), BF),
+        sd((2, 512, ff), BF), sd((ff, 128), F32), sd((ff, 128), BF), sd((2, 4, ff, 128), BF),
     ]
     scratch = [
         vm(act, BF), vm(act, BF), vm(act, BF), vm(act, BF), vm(act, F32), vm((512, 512), F32),
         vm((3, 4, 512, DH), BF), vm((2, 4, CH, CH), BF), vm((4, 512, DH), F32), vm((512, 512), BF),
-        vm(st, BF), vm((4, 2, 1024, 256), BF), vm(act, BF),
-        vm((2, ff, 1024), BF), vm((2, ff, 1024), BF), vm((2, ff, 1024), BF),
-        vm((4, 8, 512), F32), vm((4, 8, DH), F32),
+        vm(st, BF), vm((4, 2, 1024, 256), BF), vm((2, 1024, 256), BF),
+        vm((2, 1024, ff), BF), vm((2, 1024, ff), BF), vm((2, 1024, ff), BF),
+        vm((4, 8, 512), F32), vm((4, 8, DH), F32), vm((2, 4, 8, DH), F32),
         vm((4, CH, CH), F32), vm((4, CH, DH), F32), vm((4, CH, DH), F32),
         vm((2, CH, CH), F32), vm((2, CH, DH), F32), vm((2, CH, DH), F32),
         vm(st, F32), vm(st, BF), vm(st, BF), vm(st, BF), vm(st, BF), vm(st, BF), vm(st, BF), vm(st, F32),
         vm(act, BF), vm(act, BF), vm(act, BF), vm(act, F32),
         vm((2, 512, ff), BF), vm((2, 512, ff), BF), vm((2, 512, ff), BF),
         vm((CH, 1024), F32), vm(act, BF), vm((2, 128, 1024), BF), vm((2, 128, 1024), F32), vm((ff, 128), F32), vm((2, 4, ff, 128), BF),
-        *scatter_bufs((ff, 128), BF), vm((2, 4, ff, 128), BF),
+        *scatter_bufs((ff, 128), BF)[:-1], vm((2, 4, ff, 128), BF),
         pltpu.SemaphoreType.DMA((160,)), pltpu.SemaphoreType.DMA((160,)), pltpu.SemaphoreType.DMA((40,)),
     ]
     vin = pl.BlockSpec(memory_space=pltpu.VMEM)
@@ -654,7 +690,7 @@
     return g * (1.0 + v * (1.0 - g))
 
 
-N_BACK_IN = 20
+N_BACK_IN = 22
 
 
 def cut_bufs(refs):
@@ -667,15 +703,17 @@
 
 def attn_backward(*refs):
     ins, refs = refs[:N_BACK_IN], refs[N_BACK_IN:]
-    outs, refs = refs[:9], refs[9:]
+    outs, refs = refs[:10], refs[10:]
     bufs, refs = refs[:N_BACK_IN], refs[N_BACK_IN:]
-    out_o, gtok_o, gq_o, gk_o, gv_o, gg_o, go_o, gl_o, gr_o = outs
-    (ids, rate, dr, wo, att, pg, qkv, left_acc, n2, dpr, pm, sb, pkq, n1, mix, wb, fs, fo, dx1, x) = bufs
+    out_o, gtok_o, gq_o, gk_o, gv_o, gg_o, go_o, gl_o, gr_o, gd_o = outs
     (
-        grid, wend, gin, mask, endf, inf, dm, dob, dp, vf, vs, vr, ts, tr, ws, wr, rf, du,
-        tmp, nsend, nrecv, frecv, gtok, gw, gout, gleft, gright,
-    ) = refs[:27]
-    refs = refs[27:]
+        ids, rate, fs, left_acc, dr, wo, att, pg, qkv, n2, dpr, pm, sb, pkq, dsz, mix, n1, wb, fo, dx1, x, dnear
+    ) = bufs
+    (
+        fac, grid, wend, gin, mask, endf, inf, dm, dob, dp, vf, vs, vr, ts, tr, ws, wr, rf, du,
+        tmp, nsend, nrecv, frecv, drz, gtok, gw, gout, gleft, gright,
+    ) = refs[:29]
+    refs = refs[29:]
     sc_bufs, refs = cut_bufs(refs)
     send, recv, local = refs
     pc = Place()
@@ -688,20 +726,29 @@
             got.pop(0).wait()
 
     pc.meet()
-    ready(2)
+    left = Scatter(ln, "cols", (left_acc, None, None) + sc_bufs[0])
+    right = Scatter(ln, "cols", sc_bufs[1])
+    s_out = Scatter(ln, "cols", sc_bufs[2])
+    s_w = [Scatter(ln, "rows", sc_bufs[3 + i]) for i in range(4)]
+    ready(3)
+    f_cp = ln.go(fs, frecv, "P")
     fill_decay(rate, grid, wend, gin)
     fill_masks(pc, ids, mask, endf, inf)
+    backward_factors(pc, ids, rate, fac)
     ready(4)
+    for b in range(2):
+        left.first_stage(b, True)
+    ready(6)
 
     def mine(s):
         return pl.ds(pl.multiple_of(s * CH + pc.t * 128, 128), 128)
 
     def through(b, _):
-        dm[:, cols256(b)] = dg(dr[...], wo[cols256(b), :], 1, 1)
+        dm[:, cols256(b)] = dg(dr[...], wo[b], 1, 0)
         return 0
 
     lax.fori_loop(0, 2, through, 0)
-    ready(7)
+    ready(9)
     v_cp = []
     for s in range(2):
         rs_ = pl.ds(s * CH, CH)
@@ -724,23 +771,20 @@
         lax.fori_loop(0, 4, outer, 0)
         v_cp.append(ln.go(vs.at[s], vr.at[s], "Q"))
 
-    left = Scatter(ln, "cols", (left_acc, None, None) + sc_bufs[0])
-    right = Scatter(ln, "cols", sc_bufs[1])
-    s_out = Scatter(ln, "cols", sc_bufs[2])
-    s_w = [Scatter(ln, "rows", sc_bufs[3 + i]) for i in range(4)]
-
     def product(i):
         return lambda b, j: dg(n1[:, cols256(j)], dp[i, :, cols256(b)], 0, 0)
 
-    ready(8)
-    for b in range(2):
-        left.first_stage(b, True)
-    ready(10)
+    ready(11)
     for b in range(2):
         right.core_stage(b, lambda b, i: dg(dpr[b], n2[:, cols256(i)], 0, 0))
-    ready(13)
-
-    for s in range(2):
+    for b in range(2):
+        left.second_stage(b)
+    ready(15)
+    z_cp = ln.go(dsz, drz, "Q")
+    for b in range(2):
+        right.first_stage(b)
+
+    def inner(s):
         rs_ = pl.ds(s * CH, CH)
 
         def inside(h, _):
@@ -754,73 +798,22 @@
 
         lax.fori_loop(0, 4, inside, 0)
 
-    for b in range(2):
-        right.first_stage(b)
-    ready(20)
-    f_cp = ln.go(fs, frecv, "P")
-    for b in range(2):
-        s_out.core_stage(b, lambda b, i: dg(mix[:, cols256(b)], dr[:, cols256(i)], 0, 0))
-    for i in (3, 2):
-        for b in range(2):
-            s_w[i].core_stage(b, product(i))
-    t_cp, w_cp = [], []
-    for s in range(2):
+    def pair_up(s):
         v_cp[s].wait_recv()
-        before = jnp.where(pc.k > 0, last_id(ids, (pc.k + 3) % 4, 1, s), -1.0)
-        fb = same(before, last_id(ids, pc.k, 0, s))
-
-        def pair(h, _):
-            lane = jnp.exp(-CH * rate[h, 0:1, :]) * fb
-            g = vr[s, h].astype(F32)
-            wo_ = jnp.where(pc.zh == 0, jnp.ones_like(lane), lane)
-            wr_ = jnp.where(pc.zh == 0, lane, jnp.ones_like(lane))
-            tot = wo_ * vf[s, h] + wr_ * g
-            rf[s, h] = jnp.where(pc.zh == 0, g, jnp.zeros_like(g))
-            vf[s, h] = tot
-            ts[s, h] = tot.astype(BF)
-            return 0
-
-        lax.fori_loop(0, 4, pair, 0)
-        t_cp.append(ln.go(ts.at[s], tr.at[s], "C"))
-    for b in range(2):
-        left.second_stage(b)
-    for s in range(2):
+        pair_sum(fac, s, vf, vr, ts, rf)
+        return ln.go(ts.at[s], tr.at[s], "C")
+
+    def quad_up(s):
         t_cp[s].wait_recv()
-        low = last_id(ids, pc.y * 2, 1, s)
-        before = jnp.where(pc.y > 0, last_id(ids, (pc.y * 2 + 3) % 4, 1, s), -1.0)
-        fb = same(before, low)
-        here = jnp.where(pc.zh == 1, last_id(ids, pc.k, 1, s), last_id(ids, pc.k, 0, s))
-        fp = same(here, low) * jnp.where(pc.c == 0, 1.0, 0.0)
-        far = (1 - pc.zh).astype(F32) * CH
-
-        def quad(h, _):
-            one = rate[h, 0:1, :]
-            lane = jnp.exp(-2.0 * CH * one) * fb
-            g = tr[s, h].astype(F32)
-            wo_ = jnp.where(pc.c == 0, jnp.ones_like(lane), lane)
-            wr_ = jnp.where(pc.c == 0, lane, jnp.ones_like(lane))
-            ws[s, h] = (wo_ * vf[s, h] + wr_ * g).astype(BF)
-            rf[s, h] = rf[s, h] + (jnp.exp(-far * one) * fp) * g
-            return 0
-
-        lax.fori_loop(0, 4, quad, 0)
-        w_cp.append(ln.go(ws.at[s], wr.at[s], "Y"))
-    for b in range(2):
-        right.second_stage(b)
-        s_out.first_stage(b)
-    for i in (3, 2):
-        for b in range(2):
-            s_w[i].first_stage(b)
-    n_cp = []
-    for s in range(2):
+        quad_sum(fac, s, vf, tr, ws, rf)
+        return ln.go(ws.at[s], wr.at[s], "Y")
+
+    def close_up(s):
         w_cp[s].wait_recv()
-        here = jnp.where(pc.zh == 1, last_id(ids, pc.k, 1, s), last_id(ids, pc.k, 0, s))
-        fp = same(here, last_id(ids, 1, 1, s)) * jnp.where(pc.y == 0, 1.0, 0.0)
-        far = (2 * (1 - pc.c) + (1 - pc.zh)).astype(F32) * CH
         rs_ = pl.ds(s * CH, CH)
 
         def close(h, _):
-            d = (rf[s, h] + (jnp.exp(-far * rate[h, 0:1, :]) * fp) * wr[s, h].astype(F32)).astype(BF)
+            d = (rf[s, h] + fac[s, h, 6:7, :] * wr[s, h].astype(F32)).astype(BF)
             k, v = qkv[0, h, rs_, :], qkv[1, h, rs_, :]
             w = wend[h] * endf[s]
             kw = (k.astype(F32) * w).astype(BF)
@@ -830,6 +823,9 @@
             return 0
 
         lax.fori_loop(0, 4, close, 0)
+
+    def through_weights(s):
+        rs_ = pl.ds(s * CH, CH)
         acc = None
         for i in range(4):
             for b in range(2):
@@ -837,24 +833,59 @@
                 acc = p if acc is None else acc + p
         tmp[...] = acc
         nsend[s] = tmp[rows128(1 - pc.t), :].astype(BF)
-        n_cp.append(ln.go(nsend.at[s], nrecv.at[s], "P"))
         gtok[s] = tmp[rows128(pc.t), :]
+        return ln.go(nsend.at[s], nrecv.at[s], "P")
+
+    def out_core(b):
+        s_out.core_stage(b, lambda b, i: dg(mix[:, cols256(b)], dr[:, cols256(i)], 0, 0))
+
+    inner(0)
+    t_cp = [pair_up(0)]
+    t_cp.append(pair_up(1))
+    ready(17)
+    for b in range(2):
+        out_core(b)
+    w_cp = [quad_up(0), quad_up(1)]
+    inner(1)
+    for b in range(2):
+        right.second_stage(b)
+    for b in range(2):
+        s_out.first_stage(b)
+    left.plane_stage()
+    for b in range(2):
+        s_w[3].core_stage(b, product(3))
+    ready(22)
+    close_up(0)
+    close_up(1)
+    for b in range(2):
+        s_w[3].first_stage(b)
     for i in (0, 1):
         for b in range(2):
             s_w[i].core_stage(b, product(i))
-    left.plane_stage()
+    for b in range(2):
+        s_out.second_stage(b)
     right.plane_stage()
-    for b in range(2):
-        s_out.second_stage(b)
-    for i in (3, 2):
-        for b in range(2):
-            s_w[i].second_stage(b)
+    n_cp = [through_weights(0)]
     for i in (0, 1):
         for b in range(2):
             s_w[i].first_stage(b)
+    for b in range(2):
+        s_w[3].second_stage(b)
+    n_cp.append(through_weights(1))
+    for b in range(2):
+        s_w[2].core_stage(b, product(2))
+    for i in (0, 1):
+        for b in range(2):
+            s_w[i].second_stage(b)
     s_out.plane_stage()
-    for i in (3, 2):
+    s_w[3].plane_stage()
+    for b in range(2):
+        s_w[2].first_stage(b)
+    for i in (0, 1):
         s_w[i].plane_stage()
+    for b in range(2):
+        s_w[2].second_stage(b)
+    s_w[2].plane_stage()
     f_cp.wait_recv()
     frecv[...] = (fo[...] + frecv[...].astype(F32)).astype(BF)
     ln.keep(frecv, out_o)
@@ -863,15 +894,13 @@
         dn = gtok[s] + nrecv[s].astype(F32)
         gtok[s] = dx1[s] + norm_slope(x[s].astype(F32), dn, EPSILON)
     ln.keep(gtok, gtok_o)
-    for i in (0, 1):
-        for b in range(2):
-            s_w[i].second_stage(b)
+    z_cp.wait_recv()
+    dnear[...] = dnear[...] + drz[...].astype(F32)
+    ln.keep(dnear, gd_o)
     gleft[...] = left.total()
     ln.keep(gleft, gl_o)
     gright[...] = right.total()
     ln.keep(gright, gr_o)
-    for i in (0, 1):
-        s_w[i].plane_stage()
     gout[...] = s_out.total()
     ln.keep(gout, go_o)
     for i, o in ((3, gg_o), (2, gq_o), (0, gk_o), (1, gv_o)):
@@ -882,21 +911,21 @@
 
 def call_backward(*args):
     sd, vm = jax.ShapeDtypeStruct, pltpu.VMEM
-    ff = args[9].shape[2]
+    ff = args[10].shape[2]
     outs = [
         sd((2, 128, 1024), BF), sd((2, 128, 1024), F32),
         sd((128, 256), F32), sd((128, 256), F32), sd((128, 256), F32), sd((128, 256), F32),
-        sd((256, 128), F32), sd((ff, 128), F32), sd((ff, 128), F32),
+        sd((256, 128), F32), sd((ff, 128), F32), sd((ff, 128), F32), sd((ff, 128), F32),
     ]
     st = (2, 4, DH, DH)
     scratch = [vm(a.shape, a.dtype) for a in args] + [
-        vm((4, CH, CH), F32), vm((4, CH, DH), F32), vm((4, CH, DH), F32),
+        vm((2, 4, 8, DH), F32), vm((4, CH, CH), F32), vm((4, CH, DH), F32), vm((4, CH, DH), F32),
         vm((2, CH, CH), F32), vm((2, CH, DH), F32), vm((2, CH, DH), F32),
         vm((512, 512), F32), vm((4, 512, DH), BF), vm((4, 512, 512), BF),
         vm(st, F32), vm(st, BF), vm(st, BF), vm(st, BF), vm(st, BF), vm(st, BF), vm(st, BF),
         vm(st, F32), vm((8, 128), BF),
         vm((CH, 1024), F32), vm((2, 128, 1024), BF), vm((2, 128, 1024), BF), vm((2, 128, 1024), BF),
-        vm((2, 128, 1024), F32), vm((4, 128, 256), F32),
+        vm((ff, 128), BF), vm((2, 128, 1024), F32), vm((4, 128, 256), F32),
         vm((256, 128), F32), vm((ff, 128), F32), vm((ff, 128), F32),
         *scatter_bufs((ff, 128), BF, 0)[1:], *scatter_bufs((ff, 128), BF),
         *scatter_bufs((256, 128)), *scatter_bufs((128, 256)), *scatter_bufs((128, 256)),
@@ -1268,13 +1297,14 @@
     tok, cot = tokens.transpose(1, 0, 2), cotangent.transpose(1, 0, 2)
     (
         n1, n2, pkq, pg, qkv, pm, att, mix, sb, wb, wo, ids, rate,
-        dr, dx1, fs, fo, dpr, g_down, left_acc,
+        dr, dx1, fs, fo, dpr, dnear, dsz, left_acc,
     ) = call_forward(
         decay_rate, tok, cot, segment_ids, (w_query, w_key, w_value, w_gate), w_out,
         glu_left.T, glu_right.T, glu_down,
     )
-    out, g_tok, g_q, g_k, g_v, g_g, g_o, g_left, g_right = call_backward(
-        ids, rate, dr, wo, att, pg, qkv, left_acc, n2, dpr, pm, sb, pkq, n1, mix, wb, fs, fo, dx1, tok
+    out, g_tok, g_q, g_k, g_v, g_g, g_o, g_left, g_right, g_down = call_backward(
+        ids, rate, fs, left_acc, dr, wo, att, pg, qkv, n2, dpr, pm, sb, pkq, dsz, mix, n1, wb, fo, dx1, tok,
+        dnear,
     )
     return (
         out.transpose(1, 0, 2), g_tok.transpose(1, 0, 2),

time: 217 us -> 202 us (0.931)
  Pallas kernels: 204 us -> 189 us
    pallas_call x1, Pallas kernels: 72.2 us -> 64.1 us  [call_backward(): pl.pallas_call(attn_backward, out_shape=outs, in_specs=[pl.BlockSpec(memo...]
    pallas_call x1, Pallas kernels: 132 us -> 125 us  [call_forward(): pl.pallas_call(forward_and_glu, out_shape=outs, in_specs=[pl.BlockSpec(me...]
where the time goes in v3:
time: 202 us
  Pallas kernels  189 us (94%)
  local copies, waits for them, and re-layouts  12.2 us (6%)
    pallas_call x1, Pallas kernels, call_forward(): pl.pallas_call(forward_and_glu, out_shape=outs, in_specs=[pl.BlockSpec(me...  125 us
    pallas_call x1, Pallas kernels, call_backward(): pl.pallas_call(attn_backward, out_shape=outs, in_specs=[pl.BlockSpec(memo...  64.1 us
    unnamed x28, local copies, waits for them, and re-layouts  9.77 us

profile of v3, /device:TPU:0, one launch (start us, length us, event | category | flops | bytes accessed | tf_op | source)
XLA Modules:
  0.0 201.6 jit_solution(176261318823464657)
XLA Ops:
  0.6 2.5 %copy_bitcast_fusion = (bf16[2,128,1024]{2,1,0:T(8,128)(2,1)}, bf16[2,128,1024]{2,1,0:T(8,128)(2,1)}) fusion(bf16[128,2,1024]{2,1,0:T(2,128)(2,1)} %param.23, bf16[128,2,1024]{2,1,0:T(2,128)(2,1)} %param.12), kind=kLoop, calls=%fused_computation | loop fusion | bytes 2097152 | tf_op jit(solution)/shard_map/transpose | solution.py:1297
  3.1 124.6 %forward_and_glu.1 = (bf16[512,1024]{1,0:T(8,128)(2,1)}, bf16[512,1024]{1,0:T(8,128)(2,1)}, f32[512,1024]{1,0:T(8,128)}, f32[512,512]{1,0:T(8,128)}, bf16[3,4,51...) custom-call(f32[2]{0:T(128)} %rate_in.1, ...), custom_call_target="tpu_custom_call" | custom-call | tf_op jit(solution)/shard_map/forward_and_glu/pallas_call | solution.py:675
  127.7 64.1 %attention_backward.1 = (bf16[2,128,1024]{2,1,0:T(8,128)(2,1)}, f32[2,128,1024]{2,1,0:T(8,128)}, f32[128,256]{1,0:T(8,128)}, f32[128,256]{1,0:T(8,128)}, f32[128...) custom-call(f32[4,8,512]{2,1,0:T(8,128)} %get-tuple-element.41.refs_, ...), custom_call_target="tpu_custom_call" | custom-call | tf_op jit(solution)/shard_map/attention_backward/pallas_call | solution.py:935
  191.8 0.0 copy-start
  191.8 0.0 copy-start.8
  191.8 0.0 copy-start.7
  191.8 2.5 %copy.24 = bf16[128,2,1024]{2,1,0:T(2,128)(2,1)} copy(bf16[128,2,1024]{2,0,1:T(8,128)(2,1)} %bitcast.11) | data formatting | bytes 1048576
  194.3 0.0 copy-start.6
  194.3 0.0 copy-start.5
  194.3 0.0 copy-done
  194.3 0.0 copy-start.4
  194.3 0.0 copy-start.3
  194.3 0.0 copy-start.2
  194.3 1.8 copy.25
  196.1 0.0 copy-done.8
  196.1 0.0 copy-start.1
  196.1 0.7 copy.36
  196.8 0.0 copy-done.7
  196.8 0.7 copy.37
  197.4 0.0 copy-done.6
  197.4 0.7 copy.38
  198.1 0.0 copy-done.5
  198.1 0.7 copy.39
  198.8 0.0 copy-done.4
  198.8 0.7 copy.40
  199.4 0.0 copy-done.3
  199.4 0.7 copy.41
  200.2 0.0 copy-done.2
  200.2 0.7 copy.42
  200.9 0.0 copy-done.1
  200.9 0.7 copy.43
Async XLA Ops:
  191.8 2.5 %copy-start = (f32[2,128,1024]{2,1,0:T(8,128)S(1)}, f32[2,128,1024]{2,1,0:T(8,128)}, u32[]{:S(2)}) copy-start(f32[2,128,1024]{2,1,0:T(8,128)} %get-tuple-element.63) | copy-start | bytes 3145732
  191.8 4.3 %copy-start.8 = (f32[128,256]{1,0:T(8,128)S(1)}, f32[128,256]{1,0:T(8,128)}, u32[]{:S(2)}) copy-start(f32[128,256]{1,0:T(8,128)} %get-tuple-element.96) | copy-start | bytes 393220
  191.8 5.0 %copy-start.7 = (f32[128,256]{1,0:T(8,128)S(1)}, f32[128,256]{1,0:T(8,128)}, u32[]{:S(2)}) copy-start(f32[128,256]{1,0:T(8,128)} %get-tuple-element.97) | copy-start | bytes 393220
  194.3 3.1 %copy-start.6 = (f32[128,256]{1,0:T(8,128)S(1)}, f32[128,256]{1,0:T(8,128)}, u32[]{:S(2)}) copy-start(f32[128,256]{1,0:T(8,128)} %get-tuple-element.98) | copy-start | bytes 393220
  194.3 3.8 %copy-start.5 = (f32[128,256]{1,0:T(8,128)S(1)}, f32[128,256]{1,0:T(8,128)}, u32[]{:S(2)}) copy-start(f32[128,256]{1,0:T(8,128)} %get-tuple-element.99) | copy-start | bytes 393220
  194.3 4.4 %copy-start.4 = (f32[256,128]{1,0:T(8,128)S(1)}, f32[256,128]{1,0:T(8,128)}, u32[]{:S(2)}) copy-start(f32[256,128]{1,0:T(8,128)} %get-tuple-element.100) | copy-start | bytes 393220
  194.3 5.1 %copy-start.3 = (f32[704,128]{1,0:T(8,128)S(1)}, f32[704,128]{1,0:T(8,128)}, u32[]{:S(2)}) copy-start(f32[704,128]{1,0:T(8,128)} %get-tuple-element.69) | copy-start | bytes 1081348
  194.3 5.8 %copy-start.2 = (f32[704,128]{1,0:T(8,128)S(1)}, f32[704,128]{1,0:T(8,128)}, u32[]{:S(2)}) copy-start(f32[704,128]{1,0:T(8,128)} %get-tuple-element.70) | copy-start | bytes 1081348
  196.1 4.8 %copy-start.1 = (f32[704,128]{1,0:T(8,128)S(1)}, f32[704,128]{1,0:T(8,128)}, u32[]{:S(2)}) copy-start(f32[704,128]{1,0:T(8,128)} %get-tuple-element.103) | copy-start | bytes 1081348

commit v4 on v3

--- a/solution.py
+++ b/solution.py
@@ -360,7 +360,7 @@
 
 def forward_and_glu(
     rate_in, tok, cot, seg, wq, wk, wv, wg, wo_in, gl_in, gr_in, gd_in,
-    n1_o, n2_o, pkq_o, pg_o, qkv_o, p_o, att_o, mix_o, sb_o, w_o, wo_o, ids_o, rate_o,
+    xm_o, n1_o, n2_o, pkq_o, pg_o, qkv_o, p_o, att_o, mix_o, sb_o, w_o, wo_o, ids_o, rate_o,
     dr_o, dx1_o, fs_o, fo_o, dpr_o, gdown_o, dsz_o, left_o,
     xb, n1, ct, n2, x1, pg, qkv, pm, att, mix, sb, wb, wo, gl, gr, gd,
     ids, rate, fac, grid, wend, gin, mask, endf, inf, uf, us, ur, ts, tr, vs, vr, pf,
@@ -390,8 +390,8 @@
     for hh in range(2):
         rate[own * 2 + hh] = jnp.full((8, DH), rate_in[hh], F32)
     for s in range(2):
-        xb[mine(s), :] = tok[s]
-        ct[mine(s), :] = cot[s]
+        xb[mine(s), :] = tok[:, s, :]
+        ct[mine(s), :] = cot[:, s, :]
     for i, w in enumerate((wk, wv, wq, wg)):
         wb[i, own, rows128(r), :] = w[...].astype(BF)
     wo[own, rows128(r), :] = wo_in[...].T.astype(BF)
@@ -414,7 +414,7 @@
     for g in qkvgo[2:]:
         g.cross()
     for s in range(2):
-        xf = tok[s].astype(F32)
+        xf = xb[mine(s), :].astype(F32)
         n1[mine(s), :] = (xf * inverse_norm(xf, EPSILON)).astype(BF)
     for w, w_in in ((gl, gl_in), (gr, gr_in), (gd, gd_in)):
         w[own, rows128(r), :] = w_in[...].T.astype(BF)
@@ -506,6 +506,8 @@
     g_o.step3(0)
     g_o.step3(1)
     pkq_cp = ln.keep(x1, pkq_o)
+    for s in range(2):
+        ln.keep(xb.at[mine(s)], xm_o.at[s])
     for i in range(4):
         ln.keep(wb.at[i], w_o.at[i])
     ln.keep(n1, n1_o)
@@ -650,7 +652,7 @@
     act = (512, 1024)
     st = (2, 4, DH, DH)
     outs = [
-        sd(act, BF), sd(act, BF), sd(act, F32), sd((512, 512), F32), sd((3, 4, 512, DH), BF),
+        sd((2, 128, 1024), BF), sd(act, BF), sd(act, BF), sd(act, F32), sd((512, 512), F32), sd((3, 4, 512, DH), BF),
         sd((2, 4, CH, CH), BF), sd((4, 512, DH), F32), sd((512, 512), BF), sd(st, BF),
         sd((4, 2, 1024, 256), BF), sd((2, 1024, 256), BF), sd((4, 8, 512), F32), sd((4, 8, DH), F32),
         sd(act, BF), sd((2, 128, 1024), F32), sd((2, 128, 1024), BF), sd((2, 128, 1024), F32),
@@ -1294,16 +1296,15 @@
     tokens, segment_ids, decay_rate, w_query, w_key, w_value, w_gate, w_out,
     glu_left, glu_right, glu_down, cotangent,
 ):
-    tok, cot = tokens.transpose(1, 0, 2), cotangent.transpose(1, 0, 2)
     (
-        n1, n2, pkq, pg, qkv, pm, att, mix, sb, wb, wo, ids, rate,
+        own_rows, n1, n2, pkq, pg, qkv, pm, att, mix, sb, wb, wo, ids, rate,
         dr, dx1, fs, fo, dpr, dnear, dsz, left_acc,
     ) = call_forward(
-        decay_rate, tok, cot, segment_ids, (w_query, w_key, w_value, w_gate), w_out,
+        decay_rate, tokens, cotangent, segment_ids, (w_query, w_key, w_value, w_gate), w_out,
         glu_left.T, glu_right.T, glu_down,
     )
     out, g_tok, g_q, g_k, g_v, g_g, g_o, g_left, g_right, g_down = call_backward(
-        ids, rate, fs, left_acc, dr, wo, att, pg, qkv, n2, dpr, pm, sb, pkq, dsz, mix, n1, wb, fo, dx1, tok,
+        ids, rate, fs, left_acc, dr, wo, att, pg, qkv, n2, dpr, pm, sb, pkq, dsz, mix, n1, wb, fo, dx1, own_rows,
         dnear,
     )
     return (

time: 202 us -> 201 us (level)
  local copies, waits for them, and re-layouts: 12.2 us -> 9.77 us
    transpose x1 -> x0, local copies, waits for them, and re-layouts: 2.45 us -> none  [paired(): tok, cot = (tokens.transpose(1, 0, 2), cotangent.transpose(1, 0, 2))]
where the time goes in v4:
time: 201 us
  Pallas kernels  191 us (95%)
  local copies, waits for them, and re-layouts  9.77 us (5%)
    pallas_call x1, Pallas kernels, call_forward(): pl.pallas_call(forward_and_glu, out_shape=outs, in_specs=[pl.BlockSpec(me...  125 us
    pallas_call x1, Pallas kernels, call_backward(): pl.pallas_call(attn_backward, out_shape=outs, in_specs=[pl.BlockSpec(memo...  65.9 us
    unnamed x28, local copies, waits for them, and re-layouts  9.77 us

profile of v4, /device:TPU:0, one launch (start us, length us, event | category | flops | bytes accessed | tf_op | source)
XLA Modules:
  0.0 201.1 jit_solution(12352749642533319152)
XLA Ops:
  0.6 124.7 %forward_and_glu.1 = (bf16[2,128,1024]{2,1,0:T(8,128)(2,1)}, bf16[512,1024]{1,0:T(8,128)(2,1)}, bf16[512,1024]{1,0:T(8,128)(2,1)}, f32[512,1024]{1,0:T(8,128)}, ...) custom-call(f32[2]{0:T(128)} %rate_in.1, ...), custom_call_target="tpu_custom_call" | custom-call | tf_op jit(solution)/shard_map/forward_and_glu/pallas_call | solution.py:677
  125.3 65.9 %attention_backward.1 = (bf16[2,128,1024]{2,1,0:T(8,128)(2,1)}, f32[2,128,1024]{2,1,0:T(8,128)}, f32[128,256]{1,0:T(8,128)}, f32[128,256]{1,0:T(8,128)}, f32[128...) custom-call(f32[4,8,512]{2,1,0:T(8,128)} %get-tuple-element.42.refs_, ...), custom_call_target="tpu_custom_call" | custom-call | tf_op jit(solution)/shard_map/attention_backward/pallas_call | solution.py:937
  191.3 0.0 copy-start
  191.3 0.0 copy-start.8
  191.3 0.0 copy-start.7
  191.3 2.5 %copy.22 = bf16[128,2,1024]{2,1,0:T(2,128)(2,1)} copy(bf16[128,2,1024]{2,0,1:T(8,128)(2,1)} %bitcast.7) | data formatting | bytes 1048576
  193.8 0.0 copy-start.6
  193.8 0.0 copy-start.5
  193.8 0.0 copy-done
  193.8 0.0 copy-start.4
  193.8 0.0 copy-start.3
  193.8 0.0 copy-start.2
  193.8 1.8 copy.23
  195.6 0.0 copy-done.8
  195.6 0.0 copy-start.1
  195.6 0.7 copy.32
  196.3 0.0 copy-done.7
  196.3 0.7 copy.33
  196.9 0.0 copy-done.6
  196.9 0.7 copy.34
  197.6 0.0 copy-done.5
  197.6 0.7 copy.35
  198.2 0.0 copy-done.4
  198.2 0.7 copy.36
  198.9 0.0 copy-done.3
  198.9 0.7 copy.37
  199.6 0.0 copy-done.2
  199.6 0.7 copy.38
  200.4 0.0 copy-done.1
  200.4 0.7 copy.39
Async XLA Ops:
  191.3 2.5 %copy-start = (f32[2,128,1024]{2,1,0:T(8,128)S(1)}, f32[2,128,1024]{2,1,0:T(8,128)}, u32[]{:S(2)}) copy-start(f32[2,128,1024]{2,1,0:T(8,128)} %get-tuple-element.65) | copy-start | bytes 3145732
  191.3 4.3 %copy-start.8 = (f32[128,256]{1,0:T(8,128)S(1)}, f32[128,256]{1,0:T(8,128)}, u32[]{:S(2)}) copy-start(f32[128,256]{1,0:T(8,128)} %get-tuple-element.96) | copy-start | bytes 393220
  191.3 5.0 %copy-start.7 = (f32[128,256]{1,0:T(8,128)S(1)}, f32[128,256]{1,0:T(8,128)}, u32[]{:S(2)}) copy-start(f32[128,256]{1,0:T(8,128)} %get-tuple-element.97) | copy-start | bytes 393220
  193.8 3.1 %copy-start.6 = (f32[128,256]{1,0:T(8,128)S(1)}, f32[128,256]{1,0:T(8,128)}, u32[]{:S(2)}) copy-start(f32[128,256]{1,0:T(8,128)} %get-tuple-element.98) | copy-start | bytes 393220
  193.8 3.8 %copy-start.5 = (f32[128,256]{1,0:T(8,128)S(1)}, f32[128,256]{1,0:T(8,128)}, u32[]{:S(2)}) copy-start(f32[128,256]{1,0:T(8,128)} %get-tuple-element.99) | copy-start | bytes 393220
  193.8 4.4 %copy-start.4 = (f32[256,128]{1,0:T(8,128)S(1)}, f32[256,128]{1,0:T(8,128)}, u32[]{:S(2)}) copy-start(f32[256,128]{1,0:T(8,128)} %get-tuple-element.100) | copy-start | bytes 393220
  193.8 5.1 %copy-start.3 = (f32[704,128]{1,0:T(8,128)S(1)}, f32[704,128]{1,0:T(8,128)}, u32[]{:S(2)}) copy-start(f32[704,128]{1,0:T(8,128)} %get-tuple-element.71) | copy-start | bytes 1081348
  193.8 5.8 %copy-start.2 = (f32[704,128]{1,0:T(8,128)S(1)}, f32[704,128]{1,0:T(8,128)}, u32[]{:S(2)}) copy-start(f32[704,128]{1,0:T(8,128)} %get-tuple-element.72) | copy-start | bytes 1081348
  195.6 4.8 %copy-start.1 = (f32[704,128]{1,0:T(8,128)S(1)}, f32[704,128]{1,0:T(8,128)}, u32[]{:S(2)}) copy-start(f32[704,128]{1,0:T(8,128)} %get-tuple-element.103) | copy-start | bytes 1081348
